TPU v7x, 32 devices: a whole 2x2x4 slice. The times are simulated.
32 devices in a mesh: groups: 2 (over y), role: 4 (over x, core), tp: 4 (over z).
Axes of the slice: x: 2, y: 2, z: 4, core: 2. Of those that a mesh axis runs over, the one named last changes fastest.
Arguments:
- residual: bfloat16 [64, 8192], P(('groups', 'tp'), 'role'), parts along dimension 0, may hold values from -20 to 20
- attn_gain: float32 [8192], P('role'), may hold values from 0.1 to 1.9
- w_query: bfloat16 [8192, 4096], P('role', 'tp'), may hold values from -0.0625 to 0.0625
- w_key: bfloat16 [8192, 512], P('role', 'tp'), may hold values from -0.0625 to 0.0625
- w_value: bfloat16 [8192, 512], P('role', 'tp'), may hold values from -0.0625 to 0.0625
- w_output: bfloat16 [4096, 8192], P('tp', 'role'), may hold values from -0.09375 to 0.09375
- cache_keys: bfloat16 [64, 256, 512], P(('groups', 'role', 'tp')), parts along dimension 0, may hold values from -300 to 300
- cache_values: bfloat16 [64, 256, 512], P(('groups', 'role', 'tp')), parts along dimension 0, may hold values from -12 to 12
- lengths: int32 [64], P(('groups', 'role', 'tp')), parts along dimension 0, may hold values from 2 to 256
- served: int32 [64], P('groups'), parts along dimension 0, may hold values 0 or 1
- ffn_gain: float32 [8192], P('role'), may hold values from 0.1 to 1.9
- w_gate: bfloat16 [8192, 14336], P('role', 'tp'), may hold values from -0.0625 to 0.0625
- w_up: bfloat16 [8192, 14336], P('role', 'tp'), may hold values from -0.0625 to 0.0625
- w_down: bfloat16 [14336, 8192], P('tp', 'role'), may hold values from -0.046875 to 0.046875
Outputs:
- layer_out: bfloat16 [64, 8192], P(('groups', 'tp'), 'role'), parts along dimension 0
There are 2 independent parts, one for each index of `groups`. A program takes and returns all parts, laid end to end along the dimension named above; an argument that names none is the same for every part. Nothing has to cross between parts.
Inputs may be any that keep to these rules, and one draw needn't show every extreme that they name: Each request's new token stands at position lengths; cached positions from lengths on are unused.
All inputs are finite; a program needn't handle non-finite values.
Results may differ from a plain program's by a relative error of at most 0.024.
Values may be sent and summed in bfloat16 or wider, within the bound.
No kernel may reach another device: no remote copies, remote signals or barrier semaphores. Data moves between devices by JAX's collectives and lax.ppermute only.
A program may use at most 128 MiB of HBM per device.

v0:
```python
import jax
import jax.numpy as jnp
from jax import lax
from jax.sharding import PartitionSpec as P

D = 8192
HEADS = 32
KV_HEADS = 4
HEAD_DIM = 128
WINDOW = 256
GROUP = 8


epsilon = 1e-05
rope_base = 500000.0


def rotate(vectors, positions):
    halfway = vectors.shape[-1] // 2
    frequency = jnp.power(
        jnp.float32(rope_base), -jnp.arange(halfway, dtype=jnp.float32) * 2.0 / vectors.shape[-1]
    )
    angles = positions.astype(jnp.float32)[:, None, None] * frequency[None, None, :]
    cosine = jnp.cos(angles)
    sine_part = jnp.sin(angles)
    leading = vectors[..., :halfway]
    trailing = vectors[..., halfway:]
    return jnp.concatenate(
        [leading * cosine - trailing * sine_part, trailing * cosine + leading * sine_part], axis=-1
    )


def attend(queries, new_key, new_value, keys, values, lengths):
    batch_rows = queries.shape[0]
    factor = HEAD_DIM ** (-0.5)
    grouped = queries.reshape(batch_rows, KV_HEADS, GROUP, HEAD_DIM)
    key_blocks = keys.reshape(batch_rows, WINDOW, KV_HEADS, HEAD_DIM)
    value_blocks = values.reshape(batch_rows, WINDOW, KV_HEADS, HEAD_DIM)
    scores = (
        jnp.einsum("nkgd,nwkd->nkgw", grouped, key_blocks, preferred_element_type=jnp.float32)
        * factor
    )
    self_score = (
        jnp.einsum("nkgd,nkd->nkg", grouped, new_key, preferred_element_type=jnp.float32) * factor
    )
    usable = jnp.arange(WINDOW, dtype=jnp.int32)[None, :] < lengths[:, None]
    scores = jnp.where(usable[:, None, None, :], scores, -jnp.inf)
    highest = jnp.maximum(jnp.max(scores, axis=-1), self_score)
    weights = jnp.exp(scores - highest[..., None])
    self_weight = jnp.exp(self_score - highest)
    denominator = jnp.sum(weights, axis=-1) + self_weight
    chances = (weights / denominator[..., None]).astype(jnp.bfloat16)
    self_chance = (self_weight / denominator).astype(jnp.bfloat16)
    attended = jnp.einsum(
        "nkgw,nwkd->nkgd", chances, value_blocks, preferred_element_type=jnp.float32
    )
    attended = (
        attended
        + self_chance.astype(jnp.float32)[..., None] * new_value.astype(jnp.float32)[:, :, None, :]
    )
    return attended.reshape(batch_rows, HEADS * HEAD_DIM).astype(jnp.bfloat16)


def feed_forward(middle, ffn_gain, w_gate, w_up, w_down):
    widened = middle.astype(jnp.float32)
    squares = lax.psum(jnp.sum(widened * widened, axis=1), "role")
    inverse = lax.rsqrt(squares / D + epsilon)
    mid_normed = (widened * inverse[:, None] * ffn_gain[None, :]).astype(jnp.bfloat16)
    gate_part = jnp.dot(mid_normed, w_gate, preferred_element_type=jnp.float32)
    up_part = jnp.dot(mid_normed, w_up, preferred_element_type=jnp.float32)
    gate_total, up_total = (
        lax.psum(gate_part.astype(jnp.bfloat16), "role").astype(jnp.float32),
        lax.psum(up_part.astype(jnp.bfloat16), "role").astype(jnp.float32),
    )
    hidden = (jax.nn.silu(gate_total) * up_total).astype(jnp.bfloat16)
    down_terms = jnp.dot(hidden, w_down, preferred_element_type=jnp.float32)
    return lax.psum_scatter(
        down_terms.astype(jnp.bfloat16), "tp", scatter_dimension=0, tiled=True
    ).astype(jnp.float32)


def local(
    residual,
    attn_gain,
    w_query,
    w_key,
    w_value,
    w_output,
    cache_keys,
    cache_values,
    lengths,
    served,
    ffn_gain,
    w_gate,
    w_up,
    w_down,
):
    own_rows = residual.shape[0]
    tp_count = lax.axis_size("tp")
    row_start = lax.axis_index("tp") * own_rows
    live_own = lax.dynamic_slice_in_dim(served, row_start, own_rows, 0).astype(jnp.float32)[:, None]
    rows_all = lax.all_gather(residual, "tp", axis=0, tiled=True)
    widened = rows_all.astype(jnp.float32)
    squares = lax.psum(jnp.sum(widened * widened, axis=1), "role")
    inverse = lax.rsqrt(squares / D + epsilon)
    normed = (widened * inverse[:, None] * attn_gain[None, :]).astype(jnp.bfloat16)
    partial_value = jnp.concatenate(
        [
            jnp.dot(normed, w_query, preferred_element_type=jnp.float32),
            jnp.dot(normed, w_key, preferred_element_type=jnp.float32),
            jnp.dot(normed, w_value, preferred_element_type=jnp.float32),
        ],
        axis=1,
    )
    summed = lax.psum_scatter(
        partial_value.astype(jnp.bfloat16), "role", scatter_dimension=0, tiled=True
    ).astype(jnp.float32)
    gathered = lax.all_to_all(
        summed.astype(jnp.bfloat16), "tp", split_axis=0, concat_axis=1, tiled=True
    ).astype(summed.dtype)
    local_rows = gathered.shape[0]
    query_cols = w_query.shape[1]
    kv_cols = w_key.shape[1]
    blocks = gathered.reshape(local_rows, tp_count, query_cols + 2 * kv_cols)
    queries = blocks[:, :, :query_cols].reshape(local_rows, HEADS, HEAD_DIM)
    new_key = blocks[:, :, query_cols : query_cols + kv_cols].reshape(
        local_rows, KV_HEADS, HEAD_DIM
    )
    new_value = (
        blocks[:, :, query_cols + kv_cols :]
        .reshape(local_rows, KV_HEADS, HEAD_DIM)
        .astype(jnp.bfloat16)
    )
    queries = rotate(queries, lengths).astype(jnp.bfloat16)
    new_key = rotate(new_key, lengths).astype(jnp.bfloat16)
    attended = attend(queries, new_key, new_value, cache_keys, cache_values, lengths)
    head_block = lax.all_to_all(attended, "tp", split_axis=1, concat_axis=0, tiled=True)
    attn_terms = jnp.dot(
        lax.all_gather(head_block, "role", axis=0, tiled=True),
        w_output,
        preferred_element_type=jnp.float32,
    )
    attn = lax.psum_scatter(
        attn_terms.astype(jnp.bfloat16), "tp", scatter_dimension=0, tiled=True
    ).astype(jnp.float32)
    middle_own = (residual.astype(jnp.float32) + live_own * attn).astype(jnp.bfloat16)
    middle = lax.all_gather(middle_own, "tp", axis=0, tiled=True)
    ffn = feed_forward(middle, ffn_gain, w_gate, w_up, w_down)
    return (middle_own.astype(jnp.float32) + live_own * ffn).astype(jnp.bfloat16)


def solution(mesh):
    return jax.shard_map(
        local,
        mesh=mesh,
        in_specs=(
            P(("groups", "tp"), "role"),
            P("role"),
            P("role", "tp"),
            P("role", "tp"),
            P("role", "tp"),
            P("tp", "role"),
            P(("groups", "role", "tp"), None, None),
            P(("groups", "role", "tp"), None, None),
            P(("groups", "role", "tp")),
            P("groups"),
            P("role"),
            P("role", "tp"),
            P("role", "tp"),
            P("tp", "role"),
        ),
        out_specs=P(("groups", "tp"), "role"),
        check_vma=False,
    )
```

profile of v0, /device:TPU:0, one launch (start us, length us, event | category | flops | bytes accessed | tf_op | source)
XLA Modules:
  0.0 208.5 jit_solution(7875377142544412740)
XLA Ops:
  6.5 15.4 %all_gather.9 = bf16[32,2048]{1,0:T(8,128)(2,1)S(1)} all-gather(bf16[8,2048]{1,0:T(8,128)(2,1)} %param.14), channel_id=1, replica_groups=mesh['groups'=2,'role'=4,'tp'=4] {'tp'}, dimensions={0}, use_global_device_ids=true | all-gather | bytes 163840 | tf_op jit(solution)/shard_map/all_gather | solution.py:102
  22.0 0.1 fusion.11
  22.1 5.7 %psum.28 = f32[32]{0:T(128)S(1)} all-reduce(f32[32]{0:T(128)S(1)} %fusion.11), channel_id=1, replica_groups=mesh['groups'=2,'role'=4,'tp'=4] {'role'}, use_global_device_ids=true, to_apply=%region_1.0 | all-reduce | flops 32 | bytes 256 | tf_op jit(solution)/shard_map/psum | solution.py:104
  27.8 1.3 convolution_convert_fusion.6
  29.1 1.3 convolution_convert_fusion.5
  30.4 3.1 %convolution_convert_fusion.4 = bf16[32,1024]{1,0:T(8,128)(2,1)S(1)} fusion(bf16[2048,1024]{1,0:T(8,128)(2,1)} %param.16, bf16[32,2048]{1,0:T(8,128)(2,1)S(1)} %all_gather.9, f32[2048]{0:T(1024)} %param.15, f32[32]{0:T(128)S(1)} %add_rsqrt_fusion.1), kind=kOutput, calls=%fused_computation.4 | convolution fusion | flops 134512640 | bytes 4399232 | tf_op jit(solution)/shard_map/dot_general | solution.py:109
  33.5 0.6 pad_maximum_fusion
  34.2 0.7 convert_element_type.97
  35.0 20.6 %reduce-scatter.4.cloned.1.call-done = bf16[8,1280]{1,0:T(8,128)(2,1)} async-done(((bf16[32,1280]{1,0:T(8,128)(2,1)}), bf16[8,1280]{1,0:T(8,128)(2,1)}) %reduce-scatter.4.cloned.1.call-update) | async-done | bytes 20496 | tf_op jit(solution)/shard_map/reduce_scatter | solution.py:115
  55.5 1.3 all_to_all.22
  56.9 4.6 %all-to-all-start = ((bf16[4,2,1280]{2,1,0:T(2,128)(2,1)}), bf16[4,2,1280]{2,1,0:T(2,128)(2,1)S(1)}, u32[]{:S(2)}, u32[]{:S(2)}) async-start(bf16[4,2,1280]{2,1,0:T(2,128)(2,1)} %all_to_all.22), calls=%async_computation.1 | async-start | bytes 40960 | tf_op jit(solution)/shard_map/all_to_all | solution.py:118
  61.5 0.7 iota_compare_fusion
  62.2 4.9 %all-to-all-done = bf16[4,2,1280]{2,1,0:T(2,128)(2,1)S(1)} async-done(((bf16[4,2,1280]{2,1,0:T(2,128)(2,1)}), bf16[4,2,1280]{2,1,0:T(2,128)(2,1)S(1)}, u32[]{:S(2)}, u32[]{:S(2)}) %all-to-all-start) | async-done | bytes 20512 | tf_op jit(solution)/shard_map/all_to_all | solution.py:118
  67.4 0.2 fusion.26
  67.6 0.3 fusion.37
  67.9 0.2 fusion.19
  68.2 1.3 fusion.1
  69.5 8.0 %all_to_all.29 = bf16[2,4,1024]{2,0,1:T(2,128)(2,1)S(1)} all-to-all(bf16[2,4,1024]{2,0,1:T(2,128)(2,1)S(1)} %copy.30), channel_id=1, replica_groups=mesh['groups'=2,'role'=4,'tp'=4] {'tp'}, dimensions={1} | all-to-all | bytes 32768 | tf_op jit(solution)/shard_map/all_to_all | solution.py:137
  77.5 5.2 %all_gather.10 = bf16[32,1024]{1,0:T(8,128)(2,1)S(1)} all-gather(bf16[8,1024]{1,0:T(8,128)(2,1)S(1)} %all_to_all.26), channel_id=1, replica_groups=mesh['groups'=2,'role'=4,'tp'=4] {'role'}, dimensions={0}, use_global_device_ids=true | all-gather | bytes 81920 | tf_op jit(solution)/shard_map/all_gather | solution.py:139
  82.7 3.7 %convolution_convert_fusion.3 = bf16[32,2048]{1,0:T(8,128)(2,1)} fusion(bf16[32,1024]{1,0:T(8,128)(2,1)S(1)} %all_gather.10, bf16[1024,2048]{1,0:T(8,128)(2,1)} %param.19), kind=kOutput, calls=%fused_computation.3 | convolution fusion | flops 134283264 | bytes 4390912 | tf_op jit(solution)/shard_map/dot_general | solution.py:138
  86.4 0.7 dynamic-slice_convert_fusion
  87.2 16.1 %reduce-scatter.6.cloned.1.call-done = bf16[8,2048]{1,0:T(8,128)(2,1)} async-done(((bf16[32,2048]{1,0:T(8,128)(2,1)}), bf16[8,2048]{1,0:T(8,128)(2,1)}) %reduce-scatter.6.cloned.1.call-update) | async-done | bytes 32784 | tf_op jit(solution)/shard_map/reduce_scatter | solution.py:143
  103.3 0.8 add_convert_fusion.1
  104.2 13.4 %all_gather.11 = bf16[32,2048]{1,0:T(8,128)(2,1)S(1)} all-gather(bf16[8,2048]{1,0:T(8,128)(2,1)S(1)} %add_convert_fusion.1), channel_id=1, replica_groups=mesh['groups'=2,'role'=4,'tp'=4] {'tp'}, dimensions={0}, use_global_device_ids=true | all-gather | bytes 163840 | tf_op jit(solution)/shard_map/all_gather | solution.py:147
  117.5 0.1 fusion.14
  117.7 5.7 %psum.29 = f32[32]{0:T(128)S(1)} all-reduce(f32[32]{0:T(128)S(1)} %fusion.14), channel_id=1, replica_groups=mesh['groups'=2,'role'=4,'tp'=4] {'role'}, use_global_device_ids=true, to_apply=%region_7.8 | all-reduce | flops 32 | bytes 256 | tf_op jit(solution)/shard_map/psum | solution.py:66
  123.3 8.5 %convolution_convert_fusion = bf16[32,3584]{1,0:T(8,128)(2,1)} fusion(bf16[2048,3584]{1,0:T(8,128)(2,1)} %param.26, bf16[32,2048]{1,0:T(8,128)(2,1)S(1)} %all_gather.11, f32[2048]{0:T(1024)} %param.24, f32[32]{0:T(128)S(1)} %add_rsqrt_fusion), kind=kOutput, calls=%fused_computation | convolution fusion | flops 470138880 | bytes 15048832 | tf_op jit(solution)/shard_map/dot_general | solution.py:70
  131.9 8.5 %convolution_convert_fusion.1 = bf16[32,3584]{1,0:T(8,128)(2,1)} fusion(bf16[2048,3584]{1,0:T(8,128)(2,1)} %param.25, bf16[32,2048]{1,0:T(8,128)(2,1)S(1)} %all_gather.11, f32[2048]{0:T(1024)S(1)} %copy-done.1, f32[32]{0:T(128)S(1)} %add_rsqrt_fusion), kind=kOutput, calls=%fused_computation.1 | convolution fusion | flops 470138880 | bytes 15048832 | tf_op jit(solution)/shard_map/dot_general | solution.py:69
  140.5 31.7 %all-reduce.3.cloned.1.call-done = (bf16[32,3584]{1,0:T(8,128)(2,1)}, bf16[32,3584]{1,0:T(8,128)(2,1)}) async-done(((bf16[32,3584]{1,0:T(8,128)(2,1)}, bf16[32,3584]{1,0:T(8,128)(2,1)}), (bf16[32,3584]{1,0:T(8,128)(2,1)}, bf16[32,3584]{1,0:T(8,128)(2,1)})) %all-reduce.3.cloned.1.call-update) | async-done | bytes 458768 | tf_op jit(solution)/shard_map/psum | solution.py:73
  172.2 8.7 %convolution_convert_fusion.2 = bf16[32,2048]{1,0:T(8,128)(2,1)} fusion(bf16[3584,2048]{1,0:T(8,128)(2,1)} %param.27, bf16[32,3584]{1,0:T(8,128)(2,1)} %get-tuple-element.5, bf16[32,3584]{1,0:T(8,128)(2,1)} %get-tuple-element.6), kind=kOutput, calls=%fused_computation.2 | convolution fusion | flops 470745088 | bytes 15269888 | tf_op jit(solution)/shard_map/dot_general | solution.py:76
  180.9 19.6 %reduce-scatter.8.cloned.1.call-done = bf16[8,2048]{1,0:T(8,128)(2,1)} async-done(((bf16[32,2048]{1,0:T(8,128)(2,1)}), bf16[8,2048]{1,0:T(8,128)(2,1)}) %reduce-scatter.8.cloned.1.call-update) | async-done | bytes 32784 | tf_op jit(solution)/shard_map/reduce_scatter | solution.py:77
  200.5 1.4 add_convert_fusion
  (28 shorter events, 0.6 us)
Async XLA Ops:
  6.5 61.1 %copy-start = (bf16[2,256,512]{2,1,0:T(8,128)(2,1)S(1)}, bf16[2,256,512]{2,1,0:T(8,128)(2,1)}, u32[]{:S(2)}) copy-start(bf16[2,256,512]{2,1,0:T(8,128)(2,1)} %param.20) | copy-start | bytes 1572868
  6.5 49.0 %reduce-scatter.4.cloned.1.call-start = ((), (), s32[]{:S(2)}) async-start(), calls=%async_computation.5 | async-start | bytes 102400 | tf_op jit(solution)/shard_map/reduce_scatter | solution.py:115
  56.9 10.2 %all-to-all-start = ((bf16[4,2,1280]{2,1,0:T(2,128)(2,1)}), bf16[4,2,1280]{2,1,0:T(2,128)(2,1)S(1)}, u32[]{:S(2)}, u32[]{:S(2)}) async-start(bf16[4,2,1280]{2,1,0:T(2,128)(2,1)} %all_to_all.22), calls=%async_computation.1 | async-start | bytes 40960 | tf_op jit(solution)/shard_map/all_to_all | solution.py:118
  61.5 41.9 %reduce-scatter.6.cloned.1.call-start = ((), (), s32[]{:S(2)}) async-start(), calls=%async_computation.6 | async-start | bytes 163840 | tf_op jit(solution)/shard_map/reduce_scatter | solution.py:143
  67.2 64.6 %copy-start.1 = (f32[2048]{0:T(1024)S(1)}, f32[2048]{0:T(1024)}, u32[]{:S(2)}) copy-start(f32[2048]{0:T(1024)} %param.24) | copy-start | bytes 24580
  86.4 85.8 %all-reduce.3.cloned.1.call-start = ((), (), s32[]{:S(2)}) async-start(), calls=%async_computation.8 | async-start | bytes 917504 | tf_op jit(solution)/shard_map/psum | solution.py:73
  140.4 60.1 %reduce-scatter.8.cloned.1.call-start = ((), (), s32[]{:S(2)}) async-start(), calls=%async_computation.7 | async-start | bytes 163840 | tf_op jit(solution)/shard_map/reduce_scatter | solution.py:77
Sparse Core Ops, SparseCore 0:
  34.3 21.1 reduce-scatter.3
  86.5 16.7 reduce-scatter.5
  140.5 31.5 all-reduce.2
  181.0 19.4 reduce-scatter.7
where the time goes:
time: 209 us
  waiting for transfers between devices  93 us (44%)
  blocking collectives  53.3 us (26%)
  matrix products  37 us (18%)
  between operations  13.2 us (6%)
  other arithmetic  5.94 us (3%)
  starting transfers between devices  4.69 us (2%)
    psum x1, waiting for transfers between devices, feed_forward(): lax.psum(up_part.astype(jnp.bfloat16), 'role').astype(jnp.float32)  31.7 us
    reduce_scatter x1, waiting for transfers between devices, local(): lax.psum_scatter(partial_value.astype(jnp.bfloat16), 'role', scatter_dime...  20.6 us
    reduce_scatter x1, waiting for transfers between devices, feed_forward(): lax.psum_scatter(down_terms.astype(jnp.bfloat16), 'tp', scatter_dimension...  19.6 us
    reduce_scatter x1, waiting for transfers between devices, local(): lax.psum_scatter(attn_terms.astype(jnp.bfloat16), 'tp', scatter_dimension...  16.1 us
    all_gather x1, blocking collectives, local(): rows_all = lax.all_gather(residual, 'tp', axis=0, tiled=True)  15.4 us
    all_gather x1, blocking collectives, local(): middle = lax.all_gather(middle_own, 'tp', axis=0, tiled=True)  13.4 us
    dot_general x1, matrix products, feed_forward(): down_terms = jnp.dot(hidden, w_down, preferred_element_type=jnp.float32)  8.7 us
    dot_general x1, matrix products, feed_forward(): gate_part = jnp.dot(mid_normed, w_gate, preferred_element_type=jnp.float32)  8.54 us
  transfers between devices with their start and end apart: 5, of which 5 were waited for; matrix products, arithmetic and copies ran while one was open for 1% of the time, Pallas kernels for 0%

commit v1 on v0

--- a/solution.py
+++ b/solution.py
@@ -1,6 +1,10 @@
+import math
+
 import jax
 import jax.numpy as jnp
 from jax import lax
+from jax.experimental import pallas as pl
+from jax.experimental.pallas import tpu as pltpu
 from jax.sharding import PartitionSpec as P
 
 D = 8192
@@ -149,9 +153,325 @@
     return (middle_own.astype(jnp.float32) + live_own * ffn).astype(jnp.bfloat16)
 
 
+LANES = 128
+MIB = 2**20
+COVER = 100
+CHUNK = 512
+
+
+def exchange_fits(residual, w_query, w_key, w_gate):
+    tp_count, role_count = lax.axis_size("tp"), lax.axis_size("role")
+    return (
+        tp_count in (2, 4)
+        and role_count in (2, 4)
+        and residual.shape[0] % 8 == 0
+        and w_query.shape[1] % HEAD_DIM == 0
+        and w_key.shape[1] % HEAD_DIM == 0
+        and w_gate.shape[1] % (2 * LANES) == 0
+    )
+
+
+def turn(vectors, cosine, sine):
+    halfway = vectors.shape[-1] // 2
+    cosine, sine = cosine[:, None, :], sine[:, None, :]
+    leading, trailing = vectors[..., :halfway], vectors[..., halfway:]
+    return jnp.concatenate(
+        [leading * cosine - trailing * sine, trailing * cosine + leading * sine], axis=-1
+    )
+
+
+def swap(value, axis, distance):
+    count = lax.axis_size(axis)
+    return lax.ppermute(value, axis, [(i, i ^ distance) for i in range(count)])
+
+
+def in_vmem(value):
+    return pltpu.with_memory_space_constraint(value, pltpu.VMEM)
+
+
+def call(kernel, outs, args, scratch=(), limit=4 * MIB, smem=0, cost=0):
+    specs = [pl.BlockSpec(memory_space=pltpu.SMEM)] * smem
+    specs += [pl.BlockSpec(memory_space=pltpu.VMEM)] * (len(args) - smem)
+    return pl.pallas_call(
+        kernel,
+        out_shape=outs,
+        in_specs=specs,
+        out_specs=[pl.BlockSpec(memory_space=pltpu.VMEM)] * len(outs),
+        scratch_shapes=list(scratch),
+        compiler_params=pltpu.CompilerParams(vmem_limit_bytes=limit),
+        cost_estimate=pl.CostEstimate(flops=cost * 10**9, bytes_accessed=MIB, transcendentals=0),
+    )(*args)
+
+
+def split_three(column):
+    first = column.astype(jnp.bfloat16)
+    left = column - first.astype(jnp.float32)
+    second = left.astype(jnp.bfloat16)
+    third = (left - second.astype(jnp.float32)).astype(jnp.bfloat16)
+    lane = lax.broadcasted_iota(jnp.int32, (column.shape[0], LANES), 1)
+    wide = jnp.where(lane == 0, first.astype(jnp.float32), 0.0)
+    wide = jnp.where(lane == 1, second.astype(jnp.float32), wide)
+    return jnp.where(lane == 2, third.astype(jnp.float32), wide).astype(jnp.bfloat16)
+
+
+def angle_kernel(lengths_ref, cosine_ref, sine_ref):
+    count, halfway = cosine_ref.shape
+    step = lax.broadcasted_iota(jnp.int32, (1, halfway), 1).astype(jnp.float32)
+    frequency = jnp.exp(step * (-2.0 / HEAD_DIM * math.log(rope_base)))
+    angles = jnp.concatenate(
+        [lengths_ref[i].astype(jnp.float32) * frequency for i in range(count)], axis=0
+    )
+    cosine_ref[...] = jnp.cos(angles)
+    sine_ref[...] = jnp.sin(angles)
+
+
+def project_kernel(*refs):
+    *block_refs, gain_ref, wq_ref, wk_ref, wv_ref, out_ref, rows_ref = refs
+    place = lax.axis_index("tp")
+    own = block_refs[0].shape[0]
+    for k, block_ref in enumerate(block_refs):
+        start = pl.multiple_of((place ^ k) * own, own)
+        rows_ref[pl.ds(start, own), :] = block_ref[...].astype(jnp.float32)
+    rows = rows_ref[...]
+    squares = jnp.sum(rows * rows, axis=1, keepdims=True)
+    scaled = (rows * gain_ref[...]).astype(jnp.bfloat16)
+    nq, nk = wq_ref.shape[1], wk_ref.shape[1]
+    for start, w_ref in ((0, wq_ref), (nq, wk_ref), (nq + nk, wv_ref)):
+        out_ref[:, start : start + w_ref.shape[1]] = jnp.dot(
+            scaled, w_ref[...], preferred_element_type=jnp.float32
+        ).astype(jnp.bfloat16)
+    out_ref[:, nq + 2 * nk :] = split_three(squares)
+
+
+def output_kernel(attended_ref, w_ref, *refs):
+    *out_refs, rows_ref = refs
+    place = lax.axis_index("tp")
+    own = out_refs[0].shape[0]
+    rows_ref[...] = jnp.dot(attended_ref[...], w_ref[...], preferred_element_type=jnp.float32)
+    for k, out_ref in enumerate(out_refs):
+        start = pl.multiple_of((place ^ k) * own, own)
+        out_ref[...] = rows_ref[pl.ds(start, own), :].astype(jnp.bfloat16)
+
+
+def add_kernel(served_ref, stream_ref, *refs):
+    *term_refs, out_ref = refs
+    own = stream_ref.shape[0]
+    start = lax.axis_index("tp") * own
+    row = lax.broadcasted_iota(jnp.int32, (own, LANES), 0)
+    live = jnp.zeros((own, LANES), jnp.int32)
+    for i in range(own):
+        live = jnp.where(row == i, served_ref[start + i], live)
+    live = live.astype(jnp.float32)[:, :1]
+    total = term_refs[0][...].astype(jnp.float32)
+    for term_ref in term_refs[1:]:
+        total = total + term_ref[...].astype(jnp.float32)
+    out_ref[...] = (stream_ref[...].astype(jnp.float32) + live * total).astype(
+        jnp.bfloat16
+    )
+
+
+def gate_kernel(*refs):
+    *block_refs, gain_ref, w_ref, scaled_ref, keep_ref, send_ref = refs
+    rows = jnp.concatenate([ref[...].astype(jnp.float32) for ref in block_refs], axis=0)
+    squares = jnp.sum(rows * rows, axis=1, keepdims=True)
+    scaled = (rows * gain_ref[...]).astype(jnp.bfloat16)
+    scaled_ref[...] = scaled
+    width = w_ref.shape[1] // 2
+    halves(scaled, w_ref, keep_ref, send_ref, width)
+    tail = split_three(squares)
+    send_ref[:, width:] = tail
+    keep_ref[:, width:] = tail.astype(keep_ref.dtype)
+
+
+def up_kernel(scaled_ref, w_ref, keep_ref, send_ref):
+    halves(scaled_ref[...], w_ref, keep_ref, send_ref, w_ref.shape[1] // 2)
+
+
+def halves(scaled, w_ref, keep_ref, send_ref, width):
+    half = lax.rem(lax.axis_index("role"), 2)
+    for side, out_ref in ((1 - half, send_ref), (half, keep_ref)):
+        for at in range(0, width, CHUNK):
+            size = min(CHUNK, width - at)
+            start = pl.multiple_of(side * width + at, LANES)
+            out_ref[:, at : at + size] = jnp.dot(
+                scaled, w_ref[:, pl.ds(start, size)], preferred_element_type=jnp.float32
+            ).astype(out_ref.dtype)
+
+
+def pair_gate_kernel(keep_ref, got_ref, out_ref):
+    wide = out_ref.shape[1] - LANES
+    out_ref[:, :wide] = (
+        keep_ref[:, :wide] + got_ref[:, :wide].astype(jnp.float32)
+    ).astype(jnp.bfloat16)
+    squares = jnp.sum(
+        keep_ref[:, wide:] + got_ref[:, wide:].astype(jnp.float32), axis=1, keepdims=True
+    )
+    out_ref[:, wide:] = split_three(squares)
+
+
+def pair_up_kernel(keep_ref, got_ref, out_ref):
+    out_ref[...] = (keep_ref[...] + got_ref[...].astype(jnp.float32)).astype(jnp.bfloat16)
+
+
+def hidden_kernel(gate_ref, gate_got_ref, up_ref, up_got_ref, out_ref):
+    width = out_ref.shape[1]
+    squares = jnp.sum(
+        gate_ref[:, width:].astype(jnp.float32) + gate_got_ref[:, width:].astype(jnp.float32),
+        axis=1,
+        keepdims=True,
+    )
+    inverse = lax.rsqrt(squares / D + epsilon)
+    gate = gate_ref[:, :width].astype(jnp.float32) + gate_got_ref[:, :width].astype(jnp.float32)
+    up = up_ref[...].astype(jnp.float32) + up_got_ref[...].astype(jnp.float32)
+    gate, up = gate * inverse, up * inverse
+    out_ref[...] = (gate / (1.0 + jnp.exp(-gate)) * up).astype(jnp.bfloat16)
+
+
+def down_kernel(own_ref, other_ref, w_ref, *out_refs):
+    half = lax.rem(lax.axis_index("role"), 2)
+    width = own_ref.shape[1]
+    mine = pl.ds(pl.multiple_of(half * width, LANES), width)
+    theirs = pl.ds(pl.multiple_of((1 - half) * width, LANES), width)
+    own = out_refs[0].shape[0]
+    for at in range(0, w_ref.shape[1], CHUNK):
+        part = slice(at, min(at + CHUNK, w_ref.shape[1]))
+        rows = jnp.dot(own_ref[...], w_ref[mine, part], preferred_element_type=jnp.float32)
+        rows = rows + jnp.dot(
+            other_ref[...], w_ref[theirs, part], preferred_element_type=jnp.float32
+        )
+        for k, out_ref in enumerate(out_refs):
+            out_ref[:, part] = rows[k * own : (k + 1) * own].astype(jnp.bfloat16)
+
+
+def local_exchange(
+    residual,
+    attn_gain,
+    w_query,
+    w_key,
+    w_value,
+    w_output,
+    cache_keys,
+    cache_values,
+    lengths,
+    served,
+    ffn_gain,
+    w_gate,
+    w_up,
+    w_down,
+):
+    if not exchange_fits(residual, w_query, w_key, w_gate):
+        return local(
+            residual,
+            attn_gain,
+            w_query,
+            w_key,
+            w_value,
+            w_output,
+            cache_keys,
+            cache_values,
+            lengths,
+            served,
+            ffn_gain,
+            w_gate,
+            w_up,
+            w_down,
+        )
+    tp_count, role_count = lax.axis_size("tp"), lax.axis_size("role")
+    devices = tp_count * role_count
+    own, features = residual.shape
+    rows = own * tp_count
+    each = rows // devices
+    block = jax.ShapeDtypeStruct((own, features), jnp.bfloat16)
+
+    table = jax.ShapeDtypeStruct((each, HEAD_DIM // 2), jnp.float32)
+    cosine, sine = call(angle_kernel, [table] * 2, [lengths], smem=1, cost=COVER)
+    blocks = [residual] + [swap(residual, "tp", k) for k in range(1, tp_count)]
+    query_cols, kv_cols = w_query.shape[1], w_key.shape[1]
+    payload = query_cols + 2 * kv_cols + LANES
+    (sums,) = call(
+        project_kernel,
+        [jax.ShapeDtypeStruct((rows, payload), jnp.bfloat16)],
+        [*blocks, attn_gain[None, :], in_vmem(w_query), in_vmem(w_key), in_vmem(w_value)],
+        scratch=[pltpu.VMEM((rows, features), jnp.float32)],
+    )
+    parts = lax.all_to_all(sums.reshape(devices, each, payload), ("role", "tp"), 0, 0)
+    parts = parts.reshape(role_count, tp_count, each, payload).astype(jnp.float32)
+    gathered = jnp.sum(parts, axis=0).transpose(1, 0, 2)
+    squares = jnp.sum(gathered[:, :1, query_cols + 2 * kv_cols :], axis=2, keepdims=True)
+    gathered = gathered[:, :, : query_cols + 2 * kv_cols] * lax.rsqrt(squares / D + epsilon)
+    queries = gathered[:, :, :query_cols].reshape(each, HEADS, HEAD_DIM)
+    new_key = gathered[:, :, query_cols : query_cols + kv_cols].reshape(each, KV_HEADS, HEAD_DIM)
+    new_value = (
+        gathered[:, :, query_cols + kv_cols :]
+        .reshape(each, KV_HEADS, HEAD_DIM)
+        .astype(jnp.bfloat16)
+    )
+    queries = turn(queries, cosine, sine).astype(jnp.bfloat16)
+    new_key = turn(new_key, cosine, sine).astype(jnp.bfloat16)
+    attended = attend(queries, new_key, new_value, cache_keys, cache_values, lengths)
+    by_block = attended.reshape(each, tp_count, query_cols).transpose(1, 0, 2)
+    sent = jnp.broadcast_to(by_block[None], (role_count, tp_count, each, query_cols))
+    heads = lax.all_to_all(
+        sent.reshape(devices, each, query_cols), ("role", "tp"), 0, 0
+    ).reshape(rows, query_cols)
+
+    terms = call(
+        output_kernel,
+        [block] * tp_count,
+        [heads, in_vmem(w_output)],
+        cost=COVER,
+        scratch=[pltpu.VMEM((rows, features), jnp.float32)],
+    )
+    terms = [terms[0]] + [swap(terms[k], "tp", k) for k in range(1, tp_count)]
+    (middle,) = call(add_kernel, [block], [served, residual, *terms], smem=1)
+
+    blocks = [middle] + [swap(middle, "tp", k) for k in range(1, tp_count)]
+    width = w_gate.shape[1] // 2
+    wide = width + LANES
+    scaled, gate, gate_send = call(
+        gate_kernel,
+        [
+            jax.ShapeDtypeStruct((rows, features), jnp.bfloat16),
+            jax.ShapeDtypeStruct((rows, wide), jnp.float32),
+            jax.ShapeDtypeStruct((rows, wide), jnp.bfloat16),
+        ],
+        [*blocks, ffn_gain[None, :], in_vmem(w_gate)],
+        cost=COVER,
+    )
+    gate_got = swap(gate_send, "role", 1)
+    up, up_send = call(
+        up_kernel,
+        [
+            jax.ShapeDtypeStruct((rows, width), jnp.float32),
+            jax.ShapeDtypeStruct((rows, width), jnp.bfloat16),
+        ],
+        [scaled, in_vmem(w_up)],
+        cost=COVER,
+    )
+    up_got = swap(up_send, "role", 1)
+    if role_count > 2:
+        (gate,) = call(
+            pair_gate_kernel, [jax.ShapeDtypeStruct((rows, wide), jnp.bfloat16)], [gate, gate_got]
+        )
+        gate_got = swap(gate, "role", 2)
+        (up,) = call(
+            pair_up_kernel, [jax.ShapeDtypeStruct((rows, width), jnp.bfloat16)], [up, up_got]
+        )
+        up_got = swap(up, "role", 2)
+    (hidden,) = call(
+        hidden_kernel,
+        [jax.ShapeDtypeStruct((rows, width), jnp.bfloat16)],
+        [gate, gate_got, up, up_got],
+    )
+    other = swap(hidden, "role", 1)
+    terms = call(down_kernel, [block] * tp_count, [hidden, other, in_vmem(w_down)])
+    terms = [terms[0]] + [swap(terms[k], "tp", k) for k in range(1, tp_count)]
+    return call(add_kernel, [block], [served, middle, *terms], smem=1)[0]
+
+
 def solution(mesh):
     return jax.shard_map(
-        local,
+        local_exchange,
         mesh=mesh,
         in_specs=(
             P(("groups", "tp"), "role"),

time: 209 us -> 85.1 us (0.41)
  waiting for transfers between devices: 93 us -> 26.5 us
  blocking collectives: 53.3 us -> 9.22 us
  matrix products: 37 us -> 0.78 us
  starting transfers between devices: 4.69 us -> 26.1 us
  between operations: 13.2 us -> 0.24 us
  Pallas kernels: 0 us -> 12.3 us
  local copies, waits for them, and re-layouts: 1.42 us -> 8.87 us
  other arithmetic: 5.94 us -> 0.8 us
    reduce_scatter x3 -> x0, waiting for transfers between devices: 56.3 us -> none  [the longest x1 20.6 us: local(): lax.psum_scatter(partial_value.astype(jnp.bfloat16), 'role', scatter_dime...]
    dot_general x7 -> x0, matrix products: 35.2 us -> none  [the longest x1 8.7 us: feed_forward(): down_terms = jnp.dot(hidden, w_down, preferred_element_type=jnp.float32)]
    all_gather x3 -> x0, blocking collectives: 34 us -> none  [the longest x1 15.4 us: local(): rows_all = lax.all_gather(residual, 'tp', axis=0, tiled=True)]
    psum x1 -> x0, waiting for transfers between devices: 31.7 us -> none  [feed_forward(): lax.psum(up_part.astype(jnp.bfloat16), 'role').astype(jnp.float32)]
    ppermute x0 -> x17, starting transfers between devices: none -> 21.8 us  [swap(): return lax.ppermute(value, axis, [(i, i ^ distance) for i in range(count)])]
    ppermute x0 -> x17, waiting for transfers between devices: none -> 19.7 us  [swap(): return lax.ppermute(value, axis, [(i, i ^ distance) for i in range(count)])]
    pallas_call x0 -> x11, Pallas kernels: none -> 12.3 us  [call(): pl.pallas_call(kernel, out_shape=outs, in_specs=specs, out_specs=[pl.Bloc...]
    psum x2 -> x0, blocking collectives: 11.3 us -> none  [the longest x1 5.66 us: local(): squares = lax.psum(jnp.sum(widened * widened, axis=1), 'role')]
  transfers between devices with their start and end apart: 5 -> 18, of which waited for: 5 -> 12; matrix products, arithmetic and copies ran while one was open for 1% -> 0% of each run, Pallas kernels for 0% -> 4%
where the time goes in v1:
time: 85.1 us; the launch traced here: 84.8 us
  waiting for transfers between devices  26.5 us (31%)
  starting transfers between devices  26.1 us (31%)
  Pallas kernels  12.3 us (14%)
  blocking collectives  9.22 us (11%)
  local copies, waits for them, and re-layouts  8.87 us (10%)
    ppermute x17, starting transfers between devices, swap(): return lax.ppermute(value, axis, [(i, i ^ distance) for i in range(count)])  21.8 us
    ppermute x17, waiting for transfers between devices, swap(): return lax.ppermute(value, axis, [(i, i ^ distance) for i in range(count)])  19.7 us
    pallas_call x11, Pallas kernels, call(): pl.pallas_call(kernel, out_shape=outs, in_specs=specs, out_specs=[pl.Bloc...  12.3 us
    all_to_all x1, blocking collectives, local_exchange(): lax.all_to_all(sent.reshape(devices, each, query_cols), ('role', 'tp'), 0...  9.22 us
    unnamed x30, local copies, waits for them, and re-layouts  8.05 us
    all_to_all x1, waiting for transfers between devices, local_exchange(): lax.all_to_all(sums.reshape(devices, each, payload), ('role', 'tp'), 0, 0)  6.8 us
    all_to_all x1, starting transfers between devices, local_exchange(): lax.all_to_all(sums.reshape(devices, each, payload), ('role', 'tp'), 0, 0)  4.32 us
  transfers between devices with their start and end apart: 18, of which 12 were waited for; matrix products, arithmetic and copies ran while one was open for 0% of the time, Pallas kernels for 4%

profile of v1, /device:TPU:0, one launch (start us, length us, event | category | flops | bytes accessed | tf_op | source)
XLA Modules:
  0.0 84.8 jit_solution(13448959444154905529)
XLA Ops:
  0.0 5.2 %collective-permute-start.2 = (bf16[8,2048]{1,0:T(8,128)(2,1)}, bf16[8,2048]{1,0:T(8,128)(2,1)S(1)}, u32[]{:S(2)}, u32[]{:S(2)}) collective-permute-start(bf16[8,2048]{1,0:T(8,128)(2,1)} %stream_ref.1), channel_id=1, source_target_pairs={{0,3},{1,2},{2,1},{3,0},{4,7},{5,6},{6,5},{7,4},{8,11},{9,10},{10,... | collective-permute-start | bytes 98312 | tf_op jit(solution)/shard_map/ppermute | solution.py:185
  5.2 0.6 collective-permute-start
  5.8 0.7 copy-done.12
  7.3 2.9 %collective-permute-done.1.refs_2_ = bf16[8,2048]{1,0:T(8,128)(2,1)S(1)} collective-permute-done((bf16[8,2048]{1,0:T(8,128)(2,1)}, bf16[8,2048]{1,0:T(8,128)(2,1)S(1)}, u32[]{:S(2)}, u32[]{:S(2)}) %collective-permute-start.1) | collective-permute-done | bytes 32800 | tf_op jit(solution)/shard_map/ppermute | solution.py:185
  10.2 1.0 %shard_map.136 = bf16[32,1408]{1,0:T(8,128)(2,1)S(1)} custom-call(bf16[8,2048]{1,0:T(8,128)(2,1)S(1)} %copy-done.5, bf16[8,2048]{1,0:T(8,128)(2,1)S(1)} %collective-permute-done.refs_1_, bf16[8,2048]{1,0:T(8,128)(2,1)S(1)} %collective-permute-done.1.refs_2_, bf16[8,2048]{1,0:T(8,128)(2,1)S(1)} %collective-permute-done.2.refs_3_, f32[1,2048]{1,0:T(1,128)S(1)} %bitcast.35, ...), custom_call_target="tpu_custom_call" | custom-call | bytes 1048576 | tf_op jit(solution)/shard_map/pallas_call | solution.py:195
  11.2 0.7 reshape.65
  11.9 4.3 %all-to-all-start = ((bf16[16,2,1408]{2,1,0:T(2,128)(2,1)}), bf16[16,2,1408]{2,1,0:T(2,128)(2,1)S(1)}, u32[]{:S(2)}, u32[]{:S(2)}) async-start(bf16[16,2,1408]{2,1,0:T(2,128)(2,1)} %reshape.65), calls=%async_computation | async-start | bytes 180224 | tf_op jit(solution)/shard_map/all_to_all | solution.py:397
  16.4 6.8 %all-to-all-done = bf16[16,2,1408]{2,1,0:T(2,128)(2,1)S(1)} async-done(((bf16[16,2,1408]{2,1,0:T(2,128)(2,1)}), bf16[16,2,1408]{2,1,0:T(2,128)(2,1)S(1)}, u32[]{:S(2)}, u32[]{:S(2)}) %all-to-all-start) | async-done | bytes 90144 | tf_op jit(solution)/shard_map/all_to_all | solution.py:397
  24.9 9.2 %all_to_all.10 = bf16[16,2,1024]{2,1,0:T(2,128)(2,1)S(1)} all-to-all(bf16[16,2,1024]{2,1,0:T(2,128)(2,1)S(1)} %bitcast.38), channel_id=1, replica_groups=mesh['groups'=2,'role'=4,'tp'=4] {'role','tp'}, dimensions={0} | all-to-all | bytes 131072 | tf_op jit(solution)/shard_map/all_to_all | solution.py:414
  34.1 2.2 %copy-done.10 = bf16[1024,2048]{1,0:T(8,128)(2,1)S(1)} copy-done((bf16[1024,2048]{1,0:T(8,128)(2,1)S(1)}, bf16[1024,2048]{1,0:T(8,128)(2,1)}, u32[]{:S(2)}) %copy-start.10) | copy-done | bytes 4194328
  36.3 0.8 shard_map.138
  37.6 1.0 %collective-permute-start.4 = (bf16[8,2048]{1,0:T(8,128)(2,1)S(1)}, bf16[8,2048]{1,0:T(8,128)(2,1)S(1)}, u32[]{:S(2)}, u32[]{:S(2)}) collective-permute-start(bf16[8,2048]{1,0:T(8,128)(2,1)S(1)} %get-tuple-element.24), channel_id=1, source_target_pairs={{0,2},{1,3},{2,0},{3,1},{4,6},{5,7},{6,4},{7,5},{8,10},{9,11},{10,... | collective-permute-start | bytes 98312 | tf_op jit(solution)/shard_map/ppermute | solution.py:185
  38.5 3.1 %collective-permute-start.5 = (bf16[8,2048]{1,0:T(8,128)(2,1)S(1)}, bf16[8,2048]{1,0:T(8,128)(2,1)S(1)}, u32[]{:S(2)}, u32[]{:S(2)}) collective-permute-start(bf16[8,2048]{1,0:T(8,128)(2,1)S(1)} %get-tuple-element.25), channel_id=1, source_target_pairs={{0,3},{1,2},{2,1},{3,0},{4,7},{5,6},{6,5},{7,4},{8,11},{9,10},{10,... | collective-permute-start | bytes 98312 | tf_op jit(solution)/shard_map/ppermute | solution.py:185
  41.6 1.5 %collective-permute-done.4.refs_2_ = bf16[8,2048]{1,0:T(8,128)(2,1)S(1)} collective-permute-done((bf16[8,2048]{1,0:T(8,128)(2,1)S(1)}, bf16[8,2048]{1,0:T(8,128)(2,1)S(1)}, u32[]{:S(2)}, u32[]{:S(2)}) %collective-permute-start.4) | collective-permute-done | bytes 32800 | tf_op jit(solution)/shard_map/ppermute | solution.py:185
  43.1 1.2 %collective-permute-done.5.refs_3_ = bf16[8,2048]{1,0:T(8,128)(2,1)S(1)} collective-permute-done((bf16[8,2048]{1,0:T(8,128)(2,1)S(1)}, bf16[8,2048]{1,0:T(8,128)(2,1)S(1)}, u32[]{:S(2)}, u32[]{:S(2)}) %collective-permute-start.5) | collective-permute-done | bytes 32800 | tf_op jit(solution)/shard_map/ppermute | solution.py:185
  44.8 3.1 %collective-permute-start.8 = (bf16[8,2048]{1,0:T(8,128)(2,1)S(1)}, bf16[8,2048]{1,0:T(8,128)(2,1)S(1)}, u32[]{:S(2)}, u32[]{:S(2)}) collective-permute-start(bf16[8,2048]{1,0:T(8,128)(2,1)S(1)} %shard_map.139.refs_0_.stream_ref), channel_id=1, source_target_pairs={{0,3},{1,2},{2,1},{3,0},{4,7},{5,6},{6,5},{7,4},{8,11},{9,10},{10,... | collective-permute-start | bytes 98312 | tf_op jit(solution)/shard_map/ppermute | solution.py:185
  48.0 1.3 %collective-permute-start.6 = (bf16[8,2048]{1,0:T(8,128)(2,1)S(1)}, bf16[8,2048]{1,0:T(8,128)(2,1)S(1)}, u32[]{:S(2)}, u32[]{:S(2)}) collective-permute-start(bf16[8,2048]{1,0:T(8,128)(2,1)S(1)} %shard_map.139.refs_0_.stream_ref), channel_id=1, source_target_pairs={{0,1},{1,0},{2,3},{3,2},{4,5},{5,4},{6,7},{7,6},{8,9},{9,8},{10,11... | collective-permute-start | bytes 98312 | tf_op jit(solution)/shard_map/ppermute | solution.py:185
  49.3 1.3 %collective-permute-done.8.refs_3_ = bf16[8,2048]{1,0:T(8,128)(2,1)S(1)} collective-permute-done((bf16[8,2048]{1,0:T(8,128)(2,1)S(1)}, bf16[8,2048]{1,0:T(8,128)(2,1)S(1)}, u32[]{:S(2)}, u32[]{:S(2)}) %collective-permute-start.8) | collective-permute-done | bytes 32800 | tf_op jit(solution)/shard_map/ppermute | solution.py:185
  50.6 2.2 %collective-permute-done.7.refs_2_ = bf16[8,2048]{1,0:T(8,128)(2,1)S(1)} collective-permute-done((bf16[8,2048]{1,0:T(8,128)(2,1)S(1)}, bf16[8,2048]{1,0:T(8,128)(2,1)S(1)}, u32[]{:S(2)}, u32[]{:S(2)}) %collective-permute-start.7) | collective-permute-done | bytes 32800 | tf_op jit(solution)/shard_map/ppermute | solution.py:185
  52.8 2.6 %shard_map.140 = (bf16[32,2048]{1,0:T(8,128)(2,1)S(1)}, f32[32,1920]{1,0:T(8,128)S(1)}, bf16[32,1920]{1,0:T(8,128)(2,1)S(1)}) custom-call(bf16[8,2048]{1,0:T(8,128)(2,1)S(1)} %shard_map.139.refs_0_.stream_ref, bf16[8,2048]{1,0:T(8,128)(2,1)S(1)} %collective-permute-done.6.refs_1_, bf16[8,2048]{1,0:T(8,128)(2,1)S(1)} %collective-permute-done.7.refs_2_, ...), custom_call_target="tpu_custom_call" | custom-call | flops 99999997952 | bytes 1048576 | tf_op jit(solution)/shard_map/pallas_call | solution.py:195
  55.4 5.2 %copy-done.9 = bf16[2048,3584]{1,0:T(8,128)(2,1)S(1)} copy-done((bf16[2048,3584]{1,0:T(8,128)(2,1)S(1)}, bf16[2048,3584]{1,0:T(8,128)(2,1)}, u32[]{:S(2)}) %copy-start.9) | copy-done | bytes 14680088
  60.6 2.6 %shard_map.142 = (f32[32,1792]{1,0:T(8,128)S(1)}, bf16[32,1792]{1,0:T(8,128)(2,1)S(1)}) custom-call(bf16[32,2048]{1,0:T(8,128)(2,1)S(1)} %get-tuple-element.28.scaled_ref, bf16[2048,3584]{1,0:T(8,128)(2,1)S(1)} %copy-done.9), custom_call_target="tpu_custom_call" | custom-call | flops 99999997952 | bytes 1048576 | tf_op jit(solution)/shard_map/pallas_call | solution.py:195
  63.8 0.8 collective-permute-start.10
  64.7 1.3 %collective-permute-start.12 = (bf16[32,1792]{1,0:T(8,128)(2,1)S(1)}, bf16[32,1792]{1,0:T(8,128)(2,1)S(1)}, u32[]{:S(2)}, u32[]{:S(2)}) collective-permute-start(bf16[32,1792]{1,0:T(8,128)(2,1)S(1)} %shard_map.143.up_ref), channel_id=1, source_target_pairs={{0,8},{4,12},{8,0},{12,4},{1,9},{5,13},{9,1},{13,5},{2,10},{6,14},... | collective-permute-start | bytes 344072 | tf_op jit(solution)/shard_map/ppermute | solution.py:185
  66.0 5.6 %collective-permute-done.12.up_got_ref = bf16[32,1792]{1,0:T(8,128)(2,1)S(1)} collective-permute-done((bf16[32,1792]{1,0:T(8,128)(2,1)S(1)}, bf16[32,1792]{1,0:T(8,128)(2,1)S(1)}, u32[]{:S(2)}, u32[]{:S(2)}) %collective-permute-start.12) | collective-permute-done | bytes 114720 | tf_op jit(solution)/shard_map/ppermute | solution.py:185
  71.8 1.3 %collective-permute-done.13.other_ref = bf16[32,1792]{1,0:T(8,128)(2,1)S(1)} collective-permute-done((bf16[32,1792]{1,0:T(8,128)(2,1)S(1)}, bf16[32,1792]{1,0:T(8,128)(2,1)S(1)}, u32[]{:S(2)}, u32[]{:S(2)}) %collective-permute-start.13) | collective-permute-done | bytes 114720 | tf_op jit(solution)/shard_map/ppermute | solution.py:185
  73.2 2.6 %shard_map.145 = (bf16[8,2048]{1,0:T(8,128)(2,1)S(1)}, bf16[8,2048]{1,0:T(8,128)(2,1)S(1)}, bf16[8,2048]{1,0:T(8,128)(2,1)S(1)}, bf16[8,2048]{1,0:T(8,128)(2,1)S(1)}) custom-call(bf16[32,1792]{1,0:T(8,128)(2,1)S(1)} %shard_map.144.own_ref, bf16[32,1792]{1,0:T(8,128)(2,1)S(1)} %collective-permute-done.13.other_ref, bf16[3584,2048]{1,0:T(8,128)(2,1)S(1)} %copy-done.1), custom_call_target="tpu_custom_call" | custom-call | bytes 1048576 | tf_op jit(solution)/shard_map/pallas_call | solution.py:195
  76.2 1.7 %collective-permute-start.15 = (bf16[8,2048]{1,0:T(8,128)(2,1)S(1)}, bf16[8,2048]{1,0:T(8,128)(2,1)S(1)}, u32[]{:S(2)}, u32[]{:S(2)}) collective-permute-start(bf16[8,2048]{1,0:T(8,128)(2,1)S(1)} %get-tuple-element.33), channel_id=1, source_target_pairs={{0,2},{1,3},{2,0},{3,1},{4,6},{5,7},{6,4},{7,5},{8,10},{9,11},{10,... | collective-permute-start | bytes 98312 | tf_op jit(solution)/shard_map/ppermute | solution.py:185
  77.9 2.3 %collective-permute-start.16 = (bf16[8,2048]{1,0:T(8,128)(2,1)S(1)}, bf16[8,2048]{1,0:T(8,128)(2,1)S(1)}, u32[]{:S(2)}, u32[]{:S(2)}) collective-permute-start(bf16[8,2048]{1,0:T(8,128)(2,1)S(1)} %get-tuple-element.34), channel_id=1, source_target_pairs={{0,3},{1,2},{2,1},{3,0},{4,7},{5,6},{6,5},{7,4},{8,11},{9,10},{10,... | collective-permute-start | bytes 98312 | tf_op jit(solution)/shard_map/ppermute | solution.py:185
  80.2 1.1 %collective-permute-done.15.refs_2_ = bf16[8,2048]{1,0:T(8,128)(2,1)S(1)} collective-permute-done((bf16[8,2048]{1,0:T(8,128)(2,1)S(1)}, bf16[8,2048]{1,0:T(8,128)(2,1)S(1)}, u32[]{:S(2)}, u32[]{:S(2)}) %collective-permute-start.15) | collective-permute-done | bytes 32800 | tf_op jit(solution)/shard_map/ppermute | solution.py:185
  81.3 2.3 %collective-permute-done.16.refs_3_ = bf16[8,2048]{1,0:T(8,128)(2,1)S(1)} collective-permute-done((bf16[8,2048]{1,0:T(8,128)(2,1)S(1)}, bf16[8,2048]{1,0:T(8,128)(2,1)S(1)}, u32[]{:S(2)}, u32[]{:S(2)}) %collective-permute-start.16) | collective-permute-done | bytes 32800 | tf_op jit(solution)/shard_map/ppermute | solution.py:185
  83.6 1.2 %shard_map.146 = bf16[8,2048]{1,0:T(8,128)(2,1)} custom-call(s32[32]{0:T(128)S(1)} %copy-done.7, bf16[8,2048]{1,0:T(8,128)(2,1)S(1)} %shard_map.139.refs_0_.stream_ref, bf16[8,2048]{1,0:T(8,128)(2,1)S(1)} %get-tuple-element.31.refs_0_, bf16[8,2048]{1,0:T(8,128)(2,1)S(1)} %collective-permute-done.14.refs_1_, ...), custom_call_target="tpu_custom_call" | custom-call | bytes 1048576 | tf_op jit(solution)/shard_map/pallas_call | solution.py:195
  (69 shorter events, 4.9 us)
Async XLA Ops:
  0.0 23.9 %copy-start = (bf16[2,256,512]{2,1,0:T(8,128)(2,1)S(1)}, bf16[2,256,512]{2,1,0:T(8,128)(2,1)}, u32[]{:S(2)}) copy-start(bf16[2,256,512]{2,1,0:T(8,128)(2,1)} %param.20) | copy-start | bytes 1572868
  0.0 10.2 %copy-start.5 = (bf16[8,2048]{1,0:T(8,128)(2,1)S(1)}, bf16[8,2048]{1,0:T(8,128)(2,1)}, u32[]{:S(2)}) copy-start(bf16[8,2048]{1,0:T(8,128)(2,1)} %stream_ref.1) | copy-start | bytes 98308
  0.0 10.2 %copy-start.4 = (bf16[2048,128]{1,0:T(8,128)(2,1)S(1)}, bf16[2048,128]{1,0:T(8,128)(2,1)}, u32[]{:S(2)}) copy-start(bf16[2048,128]{1,0:T(8,128)(2,1)} %refs_7_.1) | copy-start | bytes 1572868
  0.0 10.2 %copy-start.3 = (bf16[2048,128]{1,0:T(8,128)(2,1)S(1)}, bf16[2048,128]{1,0:T(8,128)(2,1)}, u32[]{:S(2)}) copy-start(bf16[2048,128]{1,0:T(8,128)(2,1)} %refs_6_.1) | copy-start | bytes 1572868
  0.0 10.2 %copy-start.2 = (bf16[2048,1024]{1,0:T(8,128)(2,1)S(1)}, bf16[2048,1024]{1,0:T(8,128)(2,1)}, u32[]{:S(2)}) copy-start(bf16[2048,1024]{1,0:T(8,128)(2,1)} %refs_5_.2) | copy-start | bytes 12582916
  0.0 10.2 %copy-start.6 = (f32[2048]{0:T(1024)S(1)}, f32[2048]{0:T(1024)}, u32[]{:S(2)}) copy-start(f32[2048]{0:T(1024)} %param.15) | copy-start | bytes 24580
  0.0 7.3 %collective-permute-start.2 = (bf16[8,2048]{1,0:T(8,128)(2,1)}, bf16[8,2048]{1,0:T(8,128)(2,1)S(1)}, u32[]{:S(2)}, u32[]{:S(2)}) collective-permute-start(bf16[8,2048]{1,0:T(8,128)(2,1)} %stream_ref.1), channel_id=1, source_target_pairs={{0,3},{1,2},{2,1},{3,0},{4,7},{5,6},{6,5},{7,4},{8,11},{9,10},{10,... | collective-permute-start | bytes 98312 | tf_op jit(solution)/shard_map/ppermute | solution.py:185
  5.2 5.0 %collective-permute-start.1 = (bf16[8,2048]{1,0:T(8,128)(2,1)}, bf16[8,2048]{1,0:T(8,128)(2,1)S(1)}, u32[]{:S(2)}, u32[]{:S(2)}) collective-permute-start(bf16[8,2048]{1,0:T(8,128)(2,1)} %stream_ref.1), channel_id=1, source_target_pairs={{0,2},{1,3},{2,0},{3,1},{4,6},{5,7},{6,4},{7,5},{8,10},{9,11},{10,... | collective-permute-start | bytes 98312 | tf_op jit(solution)/shard_map/ppermute | solution.py:185
  5.2 5.0 %collective-permute-start = (bf16[8,2048]{1,0:T(8,128)(2,1)}, bf16[8,2048]{1,0:T(8,128)(2,1)S(1)}, u32[]{:S(2)}, u32[]{:S(2)}) collective-permute-start(bf16[8,2048]{1,0:T(8,128)(2,1)} %stream_ref.1), channel_id=1, source_target_pairs={{0,1},{1,0},{2,3},{3,2},{4,5},{5,4},{6,7},{7,6},{8,9},{9,8},{10,11... | collective-permute-start | bytes 98312 | tf_op jit(solution)/shard_map/ppermute | solution.py:185
  6.5 9.8 %copy-start.13 = (s32[2]{0:T(128)S(1)}, s32[2]{0:T(128)}, u32[]{:S(2)}) copy-start(s32[2]{0:T(128)} %lengths_ref.1) | copy-start | bytes 28
  6.5 18.0 %copy-start.14 = (bf16[2,256,512]{2,1,0:T(8,128)(2,1)S(1)}, bf16[2,256,512]{2,1,0:T(8,128)(2,1)}, u32[]{:S(2)}) copy-start(bf16[2,256,512]{2,1,0:T(8,128)(2,1)} %param.21) | copy-start | bytes 1572868
  11.9 11.2 %all-to-all-start = ((bf16[16,2,1408]{2,1,0:T(2,128)(2,1)}), bf16[16,2,1408]{2,1,0:T(2,128)(2,1)S(1)}, u32[]{:S(2)}, u32[]{:S(2)}) async-start(bf16[16,2,1408]{2,1,0:T(2,128)(2,1)} %reshape.65), calls=%async_computation | async-start | bytes 180224 | tf_op jit(solution)/shard_map/all_to_all | solution.py:397
  34.1 2.2 %copy-start.10 = (bf16[1024,2048]{1,0:T(8,128)(2,1)S(1)}, bf16[1024,2048]{1,0:T(8,128)(2,1)}, u32[]{:S(2)}) copy-start(bf16[1024,2048]{1,0:T(8,128)(2,1)} %w_ref.3) | copy-start | bytes 12582916
  36.3 7.9 %copy-start.7 = (s32[32]{0:T(128)S(1)}, s32[32]{0:T(128)}, u32[]{:S(2)}) copy-start(s32[32]{0:T(128)} %served_ref.3) | copy-start | bytes 388
  36.3 16.5 %copy-start.8 = (bf16[2048,3584]{1,0:T(8,128)(2,1)S(1)}, bf16[2048,3584]{1,0:T(8,128)(2,1)}, u32[]{:S(2)}) copy-start(bf16[2048,3584]{1,0:T(8,128)(2,1)} %refs_5_.3) | copy-start | bytes 44040196
  36.3 16.5 %copy-start.11 = (f32[2048]{0:T(1024)S(1)}, f32[2048]{0:T(1024)}, u32[]{:S(2)}) copy-start(f32[2048]{0:T(1024)} %param.24) | copy-start | bytes 24580
  37.1 4.5 %collective-permute-start.3 = (bf16[8,2048]{1,0:T(8,128)(2,1)S(1)}, bf16[8,2048]{1,0:T(8,128)(2,1)S(1)}, u32[]{:S(2)}, u32[]{:S(2)}) collective-permute-start(bf16[8,2048]{1,0:T(8,128)(2,1)S(1)} %get-tuple-element.23), channel_id=1, source_target_pairs={{0,1},{1,0},{2,3},{3,2},{4,5},{5,4},{6,7},{7,6},{8,9},{9,8},{10,11... | collective-permute-start | bytes 98312 | tf_op jit(solution)/shard_map/ppermute | solution.py:185
  37.6 5.5 %collective-permute-start.4 = (bf16[8,2048]{1,0:T(8,128)(2,1)S(1)}, bf16[8,2048]{1,0:T(8,128)(2,1)S(1)}, u32[]{:S(2)}, u32[]{:S(2)}) collective-permute-start(bf16[8,2048]{1,0:T(8,128)(2,1)S(1)} %get-tuple-element.24), channel_id=1, source_target_pairs={{0,2},{1,3},{2,0},{3,1},{4,6},{5,7},{6,4},{7,5},{8,10},{9,11},{10,... | collective-permute-start | bytes 98312 | tf_op jit(solution)/shard_map/ppermute | solution.py:185
  38.5 5.7 %collective-permute-start.5 = (bf16[8,2048]{1,0:T(8,128)(2,1)S(1)}, bf16[8,2048]{1,0:T(8,128)(2,1)S(1)}, u32[]{:S(2)}, u32[]{:S(2)}) collective-permute-start(bf16[8,2048]{1,0:T(8,128)(2,1)S(1)} %get-tuple-element.25), channel_id=1, source_target_pairs={{0,3},{1,2},{2,1},{3,0},{4,7},{5,6},{6,5},{7,4},{8,11},{9,10},{10,... | collective-permute-start | bytes 98312 | tf_op jit(solution)/shard_map/ppermute | solution.py:185
  44.8 5.8 %collective-permute-start.8 = (bf16[8,2048]{1,0:T(8,128)(2,1)S(1)}, bf16[8,2048]{1,0:T(8,128)(2,1)S(1)}, u32[]{:S(2)}, u32[]{:S(2)}) collective-permute-start(bf16[8,2048]{1,0:T(8,128)(2,1)S(1)} %shard_map.139.refs_0_.stream_ref), channel_id=1, source_target_pairs={{0,3},{1,2},{2,1},{3,0},{4,7},{5,6},{6,5},{7,4},{8,11},{9,10},{10,... | collective-permute-start | bytes 98312 | tf_op jit(solution)/shard_map/ppermute | solution.py:185
  48.0 4.8 %collective-permute-start.7 = (bf16[8,2048]{1,0:T(8,128)(2,1)S(1)}, bf16[8,2048]{1,0:T(8,128)(2,1)S(1)}, u32[]{:S(2)}, u32[]{:S(2)}) collective-permute-start(bf16[8,2048]{1,0:T(8,128)(2,1)S(1)} %shard_map.139.refs_0_.stream_ref), channel_id=1, source_target_pairs={{0,2},{1,3},{2,0},{3,1},{4,6},{5,7},{6,4},{7,5},{8,10},{9,11},{10,... | collective-permute-start | bytes 98312 | tf_op jit(solution)/shard_map/ppermute | solution.py:185
  48.0 4.8 %collective-permute-start.6 = (bf16[8,2048]{1,0:T(8,128)(2,1)S(1)}, bf16[8,2048]{1,0:T(8,128)(2,1)S(1)}, u32[]{:S(2)}, u32[]{:S(2)}) collective-permute-start(bf16[8,2048]{1,0:T(8,128)(2,1)S(1)} %shard_map.139.refs_0_.stream_ref), channel_id=1, source_target_pairs={{0,1},{1,0},{2,3},{3,2},{4,5},{5,4},{6,7},{7,6},{8,9},{9,8},{10,11... | collective-permute-start | bytes 98312 | tf_op jit(solution)/shard_map/ppermute | solution.py:185
  55.4 8.3 %collective-permute-start.9 = (bf16[32,1920]{1,0:T(8,128)(2,1)S(1)}, bf16[32,1920]{1,0:T(8,128)(2,1)S(1)}, u32[]{:S(2)}, u32[]{:S(2)}) collective-permute-start(bf16[32,1920]{1,0:T(8,128)(2,1)S(1)} %get-tuple-element.27), channel_id=1, source_target_pairs={{0,4},{4,0},{8,12},{12,8},{1,5},{5,1},{9,13},{13,9},{2,6},{6,2},{1... | collective-permute-start | bytes 368648 | tf_op jit(solution)/shard_map/ppermute | solution.py:185
  55.4 5.2 %copy-start.9 = (bf16[2048,3584]{1,0:T(8,128)(2,1)S(1)}, bf16[2048,3584]{1,0:T(8,128)(2,1)}, u32[]{:S(2)}) copy-start(bf16[2048,3584]{1,0:T(8,128)(2,1)} %w_ref.4) | copy-start | bytes 44040196
  60.6 12.6 %copy-start.1 = (bf16[3584,2048]{1,0:T(8,128)(2,1)S(1)}, bf16[3584,2048]{1,0:T(8,128)(2,1)}, u32[]{:S(2)}) copy-start(bf16[3584,2048]{1,0:T(8,128)(2,1)} %w_ref.5) | copy-start | bytes 44040196
  63.2 1.5 %collective-permute-start.11 = (bf16[32,1792]{1,0:T(8,128)(2,1)S(1)}, bf16[32,1792]{1,0:T(8,128)(2,1)S(1)}, u32[]{:S(2)}, u32[]{:S(2)}) collective-permute-start(bf16[32,1792]{1,0:T(8,128)(2,1)S(1)} %get-tuple-element.30), channel_id=1, source_target_pairs={{0,4},{4,0},{8,12},{12,8},{1,5},{5,1},{9,13},{13,9},{2,6},{6,2},{1... | collective-permute-start | bytes 344072 | tf_op jit(solution)/shard_map/ppermute | solution.py:185
  63.8 7.8 %collective-permute-start.10 = (bf16[32,1920]{1,0:T(8,128)(2,1)S(1)}, bf16[32,1920]{1,0:T(8,128)(2,1)S(1)}, u32[]{:S(2)}, u32[]{:S(2)}) collective-permute-start(bf16[32,1920]{1,0:T(8,128)(2,1)S(1)} %shard_map.141.gate_ref), channel_id=1, source_target_pairs={{0,8},{4,12},{8,0},{12,4},{1,9},{5,13},{9,1},{13,5},{2,10},{6,14},... | collective-permute-start | bytes 368648 | tf_op jit(solution)/shard_map/ppermute | solution.py:185
  64.7 6.9 %collective-permute-start.12 = (bf16[32,1792]{1,0:T(8,128)(2,1)S(1)}, bf16[32,1792]{1,0:T(8,128)(2,1)S(1)}, u32[]{:S(2)}, u32[]{:S(2)}) collective-permute-start(bf16[32,1792]{1,0:T(8,128)(2,1)S(1)} %shard_map.143.up_ref), channel_id=1, source_target_pairs={{0,8},{4,12},{8,0},{12,4},{1,9},{5,13},{9,1},{13,5},{2,10},{6,14},... | collective-permute-start | bytes 344072 | tf_op jit(solution)/shard_map/ppermute | solution.py:185
  71.8 1.4 %collective-permute-start.13 = (bf16[32,1792]{1,0:T(8,128)(2,1)S(1)}, bf16[32,1792]{1,0:T(8,128)(2,1)S(1)}, u32[]{:S(2)}, u32[]{:S(2)}) collective-permute-start(bf16[32,1792]{1,0:T(8,128)(2,1)S(1)} %shard_map.144.own_ref), channel_id=1, source_target_pairs={{0,4},{4,0},{8,12},{12,8},{1,5},{5,1},{9,13},{13,9},{2,6},{6,2},{1... | collective-permute-start | bytes 344072 | tf_op jit(solution)/shard_map/ppermute | solution.py:185
  75.7 4.4 %collective-permute-start.14 = (bf16[8,2048]{1,0:T(8,128)(2,1)S(1)}, bf16[8,2048]{1,0:T(8,128)(2,1)S(1)}, u32[]{:S(2)}, u32[]{:S(2)}) collective-permute-start(bf16[8,2048]{1,0:T(8,128)(2,1)S(1)} %get-tuple-element.32), channel_id=1, source_target_pairs={{0,1},{1,0},{2,3},{3,2},{4,5},{5,4},{6,7},{7,6},{8,9},{9,8},{10,11... | collective-permute-start | bytes 98312 | tf_op jit(solution)/shard_map/ppermute | solution.py:185
  76.2 5.1 %collective-permute-start.15 = (bf16[8,2048]{1,0:T(8,128)(2,1)S(1)}, bf16[8,2048]{1,0:T(8,128)(2,1)S(1)}, u32[]{:S(2)}, u32[]{:S(2)}) collective-permute-start(bf16[8,2048]{1,0:T(8,128)(2,1)S(1)} %get-tuple-element.33), channel_id=1, source_target_pairs={{0,2},{1,3},{2,0},{3,1},{4,6},{5,7},{6,4},{7,5},{8,10},{9,11},{10,... | collective-permute-start | bytes 98312 | tf_op jit(solution)/shard_map/ppermute | solution.py:185
  77.9 5.7 %collective-permute-start.16 = (bf16[8,2048]{1,0:T(8,128)(2,1)S(1)}, bf16[8,2048]{1,0:T(8,128)(2,1)S(1)}, u32[]{:S(2)}, u32[]{:S(2)}) collective-permute-start(bf16[8,2048]{1,0:T(8,128)(2,1)S(1)} %get-tuple-element.34), channel_id=1, source_target_pairs={{0,3},{1,2},{2,1},{3,0},{4,7},{5,6},{6,5},{7,4},{8,11},{9,10},{10,... | collective-permute-start | bytes 98312 | tf_op jit(solution)/shard_map/ppermute | solution.py:185
  (1 other events, 0.7 us)

commit v2 on v1

--- a/solution.py
+++ b/solution.py
@@ -155,28 +155,19 @@
 
 LANES = 128
 MIB = 2**20
-COVER = 100
+COVER = (100, 100, 100, 100, 1, 1, 1, 1, 1, 1)
 CHUNK = 512
 
 
 def exchange_fits(residual, w_query, w_key, w_gate):
     tp_count, role_count = lax.axis_size("tp"), lax.axis_size("role")
     return (
-        tp_count in (2, 4)
-        and role_count in (2, 4)
+        tp_count == KV_HEADS
+        and role_count == 4
         and residual.shape[0] % 8 == 0
-        and w_query.shape[1] % HEAD_DIM == 0
-        and w_key.shape[1] % HEAD_DIM == 0
+        and w_query.shape[1] == GROUP * LANES
+        and w_key.shape[1] == LANES
         and w_gate.shape[1] % (2 * LANES) == 0
-    )
-
-
-def turn(vectors, cosine, sine):
-    halfway = vectors.shape[-1] // 2
-    cosine, sine = cosine[:, None, :], sine[:, None, :]
-    leading, trailing = vectors[..., :halfway], vectors[..., halfway:]
-    return jnp.concatenate(
-        [leading * cosine - trailing * sine, trailing * cosine + leading * sine], axis=-1
     )
 
 
@@ -215,18 +206,20 @@
 
 
 def angle_kernel(lengths_ref, cosine_ref, sine_ref):
-    count, halfway = cosine_ref.shape
-    step = lax.broadcasted_iota(jnp.int32, (1, halfway), 1).astype(jnp.float32)
-    frequency = jnp.exp(step * (-2.0 / HEAD_DIM * math.log(rope_base)))
+    count, width = cosine_ref.shape
+    lane = lax.broadcasted_iota(jnp.int32, (1, width), 1)
+    step = lax.rem(lane, width // 2).astype(jnp.float32)
+    frequency = jnp.exp(step * (-2.0 / width * math.log(rope_base)))
     angles = jnp.concatenate(
         [lengths_ref[i].astype(jnp.float32) * frequency for i in range(count)], axis=0
     )
     cosine_ref[...] = jnp.cos(angles)
-    sine_ref[...] = jnp.sin(angles)
-
-
-def project_kernel(*refs):
-    *block_refs, gain_ref, wq_ref, wk_ref, wv_ref, out_ref, rows_ref = refs
+    sine = jnp.sin(angles)
+    sine_ref[...] = jnp.where(lane < width // 2, -sine, sine)
+
+
+def project_kernel(_, *refs):
+    *block_refs, gain_ref, wq_ref, wk_ref, wv_ref, out_ref, rows_ref, sums_ref, packed_ref = refs
     place = lax.axis_index("tp")
     own = block_refs[0].shape[0]
     for k, block_ref in enumerate(block_refs):
@@ -235,19 +228,104 @@
     rows = rows_ref[...]
     squares = jnp.sum(rows * rows, axis=1, keepdims=True)
     scaled = (rows * gain_ref[...]).astype(jnp.bfloat16)
-    nq, nk = wq_ref.shape[1], wk_ref.shape[1]
-    for start, w_ref in ((0, wq_ref), (nq, wk_ref), (nq + nk, wv_ref)):
-        out_ref[:, start : start + w_ref.shape[1]] = jnp.dot(
-            scaled, w_ref[...], preferred_element_type=jnp.float32
-        ).astype(jnp.bfloat16)
-    out_ref[:, nq + 2 * nk :] = split_three(squares)
-
-
-def output_kernel(attended_ref, w_ref, *refs):
-    *out_refs, rows_ref = refs
+    count = rows.shape[0]
+    groups = 0
+    for w_ref in (wq_ref, wk_ref, wv_ref):
+        product = jnp.dot(scaled, w_ref[...], preferred_element_type=jnp.float32)
+        for at in range(0, w_ref.shape[1], LANES):
+            sums_ref[groups * count : (groups + 1) * count, :] = product[:, at : at + LANES]
+            groups += 1
+    sums_ref[groups * count :, :] = split_three(squares).astype(jnp.float32)
+    groups += 1
+    devices, depth, _ = out_ref.shape
+    each = count // devices
+    queries = wq_ref.shape[1] // LANES
+    packed_ref[...] = jnp.zeros_like(packed_ref)
+    for n in range(each):
+        for g in range(groups):
+            row = packed_row(n, g, each, queries, groups)
+            packed_ref[pl.ds(row, devices, stride=depth), :] = sums_ref[
+                pl.ds(g * count + n, devices, stride=each), :
+            ]
+    out_ref[...] = packed_ref[...].reshape(out_ref.shape).astype(jnp.bfloat16)
+
+
+def packed_row(n, g, each, queries, groups):
+    if g < queries:
+        return n * queries + g
+    return each * queries + n * (groups - queries) + g - queries
+
+
+def attend_kernel(
+    lengths_ref, got_ref, cosine_ref, sine_ref, keys_ref, values_ref, out_ref
+):
+    tp_count = KV_HEADS
+    devices, depth, width = got_ref.shape
+    each, window, _ = keys_ref.shape
+    groups = GROUP + 3
+    total = jnp.sum(
+        got_ref[...].astype(jnp.float32).reshape(devices // tp_count, tp_count, depth, width),
+        axis=0,
+    )
+    factor = HEAD_DIM ** (-0.5)
+    scores, own_scores, own_values = [], [], []
+    for n in range(each):
+        cosine, sine = cosine_ref[n : n + 1, :], sine_ref[n : n + 1, :]
+        tail = packed_row(n, GROUP, each, GROUP, groups)
+        squares = jnp.sum(total[0, tail + 2 : tail + 3, :], axis=1, keepdims=True)
+        inverse = lax.rsqrt(squares / D + epsilon)
+        usable = lax.broadcasted_iota(jnp.int32, (GROUP, window), 1) < lengths_ref[n]
+        for h in range(tp_count):
+            query = total[h, n * GROUP : (n + 1) * GROUP, :] * inverse
+            key = total[h, tail : tail + 1, :] * inverse
+            query = query * cosine + pltpu.roll(query, width // 2, 1) * sine
+            key = key * cosine + pltpu.roll(key, width // 2, 1) * sine
+            query = query.astype(jnp.bfloat16)
+            key = key.astype(jnp.bfloat16).astype(jnp.float32)
+            score = lax.dot_general(
+                query,
+                keys_ref[n, :, h * width : (h + 1) * width],
+                (((1,), (1,)), ((), ())),
+                preferred_element_type=jnp.float32,
+            )
+            scores.append(jnp.where(usable, score * factor, -jnp.inf))
+            own_scores.append(
+                jnp.sum(query.astype(jnp.float32) * key, axis=1, keepdims=True) * factor
+            )
+            value = (total[h, tail + 1 : tail + 2, :] * inverse).astype(jnp.bfloat16)
+            own_values.append(value.astype(jnp.float32))
+    scores, own_scores = jnp.concatenate(scores, axis=0), jnp.concatenate(own_scores, axis=0)
+    highest = jnp.maximum(jnp.max(scores, axis=1, keepdims=True), own_scores)
+    weights, own_weights = jnp.exp(scores - highest), jnp.exp(own_scores - highest)
+    denominator = jnp.sum(weights, axis=1, keepdims=True) + own_weights
+    chances = (weights / denominator).astype(jnp.bfloat16)
+    own_chances = (own_weights / denominator).astype(jnp.bfloat16).astype(jnp.float32)
+    for n in range(each):
+        for h in range(tp_count):
+            at = (n * tp_count + h) * GROUP
+            attended = jnp.dot(
+                chances[at : at + GROUP],
+                values_ref[n, :, h * width : (h + 1) * width],
+                preferred_element_type=jnp.float32,
+            )
+            attended = attended + own_chances[at : at + GROUP] * own_values[n * tp_count + h]
+            for r in range(devices // tp_count):
+                out_ref[r * tp_count + h, n * GROUP : (n + 1) * GROUP, :] = attended.astype(
+                    jnp.bfloat16
+                )
+
+
+def output_kernel(heads_ref, w_ref, *refs):
+    *out_refs, heads_wide_ref, rows_ref = refs
     place = lax.axis_index("tp")
     own = out_refs[0].shape[0]
-    rows_ref[...] = jnp.dot(attended_ref[...], w_ref[...], preferred_element_type=jnp.float32)
+    groups = w_ref.shape[0] // LANES
+    heads_wide_ref[...] = heads_ref[...].astype(jnp.float32).reshape(heads_wide_ref.shape)
+    attended = jnp.concatenate(
+        [heads_wide_ref[pl.ds(g, rows_ref.shape[0], stride=groups), :] for g in range(groups)],
+        axis=1,
+    ).astype(jnp.bfloat16)
+    rows_ref[...] = jnp.dot(attended, w_ref[...], preferred_element_type=jnp.float32)
     for k, out_ref in enumerate(out_refs):
         start = pl.multiple_of((place ^ k) * own, own)
         out_ref[...] = rows_ref[pl.ds(start, own), :].astype(jnp.bfloat16)
@@ -270,41 +348,46 @@
     )
 
 
-def gate_kernel(*refs):
-    *block_refs, gain_ref, w_ref, scaled_ref, keep_ref, send_ref = refs
+def gate_send_kernel(*refs):
+    *block_refs, gain_ref, w_ref, scaled_ref, tail_ref, send_ref = refs
     rows = jnp.concatenate([ref[...].astype(jnp.float32) for ref in block_refs], axis=0)
     squares = jnp.sum(rows * rows, axis=1, keepdims=True)
     scaled = (rows * gain_ref[...]).astype(jnp.bfloat16)
     scaled_ref[...] = scaled
+    half = lax.rem(lax.axis_index("role"), 2)
+    one_half(scaled, w_ref, send_ref, 1 - half)
+    tail = split_three(squares)
+    send_ref[:, w_ref.shape[1] // 2 :] = tail
+    tail_ref[...] = tail.astype(jnp.float32)
+
+
+def send_kernel(scaled_ref, w_ref, send_ref):
+    half = lax.rem(lax.axis_index("role"), 2)
+    one_half(scaled_ref[...], w_ref, send_ref, 1 - half)
+
+
+def keep_kernel(scaled_ref, w_ref, keep_ref):
+    half = lax.rem(lax.axis_index("role"), 2)
+    one_half(scaled_ref[...], w_ref, keep_ref, half)
+
+
+def one_half(scaled, w_ref, out_ref, side):
     width = w_ref.shape[1] // 2
-    halves(scaled, w_ref, keep_ref, send_ref, width)
-    tail = split_three(squares)
-    send_ref[:, width:] = tail
-    keep_ref[:, width:] = tail.astype(keep_ref.dtype)
-
-
-def up_kernel(scaled_ref, w_ref, keep_ref, send_ref):
-    halves(scaled_ref[...], w_ref, keep_ref, send_ref, w_ref.shape[1] // 2)
-
-
-def halves(scaled, w_ref, keep_ref, send_ref, width):
-    half = lax.rem(lax.axis_index("role"), 2)
-    for side, out_ref in ((1 - half, send_ref), (half, keep_ref)):
-        for at in range(0, width, CHUNK):
-            size = min(CHUNK, width - at)
-            start = pl.multiple_of(side * width + at, LANES)
-            out_ref[:, at : at + size] = jnp.dot(
-                scaled, w_ref[:, pl.ds(start, size)], preferred_element_type=jnp.float32
-            ).astype(out_ref.dtype)
-
-
-def pair_gate_kernel(keep_ref, got_ref, out_ref):
-    wide = out_ref.shape[1] - LANES
-    out_ref[:, :wide] = (
-        keep_ref[:, :wide] + got_ref[:, :wide].astype(jnp.float32)
-    ).astype(jnp.bfloat16)
+    for at in range(0, width, CHUNK):
+        size = min(CHUNK, width - at)
+        start = pl.multiple_of(side * width + at, LANES)
+        out_ref[:, at : at + size] = jnp.dot(
+            scaled, w_ref[:, pl.ds(start, size)], preferred_element_type=jnp.float32
+        ).astype(out_ref.dtype)
+
+
+def pair_gate_kernel(keep_ref, tail_ref, got_ref, out_ref):
+    wide = keep_ref.shape[1]
+    out_ref[:, :wide] = (keep_ref[...] + got_ref[:, :wide].astype(jnp.float32)).astype(
+        jnp.bfloat16
+    )
     squares = jnp.sum(
-        keep_ref[:, wide:] + got_ref[:, wide:].astype(jnp.float32), axis=1, keepdims=True
+        tail_ref[...] + got_ref[:, wide:].astype(jnp.float32), axis=1, keepdims=True
     )
     out_ref[:, wide:] = split_three(squares)
 
@@ -327,16 +410,25 @@
     out_ref[...] = (gate / (1.0 + jnp.exp(-gate)) * up).astype(jnp.bfloat16)
 
 
-def down_kernel(own_ref, other_ref, w_ref, *out_refs):
+def down_own_kernel(own_ref, w_ref, rows_ref):
     half = lax.rem(lax.axis_index("role"), 2)
     width = own_ref.shape[1]
     mine = pl.ds(pl.multiple_of(half * width, LANES), width)
+    for at in range(0, w_ref.shape[1], CHUNK):
+        part = slice(at, min(at + CHUNK, w_ref.shape[1]))
+        rows_ref[:, part] = jnp.dot(
+            own_ref[...], w_ref[mine, part], preferred_element_type=jnp.float32
+        )
+
+
+def down_kernel(other_ref, w_ref, rows_ref, *out_refs):
+    half = lax.rem(lax.axis_index("role"), 2)
+    width = other_ref.shape[1]
     theirs = pl.ds(pl.multiple_of((1 - half) * width, LANES), width)
     own = out_refs[0].shape[0]
     for at in range(0, w_ref.shape[1], CHUNK):
         part = slice(at, min(at + CHUNK, w_ref.shape[1]))
-        rows = jnp.dot(own_ref[...], w_ref[mine, part], preferred_element_type=jnp.float32)
-        rows = rows + jnp.dot(
+        rows = rows_ref[:, part] + jnp.dot(
             other_ref[...], w_ref[theirs, part], preferred_element_type=jnp.float32
         )
         for k, out_ref in enumerate(out_refs):
@@ -383,44 +475,40 @@
     each = rows // devices
     block = jax.ShapeDtypeStruct((own, features), jnp.bfloat16)
 
-    table = jax.ShapeDtypeStruct((each, HEAD_DIM // 2), jnp.float32)
-    cosine, sine = call(angle_kernel, [table] * 2, [lengths], smem=1, cost=COVER)
+    table = jax.ShapeDtypeStruct((each, HEAD_DIM), jnp.float32)
+    cosine, sine = call(angle_kernel, [table] * 2, [lengths], smem=1, cost=COVER[0])
     blocks = [residual] + [swap(residual, "tp", k) for k in range(1, tp_count)]
-    query_cols, kv_cols = w_query.shape[1], w_key.shape[1]
-    payload = query_cols + 2 * kv_cols + LANES
+    payload = w_query.shape[1] + 2 * w_key.shape[1] + LANES
+    depth = -(-each * payload // (LANES * 8)) * 8
     (sums,) = call(
         project_kernel,
-        [jax.ShapeDtypeStruct((rows, payload), jnp.bfloat16)],
-        [*blocks, attn_gain[None, :], in_vmem(w_query), in_vmem(w_key), in_vmem(w_value)],
-        scratch=[pltpu.VMEM((rows, features), jnp.float32)],
-    )
-    parts = lax.all_to_all(sums.reshape(devices, each, payload), ("role", "tp"), 0, 0)
-    parts = parts.reshape(role_count, tp_count, each, payload).astype(jnp.float32)
-    gathered = jnp.sum(parts, axis=0).transpose(1, 0, 2)
-    squares = jnp.sum(gathered[:, :1, query_cols + 2 * kv_cols :], axis=2, keepdims=True)
-    gathered = gathered[:, :, : query_cols + 2 * kv_cols] * lax.rsqrt(squares / D + epsilon)
-    queries = gathered[:, :, :query_cols].reshape(each, HEADS, HEAD_DIM)
-    new_key = gathered[:, :, query_cols : query_cols + kv_cols].reshape(each, KV_HEADS, HEAD_DIM)
-    new_value = (
-        gathered[:, :, query_cols + kv_cols :]
-        .reshape(each, KV_HEADS, HEAD_DIM)
-        .astype(jnp.bfloat16)
-    )
-    queries = turn(queries, cosine, sine).astype(jnp.bfloat16)
-    new_key = turn(new_key, cosine, sine).astype(jnp.bfloat16)
-    attended = attend(queries, new_key, new_value, cache_keys, cache_values, lengths)
-    by_block = attended.reshape(each, tp_count, query_cols).transpose(1, 0, 2)
-    sent = jnp.broadcast_to(by_block[None], (role_count, tp_count, each, query_cols))
-    heads = lax.all_to_all(
-        sent.reshape(devices, each, query_cols), ("role", "tp"), 0, 0
-    ).reshape(rows, query_cols)
-
+        [jax.ShapeDtypeStruct((devices, depth, LANES), jnp.bfloat16)],
+        [cosine, *blocks, attn_gain[None, :], in_vmem(w_query), in_vmem(w_key), in_vmem(w_value)],
+        scratch=[
+            pltpu.VMEM((rows, features), jnp.float32),
+            pltpu.VMEM((rows * payload // LANES, LANES), jnp.float32),
+            pltpu.VMEM((devices * depth, LANES), jnp.float32),
+        ],
+        cost=COVER[1],
+    )
+    parts = lax.all_to_all(sums, ("role", "tp"), 0, 0)
+    (heads,) = call(
+        attend_kernel,
+        [jax.ShapeDtypeStruct((devices, each * GROUP, LANES), jnp.bfloat16)],
+        [lengths, parts, cosine, sine, in_vmem(cache_keys), in_vmem(cache_values)],
+        smem=1,
+        cost=COVER[2],
+    )
+    heads = lax.all_to_all(heads, ("role", "tp"), 0, 0)
     terms = call(
         output_kernel,
         [block] * tp_count,
         [heads, in_vmem(w_output)],
-        cost=COVER,
-        scratch=[pltpu.VMEM((rows, features), jnp.float32)],
+        scratch=[
+            pltpu.VMEM((rows * GROUP, LANES), jnp.float32),
+            pltpu.VMEM((rows, features), jnp.float32),
+        ],
+        cost=COVER[3],
     )
     terms = [terms[0]] + [swap(terms[k], "tp", k) for k in range(1, tp_count)]
     (middle,) = call(add_kernel, [block], [served, residual, *terms], smem=1)
@@ -428,43 +516,41 @@
     blocks = [middle] + [swap(middle, "tp", k) for k in range(1, tp_count)]
     width = w_gate.shape[1] // 2
     wide = width + LANES
-    scaled, gate, gate_send = call(
-        gate_kernel,
+    half_f32 = jax.ShapeDtypeStruct((rows, width), jnp.float32)
+    half_bf16 = jax.ShapeDtypeStruct((rows, width), jnp.bfloat16)
+    wide_bf16 = jax.ShapeDtypeStruct((rows, wide), jnp.bfloat16)
+    w_gate, w_up, w_down = in_vmem(w_gate), in_vmem(w_up), in_vmem(w_down)
+    scaled, tail, gate_send = call(
+        gate_send_kernel,
         [
             jax.ShapeDtypeStruct((rows, features), jnp.bfloat16),
-            jax.ShapeDtypeStruct((rows, wide), jnp.float32),
-            jax.ShapeDtypeStruct((rows, wide), jnp.bfloat16),
+            jax.ShapeDtypeStruct((rows, LANES), jnp.float32),
+            wide_bf16,
         ],
-        [*blocks, ffn_gain[None, :], in_vmem(w_gate)],
-        cost=COVER,
+        [*blocks, ffn_gain[None, :], w_gate],
+        cost=COVER[4],
     )
     gate_got = swap(gate_send, "role", 1)
-    up, up_send = call(
-        up_kernel,
-        [
-            jax.ShapeDtypeStruct((rows, width), jnp.float32),
-            jax.ShapeDtypeStruct((rows, width), jnp.bfloat16),
-        ],
-        [scaled, in_vmem(w_up)],
-        cost=COVER,
-    )
+    (gate,) = call(keep_kernel, [half_f32], [scaled, w_gate], cost=COVER[5])
+    (gate,) = call(pair_gate_kernel, [wide_bf16], [gate, tail, gate_got])
+    (up_send,) = call(send_kernel, [half_bf16], [scaled, w_up], cost=COVER[6])
     up_got = swap(up_send, "role", 1)
-    if role_count > 2:
-        (gate,) = call(
-            pair_gate_kernel, [jax.ShapeDtypeStruct((rows, wide), jnp.bfloat16)], [gate, gate_got]
-        )
-        gate_got = swap(gate, "role", 2)
-        (up,) = call(
-            pair_up_kernel, [jax.ShapeDtypeStruct((rows, width), jnp.bfloat16)], [up, up_got]
-        )
-        up_got = swap(up, "role", 2)
+    (up,) = call(keep_kernel, [half_f32], [scaled, w_up], cost=COVER[7])
+    (up,) = call(pair_up_kernel, [half_bf16], [up, up_got])
+    gate_got, up_got = swap(gate, "role", 2), swap(up, "role", 2)
     (hidden,) = call(
         hidden_kernel,
-        [jax.ShapeDtypeStruct((rows, width), jnp.bfloat16)],
+        [half_bf16],
         [gate, gate_got, up, up_got],
     )
     other = swap(hidden, "role", 1)
-    terms = call(down_kernel, [block] * tp_count, [hidden, other, in_vmem(w_down)])
+    (down,) = call(
+        down_own_kernel,
+        [jax.ShapeDtypeStruct((rows, features), jnp.float32)],
+        [hidden, w_down],
+        cost=COVER[8],
+    )
+    terms = call(down_kernel, [block] * tp_count, [other, w_down, down], cost=COVER[9])
     terms = [terms[0]] + [swap(terms[k], "tp", k) for k in range(1, tp_count)]
     return call(add_kernel, [block], [served, middle, *terms], smem=1)[0]
 

time: 85.1 us -> 75.6 us (0.89)
  blocking collectives: 9.22 us -> 19.2 us
  local copies, waits for them, and re-layouts: 8.87 us -> 0.76 us
  waiting for transfers between devices: 26.5 us -> 19.1 us
  starting transfers between devices: 26.1 us -> 21.8 us
  Pallas kernels: 12.3 us -> 14.1 us
    all_to_all x1 -> x2, blocking collectives: 9.22 us -> 19.2 us  [the longest x1 9.65 us: local_exchange(): parts = lax.all_to_all(sums, ('role', 'tp'), 0, 0)]
    unnamed x30 -> x42, local copies, waits for them, and re-layouts: 8.05 us -> 0.76 us
    all_to_all x1 -> x0, waiting for transfers between devices: 6.8 us -> none  [local_exchange(): lax.all_to_all(sums.reshape(devices, each, payload), ('role', 'tp'), 0, 0)]
    all_to_all x1 -> x0, starting transfers between devices: 4.32 us -> none  [local_exchange(): lax.all_to_all(sums.reshape(devices, each, payload), ('role', 'tp'), 0, 0)]
    pallas_call x11 -> x15, Pallas kernels: 12.3 us -> 14.1 us  [call(): pl.pallas_call(kernel, out_shape=outs, in_specs=specs, out_specs=[pl.Bloc...]
  transfers between devices with their start and end apart: 18 -> 17, of which waited for: 12 -> 9; matrix products, arithmetic and copies ran while one was open for 0% -> 0% of each run, Pallas kernels for 4% -> 8%
where the time goes in v2:
time: 75.6 us; the launch traced here: 75.3 us
  starting transfers between devices  21.8 us (29%)
  blocking collectives  19.2 us (25%)
  waiting for transfers between devices  19.1 us (25%)
  Pallas kernels  14.1 us (19%)
  local copies, waits for them, and re-layouts  0.76 us (1%)
    ppermute x17, starting transfers between devices, swap(): return lax.ppermute(value, axis, [(i, i ^ distance) for i in range(count)])  21.8 us
    ppermute x17, waiting for transfers between devices, swap(): return lax.ppermute(value, axis, [(i, i ^ distance) for i in range(count)])  19.1 us
    pallas_call x15, Pallas kernels, call(): pl.pallas_call(kernel, out_shape=outs, in_specs=specs, out_specs=[pl.Bloc...  14.1 us
    all_to_all x1, blocking collectives, local_exchange(): parts = lax.all_to_all(sums, ('role', 'tp'), 0, 0)  9.65 us
    all_to_all x1, blocking collectives, local_exchange(): heads = lax.all_to_all(heads, ('role', 'tp'), 0, 0)  9.56 us
  transfers between devices with their start and end apart: 17, of which 9 were waited for; matrix products, arithmetic and copies ran while one was open for 0% of the time, Pallas kernels for 8%

profile of v2, /device:TPU:0, one launch (start us, length us, event | category | flops | bytes accessed | tf_op | source)
XLA Modules:
  0.0 75.3 jit_solution(14471158871897664944)
XLA Ops:
  0.0 3.1 %collective-permute-start = (bf16[8,2048]{1,0:T(8,128)(2,1)}, bf16[8,2048]{1,0:T(8,128)(2,1)S(1)}, u32[]{:S(2)}, u32[]{:S(2)}) collective-permute-start(bf16[8,2048]{1,0:T(8,128)(2,1)} %stream_ref.1), channel_id=1, source_target_pairs={{0,1},{1,0},{2,3},{3,2},{4,5},{5,4},{6,7},{7,6},{8,9},{9,8},{10,11... | collective-permute-start | bytes 98312 | tf_op jit(solution)/shard_map/ppermute | solution.py:176
  3.1 2.6 %collective-permute-start.1 = (bf16[8,2048]{1,0:T(8,128)(2,1)}, bf16[8,2048]{1,0:T(8,128)(2,1)S(1)}, u32[]{:S(2)}, u32[]{:S(2)}) collective-permute-start(bf16[8,2048]{1,0:T(8,128)(2,1)} %stream_ref.1), channel_id=1, source_target_pairs={{0,2},{1,3},{2,0},{3,1},{4,6},{5,7},{6,4},{7,5},{8,10},{9,11},{10,... | collective-permute-start | bytes 98312 | tf_op jit(solution)/shard_map/ppermute | solution.py:176
  5.7 0.7 copy-done.11
  7.0 1.8 %collective-permute-done.1.refs_2_ = bf16[8,2048]{1,0:T(8,128)(2,1)S(1)} collective-permute-done((bf16[8,2048]{1,0:T(8,128)(2,1)}, bf16[8,2048]{1,0:T(8,128)(2,1)S(1)}, u32[]{:S(2)}, u32[]{:S(2)}) %collective-permute-start.1) | collective-permute-done | bytes 32800 | tf_op jit(solution)/shard_map/ppermute | solution.py:176
  8.8 2.9 %collective-permute-done.2.refs_3_ = bf16[8,2048]{1,0:T(8,128)(2,1)S(1)} collective-permute-done((bf16[8,2048]{1,0:T(8,128)(2,1)}, bf16[8,2048]{1,0:T(8,128)(2,1)S(1)}, u32[]{:S(2)}, u32[]{:S(2)}) %collective-permute-start.2) | collective-permute-done | bytes 32800 | tf_op jit(solution)/shard_map/ppermute | solution.py:176
  11.7 1.0 %shard_map.137 = bf16[16,24,128]{2,1,0:T(8,128)(2,1)S(1)} custom-call(f32[2,128]{1,0:T(2,128)S(1)} %get-tuple-element.18._.cosine_ref, bf16[8,2048]{1,0:T(8,128)(2,1)S(1)} %copy-done.1, bf16[8,2048]{1,0:T(8,128)(2,1)S(1)} %collective-permute-done.refs_1_, bf16[8,2048]{1,0:T(8,128)(2,1)S(1)} %collective-permute-done.1.refs_2_, ...), custom_call_target="tpu_custom_call" | custom-call | flops 99999997952 | bytes 1048576 | tf_op jit(solution)/shard_map/pallas_call | solution.py:186
  12.8 9.7 %all_to_all.10.got_ref = bf16[16,24,128]{2,1,0:T(8,128)(2,1)S(1)} all-to-all(bf16[16,24,128]{2,1,0:T(8,128)(2,1)S(1)} %shard_map.137), channel_id=1, replica_groups=mesh['groups'=2,'role'=4,'tp'=4] {'role','tp'}, dimensions={0} | all-to-all | bytes 196608 | tf_op jit(solution)/shard_map/all_to_all | solution.py:494
  22.4 1.4 %shard_map.138 = bf16[16,16,128]{2,1,0:T(8,128)(2,1)S(1)} custom-call(s32[2]{0:T(128)S(1)} %copy-done.12, bf16[16,24,128]{2,1,0:T(8,128)(2,1)S(1)} %all_to_all.10.got_ref, f32[2,128]{1,0:T(2,128)S(1)} %get-tuple-element.18._.cosine_ref, f32[2,128]{1,0:T(2,128)S(1)} %get-tuple-element.19.sine_ref, bf16[2,256,512]{2,1,0:T(8,128)(2,1)S(1)} %copy-done.8, ...), custom_call_target="tpu_custom_call" | custom-call | flops 99999997952 | bytes 1048576 | tf_op jit(solution)/shard_map/pallas_call | solution.py:186
  23.8 9.6 %all_to_all.11.heads_ref = bf16[16,16,128]{2,1,0:T(8,128)(2,1)S(1)} all-to-all(bf16[16,16,128]{2,1,0:T(8,128)(2,1)S(1)} %shard_map.138), channel_id=1, replica_groups=mesh['groups'=2,'role'=4,'tp'=4] {'role','tp'}, dimensions={0} | all-to-all | bytes 131072 | tf_op jit(solution)/shard_map/all_to_all | solution.py:502
  33.4 0.8 %shard_map.139 = (bf16[8,2048]{1,0:T(8,128)(2,1)S(1)}, bf16[8,2048]{1,0:T(8,128)(2,1)S(1)}, bf16[8,2048]{1,0:T(8,128)(2,1)S(1)}, bf16[8,2048]{1,0:T(8,128)(2,1)S(1)}) custom-call(bf16[16,16,128]{2,1,0:T(8,128)(2,1)S(1)} %all_to_all.11.heads_ref, bf16[1024,2048]{1,0:T(8,128)(2,1)S(1)} %copy-done.5), custom_call_target="tpu_custom_call" | custom-call | flops 99999997952 | bytes 1048576 | tf_op jit(solution)/shard_map/pallas_call | solution.py:186
  34.7 1.0 %collective-permute-start.4 = (bf16[8,2048]{1,0:T(8,128)(2,1)S(1)}, bf16[8,2048]{1,0:T(8,128)(2,1)S(1)}, u32[]{:S(2)}, u32[]{:S(2)}) collective-permute-start(bf16[8,2048]{1,0:T(8,128)(2,1)S(1)} %get-tuple-element.22), channel_id=1, source_target_pairs={{0,2},{1,3},{2,0},{3,1},{4,6},{5,7},{6,4},{7,5},{8,10},{9,11},{10,... | collective-permute-start | bytes 98312 | tf_op jit(solution)/shard_map/ppermute | solution.py:176
  35.7 3.1 %collective-permute-start.5 = (bf16[8,2048]{1,0:T(8,128)(2,1)S(1)}, bf16[8,2048]{1,0:T(8,128)(2,1)S(1)}, u32[]{:S(2)}, u32[]{:S(2)}) collective-permute-start(bf16[8,2048]{1,0:T(8,128)(2,1)S(1)} %get-tuple-element.23), channel_id=1, source_target_pairs={{0,3},{1,2},{2,1},{3,0},{4,7},{5,6},{6,5},{7,4},{8,11},{9,10},{10,... | collective-permute-start | bytes 98312 | tf_op jit(solution)/shard_map/ppermute | solution.py:176
  38.7 1.5 %collective-permute-done.4.refs_2_ = bf16[8,2048]{1,0:T(8,128)(2,1)S(1)} collective-permute-done((bf16[8,2048]{1,0:T(8,128)(2,1)S(1)}, bf16[8,2048]{1,0:T(8,128)(2,1)S(1)}, u32[]{:S(2)}, u32[]{:S(2)}) %collective-permute-start.4) | collective-permute-done | bytes 32800 | tf_op jit(solution)/shard_map/ppermute | solution.py:176
  40.2 1.2 %collective-permute-done.5.refs_3_ = bf16[8,2048]{1,0:T(8,128)(2,1)S(1)} collective-permute-done((bf16[8,2048]{1,0:T(8,128)(2,1)S(1)}, bf16[8,2048]{1,0:T(8,128)(2,1)S(1)}, u32[]{:S(2)}, u32[]{:S(2)}) %collective-permute-start.5) | collective-permute-done | bytes 32800 | tf_op jit(solution)/shard_map/ppermute | solution.py:176
  42.1 3.6 %collective-permute-start.7 = (bf16[8,2048]{1,0:T(8,128)(2,1)S(1)}, bf16[8,2048]{1,0:T(8,128)(2,1)S(1)}, u32[]{:S(2)}, u32[]{:S(2)}) collective-permute-start(bf16[8,2048]{1,0:T(8,128)(2,1)S(1)} %shard_map.140.refs_0_.stream_ref), channel_id=1, source_target_pairs={{0,2},{1,3},{2,0},{3,1},{4,6},{5,7},{6,4},{7,5},{8,10},{9,11},{10,... | collective-permute-start | bytes 98312 | tf_op jit(solution)/shard_map/ppermute | solution.py:176
  45.7 0.7 collective-permute-start.8
  46.4 1.1 %collective-permute-done.7.refs_2_ = bf16[8,2048]{1,0:T(8,128)(2,1)S(1)} collective-permute-done((bf16[8,2048]{1,0:T(8,128)(2,1)S(1)}, bf16[8,2048]{1,0:T(8,128)(2,1)S(1)}, u32[]{:S(2)}, u32[]{:S(2)}) %collective-permute-start.7) | collective-permute-done | bytes 32800 | tf_op jit(solution)/shard_map/ppermute | solution.py:176
  47.6 3.8 %collective-permute-done.8.refs_3_ = bf16[8,2048]{1,0:T(8,128)(2,1)S(1)} collective-permute-done((bf16[8,2048]{1,0:T(8,128)(2,1)S(1)}, bf16[8,2048]{1,0:T(8,128)(2,1)S(1)}, u32[]{:S(2)}, u32[]{:S(2)}) %collective-permute-start.8) | collective-permute-done | bytes 32800 | tf_op jit(solution)/shard_map/ppermute | solution.py:176
  51.4 1.4 %shard_map.141 = (bf16[32,2048]{1,0:T(8,128)(2,1)S(1)}, f32[32,128]{1,0:T(8,128)S(1)}, bf16[32,1920]{1,0:T(8,128)(2,1)S(1)}) custom-call(bf16[8,2048]{1,0:T(8,128)(2,1)S(1)} %shard_map.140.refs_0_.stream_ref, bf16[8,2048]{1,0:T(8,128)(2,1)S(1)} %collective-permute-done.6.refs_1_, bf16[8,2048]{1,0:T(8,128)(2,1)S(1)} %collective-permute-done.7.refs_2_, ...), custom_call_target="tpu_custom_call" | custom-call | flops 1000000000 | bytes 1048576 | tf_op jit(solution)/shard_map/pallas_call | solution.py:186
  52.9 1.4 %shard_map.145 = bf16[32,1792]{1,0:T(8,128)(2,1)S(1)} custom-call(bf16[32,2048]{1,0:T(8,128)(2,1)S(1)} %get-tuple-element.24.scaled_ref, bf16[2048,3584]{1,0:T(8,128)(2,1)S(1)} %bitcast.3), custom_call_target="tpu_custom_call" | custom-call | flops 1000000000 | bytes 1048576 | tf_op jit(solution)/shard_map/pallas_call | solution.py:186
  54.8 1.4 %shard_map.142.keep_ref = f32[32,1792]{1,0:T(8,128)S(1)} custom-call(bf16[32,2048]{1,0:T(8,128)(2,1)S(1)} %get-tuple-element.24.scaled_ref, bf16[2048,3584]{1,0:T(8,128)(2,1)S(1)} %copy-done), custom_call_target="tpu_custom_call" | custom-call | flops 1000000000 | bytes 1048576 | tf_op jit(solution)/shard_map/pallas_call | solution.py:186
  56.3 0.8 %collective-permute-start.10 = (bf16[32,1920]{1,0:T(8,128)(2,1)S(1)}, bf16[32,1920]{1,0:T(8,128)(2,1)S(1)}, u32[]{:S(2)}, u32[]{:S(2)}) collective-permute-start(bf16[32,1920]{1,0:T(8,128)(2,1)S(1)} %shard_map.143.gate_ref), channel_id=1, source_target_pairs={{0,8},{4,12},{8,0},{12,4},{1,9},{5,13},{9,1},{13,5},{2,10},{6,14},... | collective-permute-start | bytes 368648 | tf_op jit(solution)/shard_map/ppermute | solution.py:176
  57.1 1.4 %shard_map.144.keep_ref = f32[32,1792]{1,0:T(8,128)S(1)} custom-call(bf16[32,2048]{1,0:T(8,128)(2,1)S(1)} %get-tuple-element.24.scaled_ref, bf16[2048,3584]{1,0:T(8,128)(2,1)S(1)} %bitcast.3), custom_call_target="tpu_custom_call" | custom-call | flops 1000000000 | bytes 1048576 | tf_op jit(solution)/shard_map/pallas_call | solution.py:186
  58.5 1.4 %collective-permute-start.12 = (bf16[32,1792]{1,0:T(8,128)(2,1)S(1)}, bf16[32,1792]{1,0:T(8,128)(2,1)S(1)}, u32[]{:S(2)}, u32[]{:S(2)}) collective-permute-start(bf16[32,1792]{1,0:T(8,128)(2,1)S(1)} %shard_map.146.up_ref), channel_id=1, source_target_pairs={{0,8},{4,12},{8,0},{12,4},{1,9},{5,13},{9,1},{13,5},{2,10},{6,14},... | collective-permute-start | bytes 344072 | tf_op jit(solution)/shard_map/ppermute | solution.py:176
  59.8 4.2 %collective-permute-done.12.up_got_ref = bf16[32,1792]{1,0:T(8,128)(2,1)S(1)} collective-permute-done((bf16[32,1792]{1,0:T(8,128)(2,1)S(1)}, bf16[32,1792]{1,0:T(8,128)(2,1)S(1)}, u32[]{:S(2)}, u32[]{:S(2)}) %collective-permute-start.12) | collective-permute-done | bytes 114720 | tf_op jit(solution)/shard_map/ppermute | solution.py:176
  64.4 1.4 %shard_map.148.rows_ref = f32[32,2048]{1,0:T(8,128)S(1)} custom-call(bf16[32,1792]{1,0:T(8,128)(2,1)S(1)} %shard_map.147.own_ref, bf16[3584,2048]{1,0:T(8,128)(2,1)S(1)} %bitcast.5), custom_call_target="tpu_custom_call" | custom-call | flops 1000000000 | bytes 1048576 | tf_op jit(solution)/shard_map/pallas_call | solution.py:186
  65.7 1.4 %shard_map.149 = (bf16[8,2048]{1,0:T(8,128)(2,1)S(1)}, bf16[8,2048]{1,0:T(8,128)(2,1)S(1)}, bf16[8,2048]{1,0:T(8,128)(2,1)S(1)}, bf16[8,2048]{1,0:T(8,128)(2,1)S(1)}) custom-call(bf16[32,1792]{1,0:T(8,128)(2,1)S(1)} %collective-permute-done.13.other_ref, bf16[3584,2048]{1,0:T(8,128)(2,1)S(1)} %bitcast.5, f32[32,2048]{1,0:T(8,128)S(1)} %shard_map.148.rows_ref), custom_call_target="tpu_custom_call" | custom-call | flops 1000000000 | bytes 1048576 | tf_op jit(solution)/shard_map/pallas_call | solution.py:186
  67.1 1.3 %collective-permute-start.15 = (bf16[8,2048]{1,0:T(8,128)(2,1)S(1)}, bf16[8,2048]{1,0:T(8,128)(2,1)S(1)}, u32[]{:S(2)}, u32[]{:S(2)}) collective-permute-start(bf16[8,2048]{1,0:T(8,128)(2,1)S(1)} %get-tuple-element.29), channel_id=1, source_target_pairs={{0,2},{1,3},{2,0},{3,1},{4,6},{5,7},{6,4},{7,5},{8,10},{9,11},{10,... | collective-permute-start | bytes 98312 | tf_op jit(solution)/shard_map/ppermute | solution.py:176
  68.4 3.1 %collective-permute-start.16 = (bf16[8,2048]{1,0:T(8,128)(2,1)S(1)}, bf16[8,2048]{1,0:T(8,128)(2,1)S(1)}, u32[]{:S(2)}, u32[]{:S(2)}) collective-permute-start(bf16[8,2048]{1,0:T(8,128)(2,1)S(1)} %get-tuple-element.30), channel_id=1, source_target_pairs={{0,3},{1,2},{2,1},{3,0},{4,7},{5,6},{6,5},{7,4},{8,11},{9,10},{10,... | collective-permute-start | bytes 98312 | tf_op jit(solution)/shard_map/ppermute | solution.py:176
  71.5 0.7 collective-permute-done.15.refs_2_
  72.2 1.9 %collective-permute-done.16.refs_3_ = bf16[8,2048]{1,0:T(8,128)(2,1)S(1)} collective-permute-done((bf16[8,2048]{1,0:T(8,128)(2,1)S(1)}, bf16[8,2048]{1,0:T(8,128)(2,1)S(1)}, u32[]{:S(2)}, u32[]{:S(2)}) %collective-permute-start.16) | collective-permute-done | bytes 32800 | tf_op jit(solution)/shard_map/ppermute | solution.py:176
  74.2 1.2 %shard_map.150 = bf16[8,2048]{1,0:T(8,128)(2,1)} custom-call(s32[32]{0:T(128)S(1)} %copy-done.3, bf16[8,2048]{1,0:T(8,128)(2,1)S(1)} %shard_map.140.refs_0_.stream_ref, bf16[8,2048]{1,0:T(8,128)(2,1)S(1)} %get-tuple-element.27.refs_0_, bf16[8,2048]{1,0:T(8,128)(2,1)S(1)} %collective-permute-done.14.refs_1_, ...), custom_call_target="tpu_custom_call" | custom-call | bytes 1048576 | tf_op jit(solution)/shard_map/pallas_call | solution.py:186
  (63 shorter events, 2.8 us)
Async XLA Ops:
  0.0 11.7 %copy-start.1 = (bf16[8,2048]{1,0:T(8,128)(2,1)S(1)}, bf16[8,2048]{1,0:T(8,128)(2,1)}, u32[]{:S(2)}) copy-start(bf16[8,2048]{1,0:T(8,128)(2,1)} %stream_ref.1) | copy-start | bytes 98308
  0.0 11.7 %copy-start.10 = (f32[2048]{0:T(1024)S(1)}, f32[2048]{0:T(1024)}, u32[]{:S(2)}) copy-start(f32[2048]{0:T(1024)} %param.15) | copy-start | bytes 24580
  0.0 11.7 %copy-start.4 = (bf16[2048,1024]{1,0:T(8,128)(2,1)S(1)}, bf16[2048,1024]{1,0:T(8,128)(2,1)}, u32[]{:S(2)}) copy-start(bf16[2048,1024]{1,0:T(8,128)(2,1)} %refs_5_.2) | copy-start | bytes 12582916
  0.0 11.7 %copy-start.6 = (bf16[2048,128]{1,0:T(8,128)(2,1)S(1)}, bf16[2048,128]{1,0:T(8,128)(2,1)}, u32[]{:S(2)}) copy-start(bf16[2048,128]{1,0:T(8,128)(2,1)} %refs_6_.1) | copy-start | bytes 1572868
  0.0 11.7 %copy-start.7 = (bf16[2048,128]{1,0:T(8,128)(2,1)S(1)}, bf16[2048,128]{1,0:T(8,128)(2,1)}, u32[]{:S(2)}) copy-start(bf16[2048,128]{1,0:T(8,128)(2,1)} %refs_7_.1) | copy-start | bytes 1572868
  0.0 7.0 %collective-permute-start = (bf16[8,2048]{1,0:T(8,128)(2,1)}, bf16[8,2048]{1,0:T(8,128)(2,1)S(1)}, u32[]{:S(2)}, u32[]{:S(2)}) collective-permute-start(bf16[8,2048]{1,0:T(8,128)(2,1)} %stream_ref.1), channel_id=1, source_target_pairs={{0,1},{1,0},{2,3},{3,2},{4,5},{5,4},{6,7},{7,6},{8,9},{9,8},{10,11... | collective-permute-start | bytes 98312 | tf_op jit(solution)/shard_map/ppermute | solution.py:176
  3.1 5.6 %collective-permute-start.1 = (bf16[8,2048]{1,0:T(8,128)(2,1)}, bf16[8,2048]{1,0:T(8,128)(2,1)S(1)}, u32[]{:S(2)}, u32[]{:S(2)}) collective-permute-start(bf16[8,2048]{1,0:T(8,128)(2,1)} %stream_ref.1), channel_id=1, source_target_pairs={{0,2},{1,3},{2,0},{3,1},{4,6},{5,7},{6,4},{7,5},{8,10},{9,11},{10,... | collective-permute-start | bytes 98312 | tf_op jit(solution)/shard_map/ppermute | solution.py:176
  5.7 5.9 %collective-permute-start.2 = (bf16[8,2048]{1,0:T(8,128)(2,1)}, bf16[8,2048]{1,0:T(8,128)(2,1)S(1)}, u32[]{:S(2)}, u32[]{:S(2)}) collective-permute-start(bf16[8,2048]{1,0:T(8,128)(2,1)} %stream_ref.1), channel_id=1, source_target_pairs={{0,3},{1,2},{2,1},{3,0},{4,7},{5,6},{6,5},{7,4},{8,11},{9,10},{10,... | collective-permute-start | bytes 98312 | tf_op jit(solution)/shard_map/ppermute | solution.py:176
  11.7 10.7 %copy-start.8 = (bf16[2,256,512]{2,1,0:T(8,128)(2,1)S(1)}, bf16[2,256,512]{2,1,0:T(8,128)(2,1)}, u32[]{:S(2)}) copy-start(bf16[2,256,512]{2,1,0:T(8,128)(2,1)} %keys_ref.1) | copy-start | bytes 1572868
  11.7 10.7 %copy-start.9 = (bf16[2,256,512]{2,1,0:T(8,128)(2,1)S(1)}, bf16[2,256,512]{2,1,0:T(8,128)(2,1)}, u32[]{:S(2)}) copy-start(bf16[2,256,512]{2,1,0:T(8,128)(2,1)} %values_ref.1) | copy-start | bytes 1572868
  11.7 10.7 %copy-start.12 = (s32[2]{0:T(128)S(1)}, s32[2]{0:T(128)}, u32[]{:S(2)}) copy-start(s32[2]{0:T(128)} %lengths_ref.3) | copy-start | bytes 28
  22.4 11.0 %copy-start.5 = (bf16[1024,2048]{1,0:T(8,128)(2,1)S(1)}, bf16[1024,2048]{1,0:T(8,128)(2,1)}, u32[]{:S(2)}) copy-start(bf16[1024,2048]{1,0:T(8,128)(2,1)} %w_ref.6) | copy-start | bytes 12582916
  23.8 29.0 %slice-start = ((s8[14680064]{0:T(1024)(128)(4,1)}), s8[4194304]{0:T(1024)(128)(4,1)S(1)}, s32[]{:S(2)}) async-start(s8[14680064]{0:T(1024)(128)(4,1)} %bitcast.2), calls=%async_computation.2 | async-start | bytes 8388608
  33.4 18.0 %copy-start = (bf16[2048,3584]{1,0:T(8,128)(2,1)S(1)}, bf16[2048,3584]{1,0:T(8,128)(2,1)}, u32[]{:S(2)}) copy-start(bf16[2048,3584]{1,0:T(8,128)(2,1)} %w_ref.7) | copy-start | bytes 44040196
  33.4 18.0 %copy-start.2 = (f32[2048]{0:T(1024)S(1)}, f32[2048]{0:T(1024)}, u32[]{:S(2)}) copy-start(f32[2048]{0:T(1024)} %param.24) | copy-start | bytes 24580
  33.4 19.4 %slice-start.1 = ((s8[14680064]{0:T(1024)(128)(4,1)}), s8[4194304]{0:T(1024)(128)(4,1)S(1)}, s32[]{:S(2)}) async-start(s8[14680064]{0:T(1024)(128)(4,1)} %bitcast.2), calls=%async_computation.3 | async-start | bytes 8388608
  33.4 19.4 %slice-start.2 = ((s8[14680064]{0:T(1024)(128)(4,1)}), s8[4194304]{0:T(1024)(128)(4,1)S(1)}, s32[]{:S(2)}) async-start(s8[14680064]{0:T(1024)(128)(4,1)} %bitcast.2), calls=%async_computation.4 | async-start | bytes 8388608
  33.4 19.4 %slice-start.3 = ((s8[14680064]{0:T(1024)(128)(4,1)}), s8[2097152]{0:T(1024)(128)(4,1)S(1)}, s32[]{:S(2)}) async-start(s8[14680064]{0:T(1024)(128)(4,1)} %bitcast.2), calls=%async_computation.5 | async-start | bytes 4194304
  34.3 4.5 %collective-permute-start.3 = (bf16[8,2048]{1,0:T(8,128)(2,1)S(1)}, bf16[8,2048]{1,0:T(8,128)(2,1)S(1)}, u32[]{:S(2)}, u32[]{:S(2)}) collective-permute-start(bf16[8,2048]{1,0:T(8,128)(2,1)S(1)} %get-tuple-element.21), channel_id=1, source_target_pairs={{0,1},{1,0},{2,3},{3,2},{4,5},{5,4},{6,7},{7,6},{8,9},{9,8},{10,11... | collective-permute-start | bytes 98312 | tf_op jit(solution)/shard_map/ppermute | solution.py:176
  34.7 5.5 %collective-permute-start.4 = (bf16[8,2048]{1,0:T(8,128)(2,1)S(1)}, bf16[8,2048]{1,0:T(8,128)(2,1)S(1)}, u32[]{:S(2)}, u32[]{:S(2)}) collective-permute-start(bf16[8,2048]{1,0:T(8,128)(2,1)S(1)} %get-tuple-element.22), channel_id=1, source_target_pairs={{0,2},{1,3},{2,0},{3,1},{4,6},{5,7},{6,4},{7,5},{8,10},{9,11},{10,... | collective-permute-start | bytes 98312 | tf_op jit(solution)/shard_map/ppermute | solution.py:176
  35.7 5.7 %collective-permute-start.5 = (bf16[8,2048]{1,0:T(8,128)(2,1)S(1)}, bf16[8,2048]{1,0:T(8,128)(2,1)S(1)}, u32[]{:S(2)}, u32[]{:S(2)}) collective-permute-start(bf16[8,2048]{1,0:T(8,128)(2,1)S(1)} %get-tuple-element.23), channel_id=1, source_target_pairs={{0,3},{1,2},{2,1},{3,0},{4,7},{5,6},{6,5},{7,4},{8,11},{9,10},{10,... | collective-permute-start | bytes 98312 | tf_op jit(solution)/shard_map/ppermute | solution.py:176
  42.0 4.5 %collective-permute-start.6 = (bf16[8,2048]{1,0:T(8,128)(2,1)S(1)}, bf16[8,2048]{1,0:T(8,128)(2,1)S(1)}, u32[]{:S(2)}, u32[]{:S(2)}) collective-permute-start(bf16[8,2048]{1,0:T(8,128)(2,1)S(1)} %shard_map.140.refs_0_.stream_ref), channel_id=1, source_target_pairs={{0,1},{1,0},{2,3},{3,2},{4,5},{5,4},{6,7},{7,6},{8,9},{9,8},{10,11... | collective-permute-start | bytes 98312 | tf_op jit(solution)/shard_map/ppermute | solution.py:176
  42.1 5.4 %collective-permute-start.7 = (bf16[8,2048]{1,0:T(8,128)(2,1)S(1)}, bf16[8,2048]{1,0:T(8,128)(2,1)S(1)}, u32[]{:S(2)}, u32[]{:S(2)}) collective-permute-start(bf16[8,2048]{1,0:T(8,128)(2,1)S(1)} %shard_map.140.refs_0_.stream_ref), channel_id=1, source_target_pairs={{0,2},{1,3},{2,0},{3,1},{4,6},{5,7},{6,4},{7,5},{8,10},{9,11},{10,... | collective-permute-start | bytes 98312 | tf_op jit(solution)/shard_map/ppermute | solution.py:176
  45.7 5.7 %collective-permute-start.8 = (bf16[8,2048]{1,0:T(8,128)(2,1)S(1)}, bf16[8,2048]{1,0:T(8,128)(2,1)S(1)}, u32[]{:S(2)}, u32[]{:S(2)}) collective-permute-start(bf16[8,2048]{1,0:T(8,128)(2,1)S(1)} %shard_map.140.refs_0_.stream_ref), channel_id=1, source_target_pairs={{0,3},{1,2},{2,1},{3,0},{4,7},{5,6},{6,5},{7,4},{8,11},{9,10},{10,... | collective-permute-start | bytes 98312 | tf_op jit(solution)/shard_map/ppermute | solution.py:176
  52.8 3.4 %collective-permute-start.9 = (bf16[32,1920]{1,0:T(8,128)(2,1)S(1)}, bf16[32,1920]{1,0:T(8,128)(2,1)S(1)}, u32[]{:S(2)}, u32[]{:S(2)}) collective-permute-start(bf16[32,1920]{1,0:T(8,128)(2,1)S(1)} %get-tuple-element.26), channel_id=1, source_target_pairs={{0,4},{4,0},{8,12},{12,8},{1,5},{5,1},{9,13},{13,9},{2,6},{6,2},{1... | collective-permute-start | bytes 368648 | tf_op jit(solution)/shard_map/ppermute | solution.py:176
  54.2 4.2 %collective-permute-start.11 = (bf16[32,1792]{1,0:T(8,128)(2,1)S(1)}, bf16[32,1792]{1,0:T(8,128)(2,1)S(1)}, u32[]{:S(2)}, u32[]{:S(2)}) collective-permute-start(bf16[32,1792]{1,0:T(8,128)(2,1)S(1)} %shard_map.145), channel_id=1, source_target_pairs={{0,4},{4,0},{8,12},{12,8},{1,5},{5,1},{9,13},{13,9},{2,6},{6,2},{1... | collective-permute-start | bytes 344072 | tf_op jit(solution)/shard_map/ppermute | solution.py:176
  56.3 7.8 %collective-permute-start.10 = (bf16[32,1920]{1,0:T(8,128)(2,1)S(1)}, bf16[32,1920]{1,0:T(8,128)(2,1)S(1)}, u32[]{:S(2)}, u32[]{:S(2)}) collective-permute-start(bf16[32,1920]{1,0:T(8,128)(2,1)S(1)} %shard_map.143.gate_ref), channel_id=1, source_target_pairs={{0,8},{4,12},{8,0},{12,4},{1,9},{5,13},{9,1},{13,5},{2,10},{6,14},... | collective-permute-start | bytes 368648 | tf_op jit(solution)/shard_map/ppermute | solution.py:176
  58.5 5.6 %collective-permute-start.12 = (bf16[32,1792]{1,0:T(8,128)(2,1)S(1)}, bf16[32,1792]{1,0:T(8,128)(2,1)S(1)}, u32[]{:S(2)}, u32[]{:S(2)}) collective-permute-start(bf16[32,1792]{1,0:T(8,128)(2,1)S(1)} %shard_map.146.up_ref), channel_id=1, source_target_pairs={{0,8},{4,12},{8,0},{12,4},{1,9},{5,13},{9,1},{13,5},{2,10},{6,14},... | collective-permute-start | bytes 344072 | tf_op jit(solution)/shard_map/ppermute | solution.py:176
  64.3 1.5 %collective-permute-start.13 = (bf16[32,1792]{1,0:T(8,128)(2,1)S(1)}, bf16[32,1792]{1,0:T(8,128)(2,1)S(1)}, u32[]{:S(2)}, u32[]{:S(2)}) collective-permute-start(bf16[32,1792]{1,0:T(8,128)(2,1)S(1)} %shard_map.147.own_ref), channel_id=1, source_target_pairs={{0,4},{4,0},{8,12},{12,8},{1,5},{5,1},{9,13},{13,9},{2,6},{6,2},{1... | collective-permute-start | bytes 344072 | tf_op jit(solution)/shard_map/ppermute | solution.py:176
  67.1 4.4 %collective-permute-start.14 = (bf16[8,2048]{1,0:T(8,128)(2,1)S(1)}, bf16[8,2048]{1,0:T(8,128)(2,1)S(1)}, u32[]{:S(2)}, u32[]{:S(2)}) collective-permute-start(bf16[8,2048]{1,0:T(8,128)(2,1)S(1)} %get-tuple-element.28), channel_id=1, source_target_pairs={{0,1},{1,0},{2,3},{3,2},{4,5},{5,4},{6,7},{7,6},{8,9},{9,8},{10,11... | collective-permute-start | bytes 98312 | tf_op jit(solution)/shard_map/ppermute | solution.py:176
  67.1 5.1 %collective-permute-start.15 = (bf16[8,2048]{1,0:T(8,128)(2,1)S(1)}, bf16[8,2048]{1,0:T(8,128)(2,1)S(1)}, u32[]{:S(2)}, u32[]{:S(2)}) collective-permute-start(bf16[8,2048]{1,0:T(8,128)(2,1)S(1)} %get-tuple-element.29), channel_id=1, source_target_pairs={{0,2},{1,3},{2,0},{3,1},{4,6},{5,7},{6,4},{7,5},{8,10},{9,11},{10,... | collective-permute-start | bytes 98312 | tf_op jit(solution)/shard_map/ppermute | solution.py:176
  68.4 5.7 %collective-permute-start.16 = (bf16[8,2048]{1,0:T(8,128)(2,1)S(1)}, bf16[8,2048]{1,0:T(8,128)(2,1)S(1)}, u32[]{:S(2)}, u32[]{:S(2)}) collective-permute-start(bf16[8,2048]{1,0:T(8,128)(2,1)S(1)} %get-tuple-element.30), channel_id=1, source_target_pairs={{0,3},{1,2},{2,1},{3,0},{4,7},{5,6},{6,5},{7,4},{8,11},{9,10},{10,... | collective-permute-start | bytes 98312 | tf_op jit(solution)/shard_map/ppermute | solution.py:176
  (6 other events, 45.1 us)

commit v3 on v2

--- a/solution.py
+++ b/solution.py
@@ -155,7 +155,7 @@
 
 LANES = 128
 MIB = 2**20
-COVER = (100, 100, 100, 100, 1, 1, 1, 1, 1, 1)
+COVER = (100, 100, 100, 1, 1, 1, 1, 1, 1, 1)
 CHUNK = 512
 
 
@@ -219,13 +219,15 @@
 
 
 def project_kernel(_, *refs):
-    *block_refs, gain_ref, wq_ref, wk_ref, wv_ref, out_ref, rows_ref, sums_ref, packed_ref = refs
+    *block_refs, gain_ref, wq_ref, wk_ref, wv_ref, out_ref, stream_ref = refs[:-3]
+    rows_ref, sums_ref, packed_ref = refs[-3:]
     place = lax.axis_index("tp")
     own = block_refs[0].shape[0]
     for k, block_ref in enumerate(block_refs):
         start = pl.multiple_of((place ^ k) * own, own)
         rows_ref[pl.ds(start, own), :] = block_ref[...].astype(jnp.float32)
     rows = rows_ref[...]
+    stream_ref[...] = rows.astype(jnp.bfloat16)
     squares = jnp.sum(rows * rows, axis=1, keepdims=True)
     scaled = (rows * gain_ref[...]).astype(jnp.bfloat16)
     count = rows.shape[0]
@@ -316,19 +318,20 @@
 
 
 def output_kernel(heads_ref, w_ref, *refs):
-    *out_refs, heads_wide_ref, rows_ref = refs
-    place = lax.axis_index("tp")
-    own = out_refs[0].shape[0]
+    *out_refs, heads_wide_ref = refs
+    count = sum(ref.shape[0] for ref in out_refs)
     groups = w_ref.shape[0] // LANES
     heads_wide_ref[...] = heads_ref[...].astype(jnp.float32).reshape(heads_wide_ref.shape)
     attended = jnp.concatenate(
-        [heads_wide_ref[pl.ds(g, rows_ref.shape[0], stride=groups), :] for g in range(groups)],
-        axis=1,
+        [heads_wide_ref[pl.ds(g, count, stride=groups), :] for g in range(groups)], axis=1
     ).astype(jnp.bfloat16)
-    rows_ref[...] = jnp.dot(attended, w_ref[...], preferred_element_type=jnp.float32)
-    for k, out_ref in enumerate(out_refs):
-        start = pl.multiple_of((place ^ k) * own, own)
-        out_ref[...] = rows_ref[pl.ds(start, own), :].astype(jnp.bfloat16)
+    for at in range(0, w_ref.shape[1], CHUNK):
+        part = slice(at, min(at + CHUNK, w_ref.shape[1]))
+        rows = jnp.dot(attended, w_ref[:, part], preferred_element_type=jnp.float32)
+        start = 0
+        for out_ref in out_refs:
+            out_ref[:, part] = rows[start : start + out_ref.shape[0]].astype(jnp.bfloat16)
+            start += out_ref.shape[0]
 
 
 def add_kernel(served_ref, stream_ref, *refs):
@@ -349,8 +352,28 @@
 
 
 def gate_send_kernel(*refs):
-    *block_refs, gain_ref, w_ref, scaled_ref, tail_ref, send_ref = refs
-    rows = jnp.concatenate([ref[...].astype(jnp.float32) for ref in block_refs], axis=0)
+    served_ref, stream_ref, *term_refs, gain_ref, w_ref = refs[:-5]
+    scaled_ref, tail_ref, send_ref, middle_ref, rows_ref = refs[-5:]
+    count = stream_ref.shape[0]
+    row = lax.broadcasted_iota(jnp.int32, (count, count), 0)
+    column = lax.broadcasted_iota(jnp.int32, (count, count), 1)
+    live = jnp.sum(
+        jnp.where(row == column, served_ref[...], 0).astype(jnp.float32), axis=1, keepdims=True
+    )
+    pieces = len(term_refs) // 2
+    attn = jnp.concatenate(
+        [
+            term_refs[2 * i][...].astype(jnp.float32) + term_refs[2 * i + 1][...].astype(jnp.float32)
+            for i in range(pieces)
+        ],
+        axis=0,
+    )
+    rows = (stream_ref[...].astype(jnp.float32) + live * attn).astype(jnp.bfloat16)
+    rows = rows.astype(jnp.float32)
+    rows_ref[...] = rows
+    own = middle_ref.shape[0]
+    start = pl.multiple_of(lax.axis_index("tp") * own, own)
+    middle_ref[...] = rows_ref[pl.ds(start, own), :].astype(jnp.bfloat16)
     squares = jnp.sum(rows * rows, axis=1, keepdims=True)
     scaled = (rows * gain_ref[...]).astype(jnp.bfloat16)
     scaled_ref[...] = scaled
@@ -392,8 +415,8 @@
     out_ref[:, wide:] = split_three(squares)
 
 
-def pair_up_kernel(keep_ref, got_ref, out_ref):
-    out_ref[...] = (keep_ref[...] + got_ref[...].astype(jnp.float32)).astype(jnp.bfloat16)
+def pair_kernel(keep_ref, got_ref, out_ref):
+    out_ref[...] = (keep_ref[...].astype(jnp.float32) + got_ref[...].astype(jnp.float32)).astype(jnp.bfloat16)
 
 
 def hidden_kernel(gate_ref, gate_got_ref, up_ref, up_got_ref, out_ref):
@@ -421,18 +444,21 @@
         )
 
 
-def down_kernel(other_ref, w_ref, rows_ref, *out_refs):
+def down_kernel(other_ref, w_ref, rows_ref, *refs):
+    *out_refs, total_ref = refs
     half = lax.rem(lax.axis_index("role"), 2)
+    place = lax.axis_index("tp")
     width = other_ref.shape[1]
     theirs = pl.ds(pl.multiple_of((1 - half) * width, LANES), width)
     own = out_refs[0].shape[0]
     for at in range(0, w_ref.shape[1], CHUNK):
         part = slice(at, min(at + CHUNK, w_ref.shape[1]))
-        rows = rows_ref[:, part] + jnp.dot(
+        total_ref[:, part] = rows_ref[:, part] + jnp.dot(
             other_ref[...], w_ref[theirs, part], preferred_element_type=jnp.float32
         )
-        for k, out_ref in enumerate(out_refs):
-            out_ref[:, part] = rows[k * own : (k + 1) * own].astype(jnp.bfloat16)
+    for k, out_ref in enumerate(out_refs):
+        start = pl.multiple_of((place ^ k) * own, own)
+        out_ref[...] = total_ref[pl.ds(start, own), :].astype(jnp.bfloat16)
 
 
 def local_exchange(
@@ -477,12 +503,16 @@
 
     table = jax.ShapeDtypeStruct((each, HEAD_DIM), jnp.float32)
     cosine, sine = call(angle_kernel, [table] * 2, [lengths], smem=1, cost=COVER[0])
-    blocks = [residual] + [swap(residual, "tp", k) for k in range(1, tp_count)]
+    others = {k: swap(residual, "tp", k) for k in reversed(range(1, tp_count))}
+    blocks = [residual] + [others[k] for k in range(1, tp_count)]
     payload = w_query.shape[1] + 2 * w_key.shape[1] + LANES
     depth = -(-each * payload // (LANES * 8)) * 8
-    (sums,) = call(
+    sums, stream = call(
         project_kernel,
-        [jax.ShapeDtypeStruct((devices, depth, LANES), jnp.bfloat16)],
+        [
+            jax.ShapeDtypeStruct((devices, depth, LANES), jnp.bfloat16),
+            jax.ShapeDtypeStruct((rows, features), jnp.bfloat16),
+        ],
         [cosine, *blocks, attn_gain[None, :], in_vmem(w_query), in_vmem(w_key), in_vmem(w_value)],
         scratch=[
             pltpu.VMEM((rows, features), jnp.float32),
@@ -500,34 +530,36 @@
         cost=COVER[2],
     )
     heads = lax.all_to_all(heads, ("role", "tp"), 0, 0)
-    terms = call(
+    pieces = 2
+    piece = jax.ShapeDtypeStruct((rows // pieces, features), jnp.bfloat16)
+    attn = call(
         output_kernel,
-        [block] * tp_count,
+        [piece] * pieces,
         [heads, in_vmem(w_output)],
-        scratch=[
-            pltpu.VMEM((rows * GROUP, LANES), jnp.float32),
-            pltpu.VMEM((rows, features), jnp.float32),
-        ],
+        scratch=[pltpu.VMEM((rows * GROUP, LANES), jnp.float32)],
         cost=COVER[3],
     )
-    terms = [terms[0]] + [swap(terms[k], "tp", k) for k in range(1, tp_count)]
-    (middle,) = call(add_kernel, [block], [served, residual, *terms], smem=1)
-
-    blocks = [middle] + [swap(middle, "tp", k) for k in range(1, tp_count)]
+    terms = []
+    near = [swap(value, "tp", 1) for value in attn]
+    for value, got in zip(attn, near):
+        (paired,) = call(pair_kernel, [piece], [value, got])
+        terms += [paired, swap(paired, "tp", 2)]
     width = w_gate.shape[1] // 2
     wide = width + LANES
     half_f32 = jax.ShapeDtypeStruct((rows, width), jnp.float32)
     half_bf16 = jax.ShapeDtypeStruct((rows, width), jnp.bfloat16)
     wide_bf16 = jax.ShapeDtypeStruct((rows, wide), jnp.bfloat16)
     w_gate, w_up, w_down = in_vmem(w_gate), in_vmem(w_up), in_vmem(w_down)
-    scaled, tail, gate_send = call(
+    scaled, tail, gate_send, middle = call(
         gate_send_kernel,
         [
             jax.ShapeDtypeStruct((rows, features), jnp.bfloat16),
             jax.ShapeDtypeStruct((rows, LANES), jnp.float32),
             wide_bf16,
+            block,
         ],
-        [*blocks, ffn_gain[None, :], w_gate],
+        [served[None, :], stream, *terms, ffn_gain[None, :], w_gate],
+        scratch=[pltpu.VMEM((rows, features), jnp.float32)],
         cost=COVER[4],
     )
     gate_got = swap(gate_send, "role", 1)
@@ -536,7 +568,7 @@
     (up_send,) = call(send_kernel, [half_bf16], [scaled, w_up], cost=COVER[6])
     up_got = swap(up_send, "role", 1)
     (up,) = call(keep_kernel, [half_f32], [scaled, w_up], cost=COVER[7])
-    (up,) = call(pair_up_kernel, [half_bf16], [up, up_got])
+    (up,) = call(pair_kernel, [half_bf16], [up, up_got])
     gate_got, up_got = swap(gate, "role", 2), swap(up, "role", 2)
     (hidden,) = call(
         hidden_kernel,
@@ -550,7 +582,13 @@
         [hidden, w_down],
         cost=COVER[8],
     )
-    terms = call(down_kernel, [block] * tp_count, [other, w_down, down], cost=COVER[9])
+    terms = call(
+        down_kernel,
+        [block] * tp_count,
+        [other, w_down, down],
+        scratch=[pltpu.VMEM((rows, features), jnp.float32)],
+        cost=COVER[9],
+    )
     terms = [terms[0]] + [swap(terms[k], "tp", k) for k in range(1, tp_count)]
     return call(add_kernel, [block], [served, middle, *terms], smem=1)[0]
 

time: 75.6 us -> 70.9 us (0.938)
  starting transfers between devices: 21.8 us -> 18.1 us
    ppermute x17 -> x15, starting transfers between devices: 21.8 us -> 18.1 us  [swap(): return lax.ppermute(value, axis, [(i, i ^ distance) for i in range(count)])]
    pallas_call x15 -> x16, Pallas kernels: 14.1 us -> 13.5 us  [call(): pl.pallas_call(kernel, out_shape=outs, in_specs=specs, out_specs=[pl.Bloc...]
    ppermute x17 -> x15, waiting for transfers between devices: 19.1 us -> 18.6 us  [swap(): return lax.ppermute(value, axis, [(i, i ^ distance) for i in range(count)])]
  transfers between devices with their start and end apart: 17 -> 15, of which waited for: 9 -> 8; matrix products, arithmetic and copies ran while one was open for 0% -> 0% of each run, Pallas kernels for 8% -> 9%
where the time goes in v3:
time: 70.9 us; the launch traced here: 70.7 us
  blocking collectives  19.4 us (27%)
  waiting for transfers between devices  18.6 us (26%)
  starting transfers between devices  18.1 us (26%)
  Pallas kernels  13.5 us (19%)
  local copies, waits for them, and re-layouts  0.76 us (1%)
    ppermute x15, waiting for transfers between devices, swap(): return lax.ppermute(value, axis, [(i, i ^ distance) for i in range(count)])  18.6 us
    ppermute x15, starting transfers between devices, swap(): return lax.ppermute(value, axis, [(i, i ^ distance) for i in range(count)])  18.1 us
    pallas_call x16, Pallas kernels, call(): pl.pallas_call(kernel, out_shape=outs, in_specs=specs, out_specs=[pl.Bloc...  13.5 us
    all_to_all x1, blocking collectives, local_exchange(): heads = lax.all_to_all(heads, ('role', 'tp'), 0, 0)  9.72 us
    all_to_all x1, blocking collectives, local_exchange(): parts = lax.all_to_all(sums, ('role', 'tp'), 0, 0)  9.65 us
  transfers between devices with their start and end apart: 15, of which 8 were waited for; matrix products, arithmetic and copies ran while one was open for 0% of the time, Pallas kernels for 9%

profile of v3, /device:TPU:0, one launch (start us, length us, event | category | flops | bytes accessed | tf_op | source)
XLA Modules:
  0.0 70.7 jit_solution(9888713665968041977)
XLA Ops:
  0.0 3.1 %collective-permute-start = (bf16[8,2048]{1,0:T(8,128)(2,1)}, bf16[8,2048]{1,0:T(8,128)(2,1)S(1)}, u32[]{:S(2)}, u32[]{:S(2)}) collective-permute-start(bf16[8,2048]{1,0:T(8,128)(2,1)} %refs_0_.1), channel_id=1, source_target_pairs={{0,1},{1,0},{2,3},{3,2},{4,5},{5,4},{6,7},{7,6},{8,9},{9,8},{10,11... | collective-permute-start | bytes 98312 | tf_op jit(solution)/shard_map/ppermute | solution.py:176
  3.1 2.6 %collective-permute-start.1 = (bf16[8,2048]{1,0:T(8,128)(2,1)}, bf16[8,2048]{1,0:T(8,128)(2,1)S(1)}, u32[]{:S(2)}, u32[]{:S(2)}) collective-permute-start(bf16[8,2048]{1,0:T(8,128)(2,1)} %refs_0_.1), channel_id=1, source_target_pairs={{0,2},{1,3},{2,0},{3,1},{4,6},{5,7},{6,4},{7,5},{8,10},{9,11},{10,... | collective-permute-start | bytes 98312 | tf_op jit(solution)/shard_map/ppermute | solution.py:176
  5.7 0.7 copy-done.11
  6.4 0.6 shard_map.136
  7.0 1.8 %collective-permute-done.1.refs_2_ = bf16[8,2048]{1,0:T(8,128)(2,1)S(1)} collective-permute-done((bf16[8,2048]{1,0:T(8,128)(2,1)}, bf16[8,2048]{1,0:T(8,128)(2,1)S(1)}, u32[]{:S(2)}, u32[]{:S(2)}) %collective-permute-start.1) | collective-permute-done | bytes 32800 | tf_op jit(solution)/shard_map/ppermute | solution.py:176
  8.8 2.9 %collective-permute-done.2.refs_3_ = bf16[8,2048]{1,0:T(8,128)(2,1)S(1)} collective-permute-done((bf16[8,2048]{1,0:T(8,128)(2,1)}, bf16[8,2048]{1,0:T(8,128)(2,1)S(1)}, u32[]{:S(2)}, u32[]{:S(2)}) %collective-permute-start.2) | collective-permute-done | bytes 32800 | tf_op jit(solution)/shard_map/ppermute | solution.py:176
  11.7 1.0 %shard_map.137 = (bf16[16,24,128]{2,1,0:T(8,128)(2,1)S(1)}, bf16[32,2048]{1,0:T(8,128)(2,1)S(1)}) custom-call(f32[2,128]{1,0:T(2,128)S(1)} %get-tuple-element.19._.cosine_ref, bf16[8,2048]{1,0:T(8,128)(2,1)S(1)} %copy-done.9, bf16[8,2048]{1,0:T(8,128)(2,1)S(1)} %collective-permute-done.refs_1_, bf16[8,2048]{1,0:T(8,128)(2,1)S(1)} %collective-permute-done.1.refs_2_, ...), custom_call_target="tpu_custom_call" | custom-call | flops 99999997952 | bytes 1048576 | tf_op jit(solution)/shard_map/pallas_call | solution.py:186
  12.8 9.7 %all_to_all.10.got_ref = bf16[16,24,128]{2,1,0:T(8,128)(2,1)S(1)} all-to-all(bf16[16,24,128]{2,1,0:T(8,128)(2,1)S(1)} %get-tuple-element.21), channel_id=1, replica_groups=mesh['groups'=2,'role'=4,'tp'=4] {'role','tp'}, dimensions={0} | all-to-all | bytes 196608 | tf_op jit(solution)/shard_map/all_to_all | solution.py:524
  22.5 1.4 %shard_map.138 = bf16[16,16,128]{2,1,0:T(8,128)(2,1)S(1)} custom-call(s32[2]{0:T(128)S(1)} %copy-done.12, bf16[16,24,128]{2,1,0:T(8,128)(2,1)S(1)} %all_to_all.10.got_ref, f32[2,128]{1,0:T(2,128)S(1)} %get-tuple-element.19._.cosine_ref, f32[2,128]{1,0:T(2,128)S(1)} %get-tuple-element.22.sine_ref, bf16[2,256,512]{2,1,0:T(8,128)(2,1)S(1)} %copy-done.7, ...), custom_call_target="tpu_custom_call" | custom-call | flops 99999997952 | bytes 1048576 | tf_op jit(solution)/shard_map/pallas_call | solution.py:186
  23.9 9.7 %all_to_all.11.heads_ref = bf16[16,16,128]{2,1,0:T(8,128)(2,1)S(1)} all-to-all(bf16[16,16,128]{2,1,0:T(8,128)(2,1)S(1)} %shard_map.138), channel_id=1, replica_groups=mesh['groups'=2,'role'=4,'tp'=4] {'role','tp'}, dimensions={0} | all-to-all | bytes 131072 | tf_op jit(solution)/shard_map/all_to_all | solution.py:532
  33.6 0.8 %shard_map.139 = (bf16[16,2048]{1,0:T(8,128)(2,1)S(1)}, bf16[16,2048]{1,0:T(8,128)(2,1)S(1)}) custom-call(bf16[16,16,128]{2,1,0:T(8,128)(2,1)S(1)} %all_to_all.11.heads_ref, bf16[1024,2048]{1,0:T(8,128)(2,1)S(1)} %copy-done.1), custom_call_target="tpu_custom_call" | custom-call | flops 1000000000 | bytes 1048576 | tf_op jit(solution)/shard_map/pallas_call | solution.py:186
  34.8 1.7 %collective-permute-start.5 = (bf16[16,2048]{1,0:T(8,128)(2,1)S(1)}, bf16[16,2048]{1,0:T(8,128)(2,1)S(1)}, u32[]{:S(2)}, u32[]{:S(2)}) collective-permute-start(bf16[16,2048]{1,0:T(8,128)(2,1)S(1)} %get-tuple-element.24.keep_ref), channel_id=1, source_target_pairs={{0,1},{1,0},{2,3},{3,2},{4,5},{5,4},{6,7},{7,6},{8,9},{9,8},{10,11... | collective-permute-start | bytes 196616 | tf_op jit(solution)/shard_map/ppermute | solution.py:176
  36.5 2.8 %collective-permute-done.3.got_ref = bf16[16,2048]{1,0:T(8,128)(2,1)S(1)} collective-permute-done((bf16[16,2048]{1,0:T(8,128)(2,1)S(1)}, bf16[16,2048]{1,0:T(8,128)(2,1)S(1)}, u32[]{:S(2)}, u32[]{:S(2)}) %collective-permute-start.3) | collective-permute-done | bytes 65568 | tf_op jit(solution)/shard_map/ppermute | solution.py:176
  39.3 0.7 collective-permute-start.4
  40.0 2.4 %collective-permute-start.6 = (bf16[16,2048]{1,0:T(8,128)(2,1)S(1)}, bf16[16,2048]{1,0:T(8,128)(2,1)S(1)}, u32[]{:S(2)}, u32[]{:S(2)}) collective-permute-start(bf16[16,2048]{1,0:T(8,128)(2,1)S(1)} %shard_map.141.refs_4_), channel_id=1, source_target_pairs={{0,2},{1,3},{2,0},{3,1},{4,6},{5,7},{6,4},{7,5},{8,10},{9,11},{10,... | collective-permute-start | bytes 196616 | tf_op jit(solution)/shard_map/ppermute | solution.py:176
  42.4 3.7 %collective-permute-done.4.refs_3_ = bf16[16,2048]{1,0:T(8,128)(2,1)S(1)} collective-permute-done((bf16[16,2048]{1,0:T(8,128)(2,1)S(1)}, bf16[16,2048]{1,0:T(8,128)(2,1)S(1)}, u32[]{:S(2)}, u32[]{:S(2)}) %collective-permute-start.4) | collective-permute-done | bytes 65568 | tf_op jit(solution)/shard_map/ppermute | solution.py:176
  46.1 0.7 collective-permute-done.6.refs_5_
  46.8 1.3 %shard_map.142 = (bf16[32,2048]{1,0:T(8,128)(2,1)S(1)}, f32[32,128]{1,0:T(8,128)S(1)}, bf16[32,1920]{1,0:T(8,128)(2,1)S(1)}, bf16[8,2048]{1,0:T(8,128)(2,1)S(1)}) custom-call(s32[1,32]{1,0:T(1,128)S(1)} %bitcast.8, bf16[32,2048]{1,0:T(8,128)(2,1)S(1)} %get-tuple-element.20.refs_1_, bf16[16,2048]{1,0:T(8,128)(2,1)S(1)} %shard_map.140.refs_2_, ...), custom_call_target="tpu_custom_call" | custom-call | flops 1000000000 | bytes 1048576 | tf_op jit(solution)/shard_map/pallas_call | solution.py:186
  48.2 1.4 %shard_map.146 = bf16[32,1792]{1,0:T(8,128)(2,1)S(1)} custom-call(bf16[32,2048]{1,0:T(8,128)(2,1)S(1)} %get-tuple-element.26.scaled_ref, bf16[2048,3584]{1,0:T(8,128)(2,1)S(1)} %bitcast.4), custom_call_target="tpu_custom_call" | custom-call | flops 1000000000 | bytes 1048576 | tf_op jit(solution)/shard_map/pallas_call | solution.py:186
  49.6 0.5 collective-permute-start.9
  50.2 1.4 %shard_map.143.keep_ref = f32[32,1792]{1,0:T(8,128)S(1)} custom-call(bf16[32,2048]{1,0:T(8,128)(2,1)S(1)} %get-tuple-element.26.scaled_ref, bf16[2048,3584]{1,0:T(8,128)(2,1)S(1)} %copy-done), custom_call_target="tpu_custom_call" | custom-call | flops 1000000000 | bytes 1048576 | tf_op jit(solution)/shard_map/pallas_call | solution.py:186
  51.6 0.6 collective-permute-start.8
  52.3 1.4 %shard_map.145.keep_ref = f32[32,1792]{1,0:T(8,128)S(1)} custom-call(bf16[32,2048]{1,0:T(8,128)(2,1)S(1)} %get-tuple-element.26.scaled_ref, bf16[2048,3584]{1,0:T(8,128)(2,1)S(1)} %bitcast.4), custom_call_target="tpu_custom_call" | custom-call | flops 1000000000 | bytes 1048576 | tf_op jit(solution)/shard_map/pallas_call | solution.py:186
  53.7 1.5 %collective-permute-start.10 = (bf16[32,1792]{1,0:T(8,128)(2,1)S(1)}, bf16[32,1792]{1,0:T(8,128)(2,1)S(1)}, u32[]{:S(2)}, u32[]{:S(2)}) collective-permute-start(bf16[32,1792]{1,0:T(8,128)(2,1)S(1)} %shard_map.147.up_ref), channel_id=1, source_target_pairs={{0,8},{4,12},{8,0},{12,4},{1,9},{5,13},{9,1},{13,5},{2,10},{6,14},... | collective-permute-start | bytes 344072 | tf_op jit(solution)/shard_map/ppermute | solution.py:176
  55.2 4.2 %collective-permute-done.10.up_got_ref = bf16[32,1792]{1,0:T(8,128)(2,1)S(1)} collective-permute-done((bf16[32,1792]{1,0:T(8,128)(2,1)S(1)}, bf16[32,1792]{1,0:T(8,128)(2,1)S(1)}, u32[]{:S(2)}, u32[]{:S(2)}) %collective-permute-start.10) | collective-permute-done | bytes 114720 | tf_op jit(solution)/shard_map/ppermute | solution.py:176
  59.7 1.4 %shard_map.149.rows_ref = f32[32,2048]{1,0:T(8,128)S(1)} custom-call(bf16[32,1792]{1,0:T(8,128)(2,1)S(1)} %shard_map.148.own_ref, bf16[3584,2048]{1,0:T(8,128)(2,1)S(1)} %bitcast.6), custom_call_target="tpu_custom_call" | custom-call | flops 1000000000 | bytes 1048576 | tf_op jit(solution)/shard_map/pallas_call | solution.py:186
  61.1 1.4 %shard_map.150 = (bf16[8,2048]{1,0:T(8,128)(2,1)S(1)}, bf16[8,2048]{1,0:T(8,128)(2,1)S(1)}, bf16[8,2048]{1,0:T(8,128)(2,1)S(1)}, bf16[8,2048]{1,0:T(8,128)(2,1)S(1)}) custom-call(bf16[32,1792]{1,0:T(8,128)(2,1)S(1)} %collective-permute-done.11.other_ref, bf16[3584,2048]{1,0:T(8,128)(2,1)S(1)} %bitcast.6, f32[32,2048]{1,0:T(8,128)S(1)} %shard_map.149.rows_ref), custom_call_target="tpu_custom_call" | custom-call | flops 1000000000 | bytes 1048576 | tf_op jit(solution)/shard_map/pallas_call | solution.py:186
  62.6 1.1 %collective-permute-start.13 = (bf16[8,2048]{1,0:T(8,128)(2,1)S(1)}, bf16[8,2048]{1,0:T(8,128)(2,1)S(1)}, u32[]{:S(2)}, u32[]{:S(2)}) collective-permute-start(bf16[8,2048]{1,0:T(8,128)(2,1)S(1)} %get-tuple-element.31), channel_id=1, source_target_pairs={{0,2},{1,3},{2,0},{3,1},{4,6},{5,7},{6,4},{7,5},{8,10},{9,11},{10,... | collective-permute-start | bytes 98312 | tf_op jit(solution)/shard_map/ppermute | solution.py:176
  63.7 3.2 %collective-permute-start.14 = (bf16[8,2048]{1,0:T(8,128)(2,1)S(1)}, bf16[8,2048]{1,0:T(8,128)(2,1)S(1)}, u32[]{:S(2)}, u32[]{:S(2)}) collective-permute-start(bf16[8,2048]{1,0:T(8,128)(2,1)S(1)} %get-tuple-element.32), channel_id=1, source_target_pairs={{0,3},{1,2},{2,1},{3,0},{4,7},{5,6},{6,5},{7,4},{8,11},{9,10},{10,... | collective-permute-start | bytes 98312 | tf_op jit(solution)/shard_map/ppermute | solution.py:176
  67.0 0.7 collective-permute-done.13.refs_2_
  67.7 1.8 %collective-permute-done.14.refs_3_ = bf16[8,2048]{1,0:T(8,128)(2,1)S(1)} collective-permute-done((bf16[8,2048]{1,0:T(8,128)(2,1)S(1)}, bf16[8,2048]{1,0:T(8,128)(2,1)S(1)}, u32[]{:S(2)}, u32[]{:S(2)}) %collective-permute-start.14) | collective-permute-done | bytes 32800 | tf_op jit(solution)/shard_map/ppermute | solution.py:176
  69.5 1.2 %shard_map.151 = bf16[8,2048]{1,0:T(8,128)(2,1)} custom-call(s32[32]{0:T(128)S(1)} %copy-done.3, bf16[8,2048]{1,0:T(8,128)(2,1)S(1)} %get-tuple-element.25.stream_ref, bf16[8,2048]{1,0:T(8,128)(2,1)S(1)} %get-tuple-element.29.refs_0_, bf16[8,2048]{1,0:T(8,128)(2,1)S(1)} %collective-permute-done.12.refs_1_, ...), custom_call_target="tpu_custom_call" | custom-call | bytes 1048576 | tf_op jit(solution)/shard_map/pallas_call | solution.py:186
  (60 shorter events, 1.1 us)
Async XLA Ops:
  0.0 11.7 %copy-start.9 = (bf16[8,2048]{1,0:T(8,128)(2,1)S(1)}, bf16[8,2048]{1,0:T(8,128)(2,1)}, u32[]{:S(2)}) copy-start(bf16[8,2048]{1,0:T(8,128)(2,1)} %refs_0_.1) | copy-start | bytes 98308
  0.0 11.7 %copy-start.10 = (f32[2048]{0:T(1024)S(1)}, f32[2048]{0:T(1024)}, u32[]{:S(2)}) copy-start(f32[2048]{0:T(1024)} %param.15) | copy-start | bytes 24580
  0.0 11.7 %copy-start.4 = (bf16[2048,1024]{1,0:T(8,128)(2,1)S(1)}, bf16[2048,1024]{1,0:T(8,128)(2,1)}, u32[]{:S(2)}) copy-start(bf16[2048,1024]{1,0:T(8,128)(2,1)} %refs_5_.1) | copy-start | bytes 12582916
  0.0 11.7 %copy-start.5 = (bf16[2048,128]{1,0:T(8,128)(2,1)S(1)}, bf16[2048,128]{1,0:T(8,128)(2,1)}, u32[]{:S(2)}) copy-start(bf16[2048,128]{1,0:T(8,128)(2,1)} %refs_6_.1) | copy-start | bytes 1572868
  0.0 11.7 %copy-start.6 = (bf16[2048,128]{1,0:T(8,128)(2,1)S(1)}, bf16[2048,128]{1,0:T(8,128)(2,1)}, u32[]{:S(2)}) copy-start(bf16[2048,128]{1,0:T(8,128)(2,1)} %refs_7_.2) | copy-start | bytes 1572868
  0.0 7.0 %collective-permute-start = (bf16[8,2048]{1,0:T(8,128)(2,1)}, bf16[8,2048]{1,0:T(8,128)(2,1)S(1)}, u32[]{:S(2)}, u32[]{:S(2)}) collective-permute-start(bf16[8,2048]{1,0:T(8,128)(2,1)} %refs_0_.1), channel_id=1, source_target_pairs={{0,1},{1,0},{2,3},{3,2},{4,5},{5,4},{6,7},{7,6},{8,9},{9,8},{10,11... | collective-permute-start | bytes 98312 | tf_op jit(solution)/shard_map/ppermute | solution.py:176
  3.1 5.6 %collective-permute-start.1 = (bf16[8,2048]{1,0:T(8,128)(2,1)}, bf16[8,2048]{1,0:T(8,128)(2,1)S(1)}, u32[]{:S(2)}, u32[]{:S(2)}) collective-permute-start(bf16[8,2048]{1,0:T(8,128)(2,1)} %refs_0_.1), channel_id=1, source_target_pairs={{0,2},{1,3},{2,0},{3,1},{4,6},{5,7},{6,4},{7,5},{8,10},{9,11},{10,... | collective-permute-start | bytes 98312 | tf_op jit(solution)/shard_map/ppermute | solution.py:176
  5.7 5.9 %collective-permute-start.2 = (bf16[8,2048]{1,0:T(8,128)(2,1)}, bf16[8,2048]{1,0:T(8,128)(2,1)S(1)}, u32[]{:S(2)}, u32[]{:S(2)}) collective-permute-start(bf16[8,2048]{1,0:T(8,128)(2,1)} %refs_0_.1), channel_id=1, source_target_pairs={{0,3},{1,2},{2,1},{3,0},{4,7},{5,6},{6,5},{7,4},{8,11},{9,10},{10,... | collective-permute-start | bytes 98312 | tf_op jit(solution)/shard_map/ppermute | solution.py:176
  11.7 10.7 %copy-start.7 = (bf16[2,256,512]{2,1,0:T(8,128)(2,1)S(1)}, bf16[2,256,512]{2,1,0:T(8,128)(2,1)}, u32[]{:S(2)}) copy-start(bf16[2,256,512]{2,1,0:T(8,128)(2,1)} %keys_ref.1) | copy-start | bytes 1572868
  11.7 10.7 %copy-start.8 = (bf16[2,256,512]{2,1,0:T(8,128)(2,1)S(1)}, bf16[2,256,512]{2,1,0:T(8,128)(2,1)}, u32[]{:S(2)}) copy-start(bf16[2,256,512]{2,1,0:T(8,128)(2,1)} %values_ref.1) | copy-start | bytes 1572868
  11.7 10.7 %copy-start.12 = (s32[2]{0:T(128)S(1)}, s32[2]{0:T(128)}, u32[]{:S(2)}) copy-start(s32[2]{0:T(128)} %lengths_ref.3) | copy-start | bytes 28
  22.4 25.8 %slice-start = ((s8[14680064]{0:T(1024)(128)(4,1)}), s8[4194304]{0:T(1024)(128)(4,1)S(1)}, s32[]{:S(2)}) async-start(s8[14680064]{0:T(1024)(128)(4,1)} %bitcast.3), calls=%async_computation.2 | async-start | bytes 8388608
  22.4 11.2 %copy-start.1 = (bf16[1024,2048]{1,0:T(8,128)(2,1)S(1)}, bf16[1024,2048]{1,0:T(8,128)(2,1)}, u32[]{:S(2)}) copy-start(bf16[1024,2048]{1,0:T(8,128)(2,1)} %w_ref.6) | copy-start | bytes 12582916
  22.4 24.4 %copy-start = (bf16[2048,3584]{1,0:T(8,128)(2,1)S(1)}, bf16[2048,3584]{1,0:T(8,128)(2,1)}, u32[]{:S(2)}) copy-start(bf16[2048,3584]{1,0:T(8,128)(2,1)} %w_ref.7) | copy-start | bytes 44040196
  22.5 24.4 %copy-start.2 = (f32[2048]{0:T(1024)S(1)}, f32[2048]{0:T(1024)}, u32[]{:S(2)}) copy-start(f32[2048]{0:T(1024)} %param.24) | copy-start | bytes 24580
  22.5 24.4 %copy-start.3 = (s32[32]{0:T(128)S(1)}, s32[32]{0:T(128)}, u32[]{:S(2)}) copy-start(s32[32]{0:T(128)} %served_ref.1) | copy-start | bytes 388
  22.5 25.7 %slice-start.1 = ((s8[14680064]{0:T(1024)(128)(4,1)}), s8[4194304]{0:T(1024)(128)(4,1)S(1)}, s32[]{:S(2)}) async-start(s8[14680064]{0:T(1024)(128)(4,1)} %bitcast.3), calls=%async_computation.3 | async-start | bytes 8388608
  22.5 25.7 %slice-start.2 = ((s8[14680064]{0:T(1024)(128)(4,1)}), s8[4194304]{0:T(1024)(128)(4,1)S(1)}, s32[]{:S(2)}) async-start(s8[14680064]{0:T(1024)(128)(4,1)} %bitcast.3), calls=%async_computation.4 | async-start | bytes 8388608
  22.5 25.7 %slice-start.3 = ((s8[14680064]{0:T(1024)(128)(4,1)}), s8[2097152]{0:T(1024)(128)(4,1)S(1)}, s32[]{:S(2)}) async-start(s8[14680064]{0:T(1024)(128)(4,1)} %bitcast.3), calls=%async_computation.5 | async-start | bytes 4194304
  34.4 4.8 %collective-permute-start.3 = (bf16[16,2048]{1,0:T(8,128)(2,1)S(1)}, bf16[16,2048]{1,0:T(8,128)(2,1)S(1)}, u32[]{:S(2)}, u32[]{:S(2)}) collective-permute-start(bf16[16,2048]{1,0:T(8,128)(2,1)S(1)} %get-tuple-element.23.keep_ref), channel_id=1, source_target_pairs={{0,1},{1,0},{2,3},{3,2},{4,5},{5,4},{6,7},{7,6},{8,9},{9,8},{10,11... | collective-permute-start | bytes 196616 | tf_op jit(solution)/shard_map/ppermute | solution.py:176
  34.8 5.2 %collective-permute-start.5 = (bf16[16,2048]{1,0:T(8,128)(2,1)S(1)}, bf16[16,2048]{1,0:T(8,128)(2,1)S(1)}, u32[]{:S(2)}, u32[]{:S(2)}) collective-permute-start(bf16[16,2048]{1,0:T(8,128)(2,1)S(1)} %get-tuple-element.24.keep_ref), channel_id=1, source_target_pairs={{0,1},{1,0},{2,3},{3,2},{4,5},{5,4},{6,7},{7,6},{8,9},{9,8},{10,11... | collective-permute-start | bytes 196616 | tf_op jit(solution)/shard_map/ppermute | solution.py:176
  39.3 6.8 %collective-permute-start.4 = (bf16[16,2048]{1,0:T(8,128)(2,1)S(1)}, bf16[16,2048]{1,0:T(8,128)(2,1)S(1)}, u32[]{:S(2)}, u32[]{:S(2)}) collective-permute-start(bf16[16,2048]{1,0:T(8,128)(2,1)S(1)} %shard_map.140.refs_2_), channel_id=1, source_target_pairs={{0,2},{1,3},{2,0},{3,1},{4,6},{5,7},{6,4},{7,5},{8,10},{9,11},{10,... | collective-permute-start | bytes 196616 | tf_op jit(solution)/shard_map/ppermute | solution.py:176
  40.0 6.8 %collective-permute-start.6 = (bf16[16,2048]{1,0:T(8,128)(2,1)S(1)}, bf16[16,2048]{1,0:T(8,128)(2,1)S(1)}, u32[]{:S(2)}, u32[]{:S(2)}) collective-permute-start(bf16[16,2048]{1,0:T(8,128)(2,1)S(1)} %shard_map.141.refs_4_), channel_id=1, source_target_pairs={{0,2},{1,3},{2,0},{3,1},{4,6},{5,7},{6,4},{7,5},{8,10},{9,11},{10,... | collective-permute-start | bytes 196616 | tf_op jit(solution)/shard_map/ppermute | solution.py:176
  48.1 3.4 %collective-permute-start.7 = (bf16[32,1920]{1,0:T(8,128)(2,1)S(1)}, bf16[32,1920]{1,0:T(8,128)(2,1)S(1)}, u32[]{:S(2)}, u32[]{:S(2)}) collective-permute-start(bf16[32,1920]{1,0:T(8,128)(2,1)S(1)} %get-tuple-element.28), channel_id=1, source_target_pairs={{0,4},{4,0},{8,12},{12,8},{1,5},{5,1},{9,13},{13,9},{2,6},{6,2},{1... | collective-permute-start | bytes 368648 | tf_op jit(solution)/shard_map/ppermute | solution.py:176
  49.6 10.1 %slice-start.4 = ((s8[14680064]{0:T(1024)(128)(4,1)}), s8[4194304]{0:T(1024)(128)(4,1)S(1)}, s32[]{:S(2)}) async-start(s8[14680064]{0:T(1024)(128)(4,1)} %bitcast.5), calls=%async_computation.6 | async-start | bytes 8388608
  49.6 4.0 %collective-permute-start.9 = (bf16[32,1792]{1,0:T(8,128)(2,1)S(1)}, bf16[32,1792]{1,0:T(8,128)(2,1)S(1)}, u32[]{:S(2)}, u32[]{:S(2)}) collective-permute-start(bf16[32,1792]{1,0:T(8,128)(2,1)S(1)} %shard_map.146), channel_id=1, source_target_pairs={{0,4},{4,0},{8,12},{12,8},{1,5},{5,1},{9,13},{13,9},{2,6},{6,2},{1... | collective-permute-start | bytes 344072 | tf_op jit(solution)/shard_map/ppermute | solution.py:176
  51.6 7.8 %collective-permute-start.8 = (bf16[32,1920]{1,0:T(8,128)(2,1)S(1)}, bf16[32,1920]{1,0:T(8,128)(2,1)S(1)}, u32[]{:S(2)}, u32[]{:S(2)}) collective-permute-start(bf16[32,1920]{1,0:T(8,128)(2,1)S(1)} %shard_map.144.gate_ref), channel_id=1, source_target_pairs={{0,8},{4,12},{8,0},{12,4},{1,9},{5,13},{9,1},{13,5},{2,10},{6,14},... | collective-permute-start | bytes 368648 | tf_op jit(solution)/shard_map/ppermute | solution.py:176
  53.7 5.7 %collective-permute-start.10 = (bf16[32,1792]{1,0:T(8,128)(2,1)S(1)}, bf16[32,1792]{1,0:T(8,128)(2,1)S(1)}, u32[]{:S(2)}, u32[]{:S(2)}) collective-permute-start(bf16[32,1792]{1,0:T(8,128)(2,1)S(1)} %shard_map.147.up_ref), channel_id=1, source_target_pairs={{0,8},{4,12},{8,0},{12,4},{1,9},{5,13},{9,1},{13,5},{2,10},{6,14},... | collective-permute-start | bytes 344072 | tf_op jit(solution)/shard_map/ppermute | solution.py:176
  59.6 1.5 %collective-permute-start.11 = (bf16[32,1792]{1,0:T(8,128)(2,1)S(1)}, bf16[32,1792]{1,0:T(8,128)(2,1)S(1)}, u32[]{:S(2)}, u32[]{:S(2)}) collective-permute-start(bf16[32,1792]{1,0:T(8,128)(2,1)S(1)} %shard_map.148.own_ref), channel_id=1, source_target_pairs={{0,4},{4,0},{8,12},{12,8},{1,5},{5,1},{9,13},{13,9},{2,6},{6,2},{1... | collective-permute-start | bytes 344072 | tf_op jit(solution)/shard_map/ppermute | solution.py:176
  62.5 4.5 %collective-permute-start.12 = (bf16[8,2048]{1,0:T(8,128)(2,1)S(1)}, bf16[8,2048]{1,0:T(8,128)(2,1)S(1)}, u32[]{:S(2)}, u32[]{:S(2)}) collective-permute-start(bf16[8,2048]{1,0:T(8,128)(2,1)S(1)} %get-tuple-element.30), channel_id=1, source_target_pairs={{0,1},{1,0},{2,3},{3,2},{4,5},{5,4},{6,7},{7,6},{8,9},{9,8},{10,11... | collective-permute-start | bytes 98312 | tf_op jit(solution)/shard_map/ppermute | solution.py:176
  62.6 5.1 %collective-permute-start.13 = (bf16[8,2048]{1,0:T(8,128)(2,1)S(1)}, bf16[8,2048]{1,0:T(8,128)(2,1)S(1)}, u32[]{:S(2)}, u32[]{:S(2)}) collective-permute-start(bf16[8,2048]{1,0:T(8,128)(2,1)S(1)} %get-tuple-element.31), channel_id=1, source_target_pairs={{0,2},{1,3},{2,0},{3,1},{4,6},{5,7},{6,4},{7,5},{8,10},{9,11},{10,... | collective-permute-start | bytes 98312 | tf_op jit(solution)/shard_map/ppermute | solution.py:176
  63.7 5.7 %collective-permute-start.14 = (bf16[8,2048]{1,0:T(8,128)(2,1)S(1)}, bf16[8,2048]{1,0:T(8,128)(2,1)S(1)}, u32[]{:S(2)}, u32[]{:S(2)}) collective-permute-start(bf16[8,2048]{1,0:T(8,128)(2,1)S(1)} %get-tuple-element.32), channel_id=1, source_target_pairs={{0,3},{1,2},{2,1},{3,0},{4,7},{5,6},{6,5},{7,4},{8,11},{9,10},{10,... | collective-permute-start | bytes 98312 | tf_op jit(solution)/shard_map/ppermute | solution.py:176
  (4 other events, 26.9 us)

commit v4 on v3

--- a/solution.py
+++ b/solution.py
@@ -1,3 +1,4 @@
+import functools
 import math
 
 import jax
@@ -155,8 +156,9 @@
 
 LANES = 128
 MIB = 2**20
-COVER = (100, 100, 100, 1, 1, 1, 1, 1, 1, 1)
+COVER = (100, 100, 100, 1, 10, 10, 10, 1, 1, 1)
 CHUNK = 512
+FIRST_PART = 57
 
 
 def exchange_fits(residual, w_query, w_key, w_gate):
@@ -167,7 +169,8 @@
         and residual.shape[0] % 8 == 0
         and w_query.shape[1] == GROUP * LANES
         and w_key.shape[1] == LANES
-        and w_gate.shape[1] % (2 * LANES) == 0
+        and w_gate.shape[1] % (4 * LANES) == 0
+        and w_gate.shape[1] >= 8 * LANES
     )
 
 
@@ -351,8 +354,8 @@
     )
 
 
-def gate_send_kernel(*refs):
-    served_ref, stream_ref, *term_refs, gain_ref, w_ref = refs[:-5]
+def middle_kernel(*refs):
+    served_ref, stream_ref, *term_refs, gain_ref, wg_ref, wu_ref = refs[:-5]
     scaled_ref, tail_ref, send_ref, middle_ref, rows_ref = refs[-5:]
     count = stream_ref.shape[0]
     row = lax.broadcasted_iota(jnp.int32, (count, count), 0)
@@ -375,36 +378,34 @@
     start = pl.multiple_of(lax.axis_index("tp") * own, own)
     middle_ref[...] = rows_ref[pl.ds(start, own), :].astype(jnp.bfloat16)
     squares = jnp.sum(rows * rows, axis=1, keepdims=True)
-    scaled = (rows * gain_ref[...]).astype(jnp.bfloat16)
-    scaled_ref[...] = scaled
+    scaled_ref[...] = (rows * gain_ref[...]).astype(jnp.bfloat16)
     half = lax.rem(lax.axis_index("role"), 2)
-    one_half(scaled, w_ref, send_ref, 1 - half)
+    size = (send_ref.shape[1] - LANES) // 2
+    piece_dots(scaled_ref, wg_ref, wu_ref, send_ref, 1 - half, 0, size)
     tail = split_three(squares)
-    send_ref[:, w_ref.shape[1] // 2 :] = tail
+    send_ref[:, 2 * size :] = tail
     tail_ref[...] = tail.astype(jnp.float32)
 
 
-def send_kernel(scaled_ref, w_ref, send_ref):
+def piece_kernel(theirs, begin, size, scaled_ref, wg_ref, wu_ref, *refs):
     half = lax.rem(lax.axis_index("role"), 2)
-    one_half(scaled_ref[...], w_ref, send_ref, 1 - half)
-
-
-def keep_kernel(scaled_ref, w_ref, keep_ref):
-    half = lax.rem(lax.axis_index("role"), 2)
-    one_half(scaled_ref[...], w_ref, keep_ref, half)
-
-
-def one_half(scaled, w_ref, out_ref, side):
-    width = w_ref.shape[1] // 2
-    for at in range(0, width, CHUNK):
-        size = min(CHUNK, width - at)
-        start = pl.multiple_of(side * width + at, LANES)
-        out_ref[:, at : at + size] = jnp.dot(
-            scaled, w_ref[:, pl.ds(start, size)], preferred_element_type=jnp.float32
-        ).astype(out_ref.dtype)
-
-
-def pair_gate_kernel(keep_ref, tail_ref, got_ref, out_ref):
+    side = 1 - half if theirs else half
+    piece_dots(scaled_ref, wg_ref, wu_ref, refs[-1], side, begin, size)
+
+
+def piece_dots(scaled_ref, wg_ref, wu_ref, out_ref, side, begin, size):
+    scaled = scaled_ref[...]
+    first = side * (wg_ref.shape[1] // 2) + begin
+    for w_ref, base in ((wg_ref, 0), (wu_ref, size)):
+        for at in range(0, size, CHUNK):
+            step = min(CHUNK, size - at)
+            start = pl.multiple_of(first + at, LANES)
+            out_ref[:, base + at : base + at + step] = jnp.dot(
+                scaled, w_ref[:, pl.ds(start, step)], preferred_element_type=jnp.float32
+            ).astype(out_ref.dtype)
+
+
+def pair_tail_kernel(keep_ref, tail_ref, got_ref, out_ref):
     wide = keep_ref.shape[1]
     out_ref[:, :wide] = (keep_ref[...] + got_ref[:, :wide].astype(jnp.float32)).astype(
         jnp.bfloat16
@@ -416,49 +417,70 @@
 
 
 def pair_kernel(keep_ref, got_ref, out_ref):
-    out_ref[...] = (keep_ref[...].astype(jnp.float32) + got_ref[...].astype(jnp.float32)).astype(jnp.bfloat16)
-
-
-def hidden_kernel(gate_ref, gate_got_ref, up_ref, up_got_ref, out_ref):
-    width = out_ref.shape[1]
+    out_ref[...] = (
+        keep_ref[...].astype(jnp.float32) + got_ref[...].astype(jnp.float32)
+    ).astype(jnp.bfloat16)
+
+
+def first_hidden_kernel(own_ref, got_ref, hidden_ref, inverse_ref):
+    wide = 2 * hidden_ref.shape[1]
     squares = jnp.sum(
-        gate_ref[:, width:].astype(jnp.float32) + gate_got_ref[:, width:].astype(jnp.float32),
+        own_ref[:, wide:].astype(jnp.float32) + got_ref[:, wide:].astype(jnp.float32),
         axis=1,
         keepdims=True,
     )
     inverse = lax.rsqrt(squares / D + epsilon)
-    gate = gate_ref[:, :width].astype(jnp.float32) + gate_got_ref[:, :width].astype(jnp.float32)
-    up = up_ref[...].astype(jnp.float32) + up_got_ref[...].astype(jnp.float32)
-    gate, up = gate * inverse, up * inverse
-    out_ref[...] = (gate / (1.0 + jnp.exp(-gate)) * up).astype(jnp.bfloat16)
-
-
-def down_own_kernel(own_ref, w_ref, rows_ref):
+    inverse_ref[...] = jnp.broadcast_to(inverse, inverse_ref.shape)
+    gated(own_ref, got_ref, inverse, hidden_ref)
+
+
+def hidden_kernel(own_ref, got_ref, inverse_ref, _, hidden_ref):
+    gated(own_ref, got_ref, inverse_ref[:, :1], hidden_ref)
+
+
+def gated(own_ref, got_ref, inverse, hidden_ref):
+    size = hidden_ref.shape[1]
+    total = own_ref[:, : 2 * size].astype(jnp.float32) + got_ref[:, : 2 * size].astype(jnp.float32)
+    total = total * inverse
+    gate, up = total[:, :size], total[:, size:]
+    hidden_ref[...] = (gate / (1.0 + jnp.exp(-gate)) * up).astype(jnp.bfloat16)
+
+
+def down_dots(theirs, begin, hidden_ref, w_ref, part):
     half = lax.rem(lax.axis_index("role"), 2)
-    width = own_ref.shape[1]
-    mine = pl.ds(pl.multiple_of(half * width, LANES), width)
-    for at in range(0, w_ref.shape[1], CHUNK):
-        part = slice(at, min(at + CHUNK, w_ref.shape[1]))
-        rows_ref[:, part] = jnp.dot(
-            own_ref[...], w_ref[mine, part], preferred_element_type=jnp.float32
-        )
-
-
-def down_kernel(other_ref, w_ref, rows_ref, *refs):
-    *out_refs, total_ref = refs
-    half = lax.rem(lax.axis_index("role"), 2)
+    side = 1 - half if theirs else half
+    start = pl.multiple_of(side * (w_ref.shape[0] // 2) + begin, LANES)
+    return jnp.dot(
+        hidden_ref[...],
+        w_ref[pl.ds(start, hidden_ref.shape[1]), part],
+        preferred_element_type=jnp.float32,
+    )
+
+
+def chunks(width):
+    return [slice(at, min(at + CHUNK, width)) for at in range(0, width, CHUNK)]
+
+
+def down_kernel(theirs, begin, hidden_ref, w_ref, *refs):
+    *before_refs, rows_ref = refs
+    for part in chunks(w_ref.shape[1]):
+        rows = down_dots(theirs, begin, hidden_ref, w_ref, part)
+        for before_ref in before_refs:
+            rows = rows + before_ref[:, part]
+        rows_ref[:, part] = rows
+
+
+def last_down_kernel(theirs, begin, hidden_ref, w_ref, before_ref, *refs):
+    *out_refs, rows_ref = refs
     place = lax.axis_index("tp")
-    width = other_ref.shape[1]
-    theirs = pl.ds(pl.multiple_of((1 - half) * width, LANES), width)
     own = out_refs[0].shape[0]
-    for at in range(0, w_ref.shape[1], CHUNK):
-        part = slice(at, min(at + CHUNK, w_ref.shape[1]))
-        total_ref[:, part] = rows_ref[:, part] + jnp.dot(
-            other_ref[...], w_ref[theirs, part], preferred_element_type=jnp.float32
+    for part in chunks(w_ref.shape[1]):
+        rows_ref[:, part] = before_ref[:, part] + down_dots(
+            theirs, begin, hidden_ref, w_ref, part
         )
     for k, out_ref in enumerate(out_refs):
         start = pl.multiple_of((place ^ k) * own, own)
-        out_ref[...] = total_ref[pl.ds(start, own), :].astype(jnp.bfloat16)
+        out_ref[...] = rows_ref[pl.ds(start, own), :].astype(jnp.bfloat16)
 
 
 def local_exchange(
@@ -545,48 +567,81 @@
         (paired,) = call(pair_kernel, [piece], [value, got])
         terms += [paired, swap(paired, "tp", 2)]
     width = w_gate.shape[1] // 2
-    wide = width + LANES
-    half_f32 = jax.ShapeDtypeStruct((rows, width), jnp.float32)
-    half_bf16 = jax.ShapeDtypeStruct((rows, width), jnp.bfloat16)
-    wide_bf16 = jax.ShapeDtypeStruct((rows, wide), jnp.bfloat16)
+    first = -(-width * FIRST_PART // (100 * 2 * LANES)) * 2 * LANES
+    sizes = (first, width - first)
     w_gate, w_up, w_down = in_vmem(w_gate), in_vmem(w_up), in_vmem(w_down)
-    scaled, tail, gate_send, middle = call(
-        gate_send_kernel,
+    rows_f32 = jax.ShapeDtypeStruct((rows, features), jnp.float32)
+    row_scratch = pltpu.VMEM((rows, features), jnp.float32)
+
+    def wide(size, dtype, more=0):
+        return jax.ShapeDtypeStruct((rows, 2 * size + more), dtype)
+
+    def half_of(piece):
+        return jax.ShapeDtypeStruct((rows, sizes[piece]), jnp.bfloat16)
+
+    scaled, tail, send, middle = call(
+        middle_kernel,
         [
             jax.ShapeDtypeStruct((rows, features), jnp.bfloat16),
             jax.ShapeDtypeStruct((rows, LANES), jnp.float32),
-            wide_bf16,
+            wide(sizes[0], jnp.bfloat16, LANES),
             block,
         ],
-        [served[None, :], stream, *terms, ffn_gain[None, :], w_gate],
-        scratch=[pltpu.VMEM((rows, features), jnp.float32)],
+        [served[None, :], stream, *terms, ffn_gain[None, :], w_gate, w_up],
+        scratch=[row_scratch],
         cost=COVER[4],
     )
-    gate_got = swap(gate_send, "role", 1)
-    (gate,) = call(keep_kernel, [half_f32], [scaled, w_gate], cost=COVER[5])
-    (gate,) = call(pair_gate_kernel, [wide_bf16], [gate, tail, gate_got])
-    (up_send,) = call(send_kernel, [half_bf16], [scaled, w_up], cost=COVER[6])
-    up_got = swap(up_send, "role", 1)
-    (up,) = call(keep_kernel, [half_f32], [scaled, w_up], cost=COVER[7])
-    (up,) = call(pair_kernel, [half_bf16], [up, up_got])
-    gate_got, up_got = swap(gate, "role", 2), swap(up, "role", 2)
-    (hidden,) = call(
-        hidden_kernel,
-        [half_bf16],
-        [gate, gate_got, up, up_got],
+    got = swap(send, "role", 1)
+    (keep,) = call(
+        functools.partial(piece_kernel, False, 0, sizes[0]),
+        [wide(sizes[0], jnp.float32)],
+        [scaled, w_gate, w_up],
+        cost=COVER[5],
+    )
+    (chip_0,) = call(
+        pair_tail_kernel, [wide(sizes[0], jnp.bfloat16, LANES)], [keep, tail, got]
+    )
+    far_0 = swap(chip_0, "role", 2)
+    (send,) = call(
+        functools.partial(piece_kernel, True, sizes[0], sizes[1]),
+        [wide(sizes[1], jnp.bfloat16)],
+        [scaled, w_gate, w_up, chip_0],
+        cost=COVER[6],
+    )
+    got = swap(send, "role", 1)
+    (keep,) = call(
+        functools.partial(piece_kernel, False, sizes[0], sizes[1]),
+        [wide(sizes[1], jnp.float32)],
+        [scaled, w_gate, w_up],
+        cost=COVER[7],
+    )
+    (chip_1,) = call(pair_kernel, [wide(sizes[1], jnp.bfloat16)], [keep, got])
+    far_1 = swap(chip_1, "role", 2)
+    hidden, inverse = call(
+        first_hidden_kernel,
+        [half_of(0), jax.ShapeDtypeStruct((rows, LANES), jnp.float32)],
+        [chip_0, far_0],
     )
     other = swap(hidden, "role", 1)
     (down,) = call(
-        down_own_kernel,
-        [jax.ShapeDtypeStruct((rows, features), jnp.float32)],
-        [hidden, w_down],
-        cost=COVER[8],
+        functools.partial(down_kernel, False, 0), [rows_f32], [hidden, w_down], cost=COVER[8]
+    )
+    (down,) = call(
+        functools.partial(down_kernel, True, 0), [rows_f32], [other, w_down, down], cost=COVER[8]
+    )
+    (hidden,) = call(hidden_kernel, [half_of(1)], [chip_1, far_1, inverse, down])
+    other = swap(hidden, "role", 1)
+    (down,) = call(
+        functools.partial(down_kernel, False, sizes[0]),
+        [rows_f32],
+        [hidden, w_down, down],
+        cost=COVER[9],
     )
     terms = call(
-        down_kernel,
+        functools.partial(last_down_kernel, True, sizes[0]),
         [block] * tp_count,
         [other, w_down, down],
-        scratch=[pltpu.VMEM((rows, features), jnp.float32)],
+        scratch=[row_scratch],
         cost=COVER[9],
     )
     terms = [terms[0]] + [swap(terms[k], "tp", k) for k in range(1, tp_count)]

time: 70.9 us -> 69.2 us (0.976)
  waiting for transfers between devices: 18.6 us -> 16.7 us
    ppermute x15 -> x16, waiting for transfers between devices: 18.6 us -> 16.7 us  [swap(): return lax.ppermute(value, axis, [(i, i ^ distance) for i in range(count)])]
    pallas_call x16 -> x19, Pallas kernels: 13.5 us -> 13.9 us  [call(): pl.pallas_call(kernel, out_shape=outs, in_specs=specs, out_specs=[pl.Bloc...]
    ppermute x15 -> x16, starting transfers between devices: 18.1 us -> 18 us  [swap(): return lax.ppermute(value, axis, [(i, i ^ distance) for i in range(count)])]
  transfers between devices with their start and end apart: 15 -> 16, of which waited for: 8 -> 10; matrix products, arithmetic and copies ran while one was open for 0% -> 0% of each run, Pallas kernels for 9% -> 10%
where the time goes in v4:
time: 69.2 us; the launch traced here: 68.9 us
  blocking collectives  19.4 us (28%)
  starting transfers between devices  18 us (26%)
  waiting for transfers between devices  16.7 us (24%)
  Pallas kernels  13.9 us (20%)
  local copies, waits for them, and re-layouts  0.74 us (1%)
    ppermute x16, starting transfers between devices, swap(): return lax.ppermute(value, axis, [(i, i ^ distance) for i in range(count)])  18 us
    ppermute x16, waiting for transfers between devices, swap(): return lax.ppermute(value, axis, [(i, i ^ distance) for i in range(count)])  16.7 us
    pallas_call x19, Pallas kernels, call(): pl.pallas_call(kernel, out_shape=outs, in_specs=specs, out_specs=[pl.Bloc...  13.9 us
    all_to_all x1, blocking collectives, local_exchange(): heads = lax.all_to_all(heads, ('role', 'tp'), 0, 0)  9.72 us
    all_to_all x1, blocking collectives, local_exchange(): parts = lax.all_to_all(sums, ('role', 'tp'), 0, 0)  9.65 us
  transfers between devices with their start and end apart: 16, of which 10 were waited for; matrix products, arithmetic and copies ran while one was open for 0% of the time, Pallas kernels for 10%

profile of v4, /device:TPU:0, one launch (start us, length us, event | category | flops | bytes accessed | tf_op | source)
XLA Modules:
  0.0 68.9 jit_solution(6621722409039364247)
XLA Ops:
  0.0 3.1 %collective-permute-start = (bf16[8,2048]{1,0:T(8,128)(2,1)}, bf16[8,2048]{1,0:T(8,128)(2,1)S(1)}, u32[]{:S(2)}, u32[]{:S(2)}) collective-permute-start(bf16[8,2048]{1,0:T(8,128)(2,1)} %refs_0_.1), channel_id=1, source_target_pairs={{0,1},{1,0},{2,3},{3,2},{4,5},{5,4},{6,7},{7,6},{8,9},{9,8},{10,11... | collective-permute-start | bytes 98312 | tf_op jit(solution)/shard_map/ppermute | solution.py:179
  3.1 2.6 %collective-permute-start.1 = (bf16[8,2048]{1,0:T(8,128)(2,1)}, bf16[8,2048]{1,0:T(8,128)(2,1)S(1)}, u32[]{:S(2)}, u32[]{:S(2)}) collective-permute-start(bf16[8,2048]{1,0:T(8,128)(2,1)} %refs_0_.1), channel_id=1, source_target_pairs={{0,2},{1,3},{2,0},{3,1},{4,6},{5,7},{6,4},{7,5},{8,10},{9,11},{10,... | collective-permute-start | bytes 98312 | tf_op jit(solution)/shard_map/ppermute | solution.py:179
  5.7 0.7 copy-done.12
  7.0 1.8 %collective-permute-done.1.refs_2_ = bf16[8,2048]{1,0:T(8,128)(2,1)S(1)} collective-permute-done((bf16[8,2048]{1,0:T(8,128)(2,1)}, bf16[8,2048]{1,0:T(8,128)(2,1)S(1)}, u32[]{:S(2)}, u32[]{:S(2)}) %collective-permute-start.1) | collective-permute-done | bytes 32800 | tf_op jit(solution)/shard_map/ppermute | solution.py:179
  8.8 2.9 %collective-permute-done.2.refs_3_ = bf16[8,2048]{1,0:T(8,128)(2,1)S(1)} collective-permute-done((bf16[8,2048]{1,0:T(8,128)(2,1)}, bf16[8,2048]{1,0:T(8,128)(2,1)S(1)}, u32[]{:S(2)}, u32[]{:S(2)}) %collective-permute-start.2) | collective-permute-done | bytes 32800 | tf_op jit(solution)/shard_map/ppermute | solution.py:179
  11.7 1.0 %shard_map.137 = (bf16[16,24,128]{2,1,0:T(8,128)(2,1)S(1)}, bf16[32,2048]{1,0:T(8,128)(2,1)S(1)}) custom-call(f32[2,128]{1,0:T(2,128)S(1)} %get-tuple-element.21._.cosine_ref, bf16[8,2048]{1,0:T(8,128)(2,1)S(1)} %copy-done.9, bf16[8,2048]{1,0:T(8,128)(2,1)S(1)} %collective-permute-done.refs_1_, bf16[8,2048]{1,0:T(8,128)(2,1)S(1)} %collective-permute-done.1.refs_2_, ...), custom_call_target="tpu_custom_call" | custom-call | flops 99999997952 | bytes 1048576 | tf_op jit(solution)/shard_map/pallas_call | solution.py:189
  12.8 9.7 %all_to_all.10.got_ref = bf16[16,24,128]{2,1,0:T(8,128)(2,1)S(1)} all-to-all(bf16[16,24,128]{2,1,0:T(8,128)(2,1)S(1)} %get-tuple-element.23), channel_id=1, replica_groups=mesh['groups'=2,'role'=4,'tp'=4] {'role','tp'}, dimensions={0} | all-to-all | bytes 196608 | tf_op jit(solution)/shard_map/all_to_all | solution.py:546
  22.5 1.4 %shard_map.138 = bf16[16,16,128]{2,1,0:T(8,128)(2,1)S(1)} custom-call(s32[2]{0:T(128)S(1)} %copy-done.13, bf16[16,24,128]{2,1,0:T(8,128)(2,1)S(1)} %all_to_all.10.got_ref, f32[2,128]{1,0:T(2,128)S(1)} %get-tuple-element.21._.cosine_ref, f32[2,128]{1,0:T(2,128)S(1)} %get-tuple-element.24.sine_ref, bf16[2,256,512]{2,1,0:T(8,128)(2,1)S(1)} %copy-done.7, ...), custom_call_target="tpu_custom_call" | custom-call | flops 99999997952 | bytes 1048576 | tf_op jit(solution)/shard_map/pallas_call | solution.py:189
  23.9 9.7 %all_to_all.11.heads_ref = bf16[16,16,128]{2,1,0:T(8,128)(2,1)S(1)} all-to-all(bf16[16,16,128]{2,1,0:T(8,128)(2,1)S(1)} %shard_map.138), channel_id=1, replica_groups=mesh['groups'=2,'role'=4,'tp'=4] {'role','tp'}, dimensions={0} | all-to-all | bytes 131072 | tf_op jit(solution)/shard_map/all_to_all | solution.py:554
  33.6 0.8 %shard_map.139 = (bf16[16,2048]{1,0:T(8,128)(2,1)S(1)}, bf16[16,2048]{1,0:T(8,128)(2,1)S(1)}) custom-call(bf16[16,16,128]{2,1,0:T(8,128)(2,1)S(1)} %all_to_all.11.heads_ref, bf16[1024,2048]{1,0:T(8,128)(2,1)S(1)} %copy-done.2), custom_call_target="tpu_custom_call" | custom-call | flops 1000000000 | bytes 1048576 | tf_op jit(solution)/shard_map/pallas_call | solution.py:189
  34.8 1.7 %collective-permute-start.3 = (bf16[16,2048]{1,0:T(8,128)(2,1)S(1)}, bf16[16,2048]{1,0:T(8,128)(2,1)S(1)}, u32[]{:S(2)}, u32[]{:S(2)}) collective-permute-start(bf16[16,2048]{1,0:T(8,128)(2,1)S(1)} %get-tuple-element.25.keep_ref), channel_id=1, source_target_pairs={{0,1},{1,0},{2,3},{3,2},{4,5},{5,4},{6,7},{7,6},{8,9},{9,8},{10,11... | collective-permute-start | bytes 196616 | tf_op jit(solution)/shard_map/ppermute | solution.py:179
  36.5 2.8 %collective-permute-done.5.got_ref = bf16[16,2048]{1,0:T(8,128)(2,1)S(1)} collective-permute-done((bf16[16,2048]{1,0:T(8,128)(2,1)S(1)}, bf16[16,2048]{1,0:T(8,128)(2,1)S(1)}, u32[]{:S(2)}, u32[]{:S(2)}) %collective-permute-start.5) | collective-permute-done | bytes 65568 | tf_op jit(solution)/shard_map/ppermute | solution.py:179
  39.3 0.7 collective-permute-start.6
  40.0 2.4 %collective-permute-start.4 = (bf16[16,2048]{1,0:T(8,128)(2,1)S(1)}, bf16[16,2048]{1,0:T(8,128)(2,1)S(1)}, u32[]{:S(2)}, u32[]{:S(2)}) collective-permute-start(bf16[16,2048]{1,0:T(8,128)(2,1)S(1)} %shard_map.140.refs_2_), channel_id=1, source_target_pairs={{0,2},{1,3},{2,0},{3,1},{4,6},{5,7},{6,4},{7,5},{8,10},{9,11},{10,... | collective-permute-start | bytes 196616 | tf_op jit(solution)/shard_map/ppermute | solution.py:179
  42.3 3.7 %collective-permute-done.6.refs_5_ = bf16[16,2048]{1,0:T(8,128)(2,1)S(1)} collective-permute-done((bf16[16,2048]{1,0:T(8,128)(2,1)S(1)}, bf16[16,2048]{1,0:T(8,128)(2,1)S(1)}, u32[]{:S(2)}, u32[]{:S(2)}) %collective-permute-start.6) | collective-permute-done | bytes 65568 | tf_op jit(solution)/shard_map/ppermute | solution.py:179
  46.1 0.7 %collective-permute-done.4.refs_3_ = bf16[16,2048]{1,0:T(8,128)(2,1)S(1)} collective-permute-done((bf16[16,2048]{1,0:T(8,128)(2,1)S(1)}, bf16[16,2048]{1,0:T(8,128)(2,1)S(1)}, u32[]{:S(2)}, u32[]{:S(2)}) %collective-permute-start.4) | collective-permute-done | bytes 65568 | tf_op jit(solution)/shard_map/ppermute | solution.py:179
  46.8 1.6 %shard_map.142 = (bf16[32,2048]{1,0:T(8,128)(2,1)S(1)}, f32[32,128]{1,0:T(8,128)S(1)}, bf16[32,2176]{1,0:T(8,128)(2,1)S(1)}, bf16[8,2048]{1,0:T(8,128)(2,1)S(1)}) custom-call(s32[1,32]{1,0:T(1,128)S(1)} %bitcast.5, bf16[32,2048]{1,0:T(8,128)(2,1)S(1)} %get-tuple-element.22.refs_1_, bf16[16,2048]{1,0:T(8,128)(2,1)S(1)} %shard_map.140.refs_2_, ...), custom_call_target="tpu_custom_call" | custom-call | flops 10000000000 | bytes 1048576 | tf_op jit(solution)/shard_map/pallas_call | solution.py:189
  48.5 1.5 %shard_map.144.keep_ref = f32[32,2048]{1,0:T(8,128)S(1)} custom-call(bf16[32,2048]{1,0:T(8,128)(2,1)S(1)} %get-tuple-element.28.scaled_ref, bf16[2048,3584]{1,0:T(8,128)(2,1)S(1)} %copy-done, bf16[2048,3584]{1,0:T(8,128)(2,1)S(1)} %copy-done.1), custom_call_target="tpu_custom_call" | custom-call | flops 10000000000 | bytes 1048576 | tf_op jit(solution)/shard_map/pallas_call | solution.py:189
  50.2 0.6 collective-permute-start.10
  50.8 1.2 %shard_map.146 = bf16[32,1536]{1,0:T(8,128)(2,1)S(1)} custom-call(bf16[32,2048]{1,0:T(8,128)(2,1)S(1)} %get-tuple-element.28.scaled_ref, bf16[2048,3584]{1,0:T(8,128)(2,1)S(1)} %copy-done, bf16[2048,3584]{1,0:T(8,128)(2,1)S(1)} %copy-done.1, bf16[32,2176]{1,0:T(8,128)(2,1)S(1)} %shard_map.145.refs_0_.own_ref), custom_call_target="tpu_custom_call" | custom-call | flops 10000000000 | bytes 1048576 | tf_op jit(solution)/shard_map/pallas_call | solution.py:189
  52.2 1.2 %shard_map.143.keep_ref = f32[32,1536]{1,0:T(8,128)S(1)} custom-call(bf16[32,2048]{1,0:T(8,128)(2,1)S(1)} %get-tuple-element.28.scaled_ref, bf16[2048,3584]{1,0:T(8,128)(2,1)S(1)} %copy-done, bf16[2048,3584]{1,0:T(8,128)(2,1)S(1)} %copy-done.1), custom_call_target="tpu_custom_call" | custom-call | flops 1000000000 | bytes 1048576 | tf_op jit(solution)/shard_map/pallas_call | solution.py:189
  53.4 1.5 %collective-permute-start.9 = (bf16[32,1536]{1,0:T(8,128)(2,1)S(1)}, bf16[32,1536]{1,0:T(8,128)(2,1)S(1)}, u32[]{:S(2)}, u32[]{:S(2)}) collective-permute-start(bf16[32,1536]{1,0:T(8,128)(2,1)S(1)} %shard_map.147.own_ref), channel_id=1, source_target_pairs={{0,8},{4,12},{8,0},{12,4},{1,9},{5,13},{9,1},{13,5},{2,10},{6,14},... | collective-permute-start | bytes 294920 | tf_op jit(solution)/shard_map/ppermute | solution.py:179
  55.0 1.3 %collective-permute-done.10.got_ref = bf16[32,2176]{1,0:T(8,128)(2,1)S(1)} collective-permute-done((bf16[32,2176]{1,0:T(8,128)(2,1)S(1)}, bf16[32,2176]{1,0:T(8,128)(2,1)S(1)}, u32[]{:S(2)}, u32[]{:S(2)}) %collective-permute-start.10) | collective-permute-done | bytes 139296 | tf_op jit(solution)/shard_map/ppermute | solution.py:179
  56.6 0.8 %shard_map.149.refs_0_ = f32[32,2048]{1,0:T(8,128)S(1)} custom-call(bf16[32,1024]{1,0:T(8,128)(2,1)S(1)} %get-tuple-element.32.hidden_ref, bf16[3584,2048]{1,0:T(8,128)(2,1)S(1)} %bitcast.4), custom_call_target="tpu_custom_call" | custom-call | flops 1000000000 | bytes 1048576 | tf_op jit(solution)/shard_map/pallas_call | solution.py:189
  57.8 0.8 %shard_map.150._.refs_0_ = f32[32,2048]{1,0:T(8,128)S(1)} custom-call(bf16[32,1024]{1,0:T(8,128)(2,1)S(1)} %collective-permute-done.11.hidden_ref, bf16[3584,2048]{1,0:T(8,128)(2,1)S(1)} %bitcast.4, f32[32,2048]{1,0:T(8,128)S(1)} %shard_map.149.refs_0_), custom_call_target="tpu_custom_call" | custom-call | flops 1000000000 | bytes 1048576 | tf_op jit(solution)/shard_map/pallas_call | solution.py:189
  58.9 0.6 shard_map.152.before_ref
  60.0 0.7 shard_map.153
  60.8 1.3 %collective-permute-start.14 = (bf16[8,2048]{1,0:T(8,128)(2,1)S(1)}, bf16[8,2048]{1,0:T(8,128)(2,1)S(1)}, u32[]{:S(2)}, u32[]{:S(2)}) collective-permute-start(bf16[8,2048]{1,0:T(8,128)(2,1)S(1)} %get-tuple-element.35), channel_id=1, source_target_pairs={{0,2},{1,3},{2,0},{3,1},{4,6},{5,7},{6,4},{7,5},{8,10},{9,11},{10,... | collective-permute-start | bytes 98312 | tf_op jit(solution)/shard_map/ppermute | solution.py:179
  62.1 3.1 %collective-permute-start.15 = (bf16[8,2048]{1,0:T(8,128)(2,1)S(1)}, bf16[8,2048]{1,0:T(8,128)(2,1)S(1)}, u32[]{:S(2)}, u32[]{:S(2)}) collective-permute-start(bf16[8,2048]{1,0:T(8,128)(2,1)S(1)} %get-tuple-element.36), channel_id=1, source_target_pairs={{0,3},{1,2},{2,1},{3,0},{4,7},{5,6},{6,5},{7,4},{8,11},{9,10},{10,... | collective-permute-start | bytes 98312 | tf_op jit(solution)/shard_map/ppermute | solution.py:179
  65.1 1.4 %collective-permute-done.14.refs_2_ = bf16[8,2048]{1,0:T(8,128)(2,1)S(1)} collective-permute-done((bf16[8,2048]{1,0:T(8,128)(2,1)S(1)}, bf16[8,2048]{1,0:T(8,128)(2,1)S(1)}, u32[]{:S(2)}, u32[]{:S(2)}) %collective-permute-start.14) | collective-permute-done | bytes 32800 | tf_op jit(solution)/shard_map/ppermute | solution.py:179
  66.5 1.2 %collective-permute-done.15.refs_3_ = bf16[8,2048]{1,0:T(8,128)(2,1)S(1)} collective-permute-done((bf16[8,2048]{1,0:T(8,128)(2,1)S(1)}, bf16[8,2048]{1,0:T(8,128)(2,1)S(1)}, u32[]{:S(2)}, u32[]{:S(2)}) %collective-permute-start.15) | collective-permute-done | bytes 32800 | tf_op jit(solution)/shard_map/ppermute | solution.py:179
  67.8 1.2 %shard_map.154 = bf16[8,2048]{1,0:T(8,128)(2,1)} custom-call(s32[32]{0:T(128)S(1)} %copy-done.3, bf16[8,2048]{1,0:T(8,128)(2,1)S(1)} %get-tuple-element.27.stream_ref, bf16[8,2048]{1,0:T(8,128)(2,1)S(1)} %get-tuple-element.33.refs_0_, bf16[8,2048]{1,0:T(8,128)(2,1)S(1)} %collective-permute-done.13.refs_1_, ...), custom_call_target="tpu_custom_call" | custom-call | bytes 1048576 | tf_op jit(solution)/shard_map/pallas_call | solution.py:189
  (58 shorter events, 2.9 us)
Async XLA Ops:
  0.0 11.7 %copy-start.9 = (bf16[8,2048]{1,0:T(8,128)(2,1)S(1)}, bf16[8,2048]{1,0:T(8,128)(2,1)}, u32[]{:S(2)}) copy-start(bf16[8,2048]{1,0:T(8,128)(2,1)} %refs_0_.1) | copy-start | bytes 98308
  0.0 11.7 %copy-start.10 = (f32[2048]{0:T(1024)S(1)}, f32[2048]{0:T(1024)}, u32[]{:S(2)}) copy-start(f32[2048]{0:T(1024)} %param.15) | copy-start | bytes 24580
  0.0 11.7 %copy-start.4 = (bf16[2048,1024]{1,0:T(8,128)(2,1)S(1)}, bf16[2048,1024]{1,0:T(8,128)(2,1)}, u32[]{:S(2)}) copy-start(bf16[2048,1024]{1,0:T(8,128)(2,1)} %refs_5_.1) | copy-start | bytes 12582916
  0.0 11.7 %copy-start.5 = (bf16[2048,128]{1,0:T(8,128)(2,1)S(1)}, bf16[2048,128]{1,0:T(8,128)(2,1)}, u32[]{:S(2)}) copy-start(bf16[2048,128]{1,0:T(8,128)(2,1)} %refs_6_.1) | copy-start | bytes 1572868
  0.0 11.7 %copy-start.6 = (bf16[2048,128]{1,0:T(8,128)(2,1)S(1)}, bf16[2048,128]{1,0:T(8,128)(2,1)}, u32[]{:S(2)}) copy-start(bf16[2048,128]{1,0:T(8,128)(2,1)} %refs_7_.2) | copy-start | bytes 1572868
  0.0 7.0 %collective-permute-start = (bf16[8,2048]{1,0:T(8,128)(2,1)}, bf16[8,2048]{1,0:T(8,128)(2,1)S(1)}, u32[]{:S(2)}, u32[]{:S(2)}) collective-permute-start(bf16[8,2048]{1,0:T(8,128)(2,1)} %refs_0_.1), channel_id=1, source_target_pairs={{0,1},{1,0},{2,3},{3,2},{4,5},{5,4},{6,7},{7,6},{8,9},{9,8},{10,11... | collective-permute-start | bytes 98312 | tf_op jit(solution)/shard_map/ppermute | solution.py:179
  3.1 5.6 %collective-permute-start.1 = (bf16[8,2048]{1,0:T(8,128)(2,1)}, bf16[8,2048]{1,0:T(8,128)(2,1)S(1)}, u32[]{:S(2)}, u32[]{:S(2)}) collective-permute-start(bf16[8,2048]{1,0:T(8,128)(2,1)} %refs_0_.1), channel_id=1, source_target_pairs={{0,2},{1,3},{2,0},{3,1},{4,6},{5,7},{6,4},{7,5},{8,10},{9,11},{10,... | collective-permute-start | bytes 98312 | tf_op jit(solution)/shard_map/ppermute | solution.py:179
  5.7 5.9 %collective-permute-start.2 = (bf16[8,2048]{1,0:T(8,128)(2,1)}, bf16[8,2048]{1,0:T(8,128)(2,1)S(1)}, u32[]{:S(2)}, u32[]{:S(2)}) collective-permute-start(bf16[8,2048]{1,0:T(8,128)(2,1)} %refs_0_.1), channel_id=1, source_target_pairs={{0,3},{1,2},{2,1},{3,0},{4,7},{5,6},{6,5},{7,4},{8,11},{9,10},{10,... | collective-permute-start | bytes 98312 | tf_op jit(solution)/shard_map/ppermute | solution.py:179
  11.7 10.7 %copy-start.7 = (bf16[2,256,512]{2,1,0:T(8,128)(2,1)S(1)}, bf16[2,256,512]{2,1,0:T(8,128)(2,1)}, u32[]{:S(2)}) copy-start(bf16[2,256,512]{2,1,0:T(8,128)(2,1)} %keys_ref.1) | copy-start | bytes 1572868
  11.7 10.7 %copy-start.8 = (bf16[2,256,512]{2,1,0:T(8,128)(2,1)S(1)}, bf16[2,256,512]{2,1,0:T(8,128)(2,1)}, u32[]{:S(2)}) copy-start(bf16[2,256,512]{2,1,0:T(8,128)(2,1)} %values_ref.1) | copy-start | bytes 1572868
  11.7 10.7 %copy-start.13 = (s32[2]{0:T(128)S(1)}, s32[2]{0:T(128)}, u32[]{:S(2)}) copy-start(s32[2]{0:T(128)} %lengths_ref.3) | copy-start | bytes 28
  22.4 11.2 %copy-start.2 = (bf16[1024,2048]{1,0:T(8,128)(2,1)S(1)}, bf16[1024,2048]{1,0:T(8,128)(2,1)}, u32[]{:S(2)}) copy-start(bf16[1024,2048]{1,0:T(8,128)(2,1)} %w_ref.5) | copy-start | bytes 12582916
  22.4 24.4 %copy-start = (bf16[2048,3584]{1,0:T(8,128)(2,1)S(1)}, bf16[2048,3584]{1,0:T(8,128)(2,1)}, u32[]{:S(2)}) copy-start(bf16[2048,3584]{1,0:T(8,128)(2,1)} %wg_ref.5) | copy-start | bytes 44040196
  22.5 24.3 %copy-start.1 = (bf16[2048,3584]{1,0:T(8,128)(2,1)S(1)}, bf16[2048,3584]{1,0:T(8,128)(2,1)}, u32[]{:S(2)}) copy-start(bf16[2048,3584]{1,0:T(8,128)(2,1)} %wu_ref.5) | copy-start | bytes 44040196
  22.5 24.3 %copy-start.3 = (s32[32]{0:T(128)S(1)}, s32[32]{0:T(128)}, u32[]{:S(2)}) copy-start(s32[32]{0:T(128)} %served_ref.1) | copy-start | bytes 388
  22.5 24.3 %copy-start.11 = (f32[2048]{0:T(1024)S(1)}, f32[2048]{0:T(1024)}, u32[]{:S(2)}) copy-start(f32[2048]{0:T(1024)} %param.24) | copy-start | bytes 24580
  34.4 4.8 %collective-permute-start.5 = (bf16[16,2048]{1,0:T(8,128)(2,1)S(1)}, bf16[16,2048]{1,0:T(8,128)(2,1)S(1)}, u32[]{:S(2)}, u32[]{:S(2)}) collective-permute-start(bf16[16,2048]{1,0:T(8,128)(2,1)S(1)} %get-tuple-element.26.keep_ref), channel_id=1, source_target_pairs={{0,1},{1,0},{2,3},{3,2},{4,5},{5,4},{6,7},{7,6},{8,9},{9,8},{10,11... | collective-permute-start | bytes 196616 | tf_op jit(solution)/shard_map/ppermute | solution.py:179
  34.8 5.2 %collective-permute-start.3 = (bf16[16,2048]{1,0:T(8,128)(2,1)S(1)}, bf16[16,2048]{1,0:T(8,128)(2,1)S(1)}, u32[]{:S(2)}, u32[]{:S(2)}) collective-permute-start(bf16[16,2048]{1,0:T(8,128)(2,1)S(1)} %get-tuple-element.25.keep_ref), channel_id=1, source_target_pairs={{0,1},{1,0},{2,3},{3,2},{4,5},{5,4},{6,7},{7,6},{8,9},{9,8},{10,11... | collective-permute-start | bytes 196616 | tf_op jit(solution)/shard_map/ppermute | solution.py:179
  39.3 6.8 %collective-permute-start.6 = (bf16[16,2048]{1,0:T(8,128)(2,1)S(1)}, bf16[16,2048]{1,0:T(8,128)(2,1)S(1)}, u32[]{:S(2)}, u32[]{:S(2)}) collective-permute-start(bf16[16,2048]{1,0:T(8,128)(2,1)S(1)} %shard_map.141.refs_4_), channel_id=1, source_target_pairs={{0,2},{1,3},{2,0},{3,1},{4,6},{5,7},{6,4},{7,5},{8,10},{9,11},{10,... | collective-permute-start | bytes 196616 | tf_op jit(solution)/shard_map/ppermute | solution.py:179
  40.0 6.8 %collective-permute-start.4 = (bf16[16,2048]{1,0:T(8,128)(2,1)S(1)}, bf16[16,2048]{1,0:T(8,128)(2,1)S(1)}, u32[]{:S(2)}, u32[]{:S(2)}) collective-permute-start(bf16[16,2048]{1,0:T(8,128)(2,1)S(1)} %shard_map.140.refs_2_), channel_id=1, source_target_pairs={{0,2},{1,3},{2,0},{3,1},{4,6},{5,7},{6,4},{7,5},{8,10},{9,11},{10,... | collective-permute-start | bytes 196616 | tf_op jit(solution)/shard_map/ppermute | solution.py:179
  48.4 1.6 %collective-permute-start.7 = (bf16[32,2176]{1,0:T(8,128)(2,1)S(1)}, bf16[32,2176]{1,0:T(8,128)(2,1)S(1)}, u32[]{:S(2)}, u32[]{:S(2)}) collective-permute-start(bf16[32,2176]{1,0:T(8,128)(2,1)S(1)} %get-tuple-element.30), channel_id=1, source_target_pairs={{0,4},{4,0},{8,12},{12,8},{1,5},{5,1},{9,13},{13,9},{2,6},{6,2},{1... | collective-permute-start | bytes 417800 | tf_op jit(solution)/shard_map/ppermute | solution.py:179
  50.2 6.1 %collective-permute-start.10 = (bf16[32,2176]{1,0:T(8,128)(2,1)S(1)}, bf16[32,2176]{1,0:T(8,128)(2,1)S(1)}, u32[]{:S(2)}, u32[]{:S(2)}) collective-permute-start(bf16[32,2176]{1,0:T(8,128)(2,1)S(1)} %shard_map.145.refs_0_.own_ref), channel_id=1, source_target_pairs={{0,8},{4,12},{8,0},{12,4},{1,9},{5,13},{9,1},{13,5},{2,10},{6,14},... | collective-permute-start | bytes 417800 | tf_op jit(solution)/shard_map/ppermute | solution.py:179
  50.8 5.7 %slice-start = ((s8[14680064]{0:T(1024)(128)(4,1)}), s8[2097152]{0:T(1024)(128)(4,1)S(1)}, s32[]{:S(2)}) async-start(s8[14680064]{0:T(1024)(128)(4,1)} %bitcast.3), calls=%async_computation.2 | async-start | bytes 4194304
  50.8 5.7 %slice-start.1 = ((s8[14680064]{0:T(1024)(128)(4,1)}), s8[4194304]{0:T(1024)(128)(4,1)S(1)}, s32[]{:S(2)}) async-start(s8[14680064]{0:T(1024)(128)(4,1)} %bitcast.3), calls=%async_computation.3 | async-start | bytes 8388608
  50.8 5.7 %slice-start.2 = ((s8[14680064]{0:T(1024)(128)(4,1)}), s8[4194304]{0:T(1024)(128)(4,1)S(1)}, s32[]{:S(2)}) async-start(s8[14680064]{0:T(1024)(128)(4,1)} %bitcast.3), calls=%async_computation.4 | async-start | bytes 8388608
  52.0 1.4 %collective-permute-start.8 = (bf16[32,1536]{1,0:T(8,128)(2,1)S(1)}, bf16[32,1536]{1,0:T(8,128)(2,1)S(1)}, u32[]{:S(2)}, u32[]{:S(2)}) collective-permute-start(bf16[32,1536]{1,0:T(8,128)(2,1)S(1)} %shard_map.146), channel_id=1, source_target_pairs={{0,4},{4,0},{8,12},{12,8},{1,5},{5,1},{9,13},{13,9},{2,6},{6,2},{1... | collective-permute-start | bytes 294920 | tf_op jit(solution)/shard_map/ppermute | solution.py:179
  53.4 5.2 %collective-permute-start.9 = (bf16[32,1536]{1,0:T(8,128)(2,1)S(1)}, bf16[32,1536]{1,0:T(8,128)(2,1)S(1)}, u32[]{:S(2)}, u32[]{:S(2)}) collective-permute-start(bf16[32,1536]{1,0:T(8,128)(2,1)S(1)} %shard_map.147.own_ref), channel_id=1, source_target_pairs={{0,8},{4,12},{8,0},{12,4},{1,9},{5,13},{9,1},{13,5},{2,10},{6,14},... | collective-permute-start | bytes 294920 | tf_op jit(solution)/shard_map/ppermute | solution.py:179
  56.4 1.3 %collective-permute-start.11 = (bf16[32,1024]{1,0:T(8,128)(2,1)S(1)}, bf16[32,1024]{1,0:T(8,128)(2,1)S(1)}, u32[]{:S(2)}, u32[]{:S(2)}) collective-permute-start(bf16[32,1024]{1,0:T(8,128)(2,1)S(1)} %get-tuple-element.32.hidden_ref), channel_id=1, source_target_pairs={{0,4},{4,0},{8,12},{12,8},{1,5},{5,1},{9,13},{13,9},{2,6},{6,2},{1... | collective-permute-start | bytes 196616 | tf_op jit(solution)/shard_map/ppermute | solution.py:179
  58.7 1.3 %collective-permute-start.12 = (bf16[32,768]{1,0:T(8,128)(2,1)S(1)}, bf16[32,768]{1,0:T(8,128)(2,1)S(1)}, u32[]{:S(2)}, u32[]{:S(2)}) collective-permute-start(bf16[32,768]{1,0:T(8,128)(2,1)S(1)} %shard_map.151.hidden_ref), channel_id=1, source_target_pairs={{0,4},{4,0},{8,12},{12,8},{1,5},{5,1},{9,13},{13,9},{2,6},{6,2},{1... | collective-permute-start | bytes 147464 | tf_op jit(solution)/shard_map/ppermute | solution.py:179
  60.7 4.5 %collective-permute-start.13 = (bf16[8,2048]{1,0:T(8,128)(2,1)S(1)}, bf16[8,2048]{1,0:T(8,128)(2,1)S(1)}, u32[]{:S(2)}, u32[]{:S(2)}) collective-permute-start(bf16[8,2048]{1,0:T(8,128)(2,1)S(1)} %get-tuple-element.34), channel_id=1, source_target_pairs={{0,1},{1,0},{2,3},{3,2},{4,5},{5,4},{6,7},{7,6},{8,9},{9,8},{10,11... | collective-permute-start | bytes 98312 | tf_op jit(solution)/shard_map/ppermute | solution.py:179
  60.8 5.8 %collective-permute-start.14 = (bf16[8,2048]{1,0:T(8,128)(2,1)S(1)}, bf16[8,2048]{1,0:T(8,128)(2,1)S(1)}, u32[]{:S(2)}, u32[]{:S(2)}) collective-permute-start(bf16[8,2048]{1,0:T(8,128)(2,1)S(1)} %get-tuple-element.35), channel_id=1, source_target_pairs={{0,2},{1,3},{2,0},{3,1},{4,6},{5,7},{6,4},{7,5},{8,10},{9,11},{10,... | collective-permute-start | bytes 98312 | tf_op jit(solution)/shard_map/ppermute | solution.py:179
  62.1 5.7 %collective-permute-start.15 = (bf16[8,2048]{1,0:T(8,128)(2,1)S(1)}, bf16[8,2048]{1,0:T(8,128)(2,1)S(1)}, u32[]{:S(2)}, u32[]{:S(2)}) collective-permute-start(bf16[8,2048]{1,0:T(8,128)(2,1)S(1)} %get-tuple-element.36), channel_id=1, source_target_pairs={{0,3},{1,2},{2,1},{3,0},{4,7},{5,6},{6,5},{7,4},{8,11},{9,10},{10,... | collective-permute-start | bytes 98312 | tf_op jit(solution)/shard_map/ppermute | solution.py:179
  (2 other events, 5.2 us)

commit v5 on v4

--- a/solution.py
+++ b/solution.py
@@ -156,7 +156,7 @@
 
 LANES = 128
 MIB = 2**20
-COVER = (100, 100, 100, 1, 10, 10, 10, 1, 1, 1)
+COVER = (100, 100, 1, 1, 1, 1, 1, 1, 1, 1)
 CHUNK = 512
 FIRST_PART = 57
 
@@ -355,7 +355,7 @@
 
 
 def middle_kernel(*refs):
-    served_ref, stream_ref, *term_refs, gain_ref, wg_ref, wu_ref = refs[:-5]
+    served_ref, stream_ref, *term_refs, gain_ref, wg_ref, wu_ref, _ = refs[:-5]
     scaled_ref, tail_ref, send_ref, middle_ref, rows_ref = refs[-5:]
     count = stream_ref.shape[0]
     row = lax.broadcasted_iota(jnp.int32, (count, count), 0)
@@ -587,7 +587,7 @@
             wide(sizes[0], jnp.bfloat16, LANES),
             block,
         ],
-        [served[None, :], stream, *terms, ffn_gain[None, :], w_gate, w_up],
+        [served[None, :], stream, *terms, ffn_gain[None, :], w_gate, w_up, w_down],
         scratch=[row_scratch],
         cost=COVER[4],
     )

time: 69.2 us -> 69.7 us (level)
  no operation moved by 1% of the time
where the time goes in v5:
time: 69.7 us; the launch traced here: 69.5 us
  blocking collectives  19.6 us (28%)
  starting transfers between devices  18 us (26%)
  waiting for transfers between devices  16.8 us (24%)
  Pallas kernels  13.9 us (20%)
  local copies, waits for them, and re-layouts  0.77 us (1%)
    ppermute x16, starting transfers between devices, swap(): return lax.ppermute(value, axis, [(i, i ^ distance) for i in range(count)])  18 us
    ppermute x16, waiting for transfers between devices, swap(): return lax.ppermute(value, axis, [(i, i ^ distance) for i in range(count)])  16.8 us
    pallas_call x19, Pallas kernels, call(): pl.pallas_call(kernel, out_shape=outs, in_specs=specs, out_specs=[pl.Bloc...  13.9 us
    all_to_all x1, blocking collectives, local_exchange(): parts = lax.all_to_all(sums, ('role', 'tp'), 0, 0)  10.1 us
    all_to_all x1, blocking collectives, local_exchange(): heads = lax.all_to_all(heads, ('role', 'tp'), 0, 0)  9.54 us
  transfers between devices with their start and end apart: 16, of which 10 were waited for; matrix products, arithmetic and copies ran while one was open for 0% of the time, Pallas kernels for 10%

profile of v5, /device:TPU:0, one launch (start us, length us, event | category | flops | bytes accessed | tf_op | source)
XLA Modules:
  0.0 69.5 jit_solution(6455488241882270094)
XLA Ops:
  0.0 3.1 %collective-permute-start = (bf16[8,2048]{1,0:T(8,128)(2,1)}, bf16[8,2048]{1,0:T(8,128)(2,1)S(1)}, u32[]{:S(2)}, u32[]{:S(2)}) collective-permute-start(bf16[8,2048]{1,0:T(8,128)(2,1)} %refs_0_.1), channel_id=1, source_target_pairs={{0,1},{1,0},{2,3},{3,2},{4,5},{5,4},{6,7},{7,6},{8,9},{9,8},{10,11... | collective-permute-start | bytes 98312 | tf_op jit(solution)/shard_map/ppermute | solution.py:179
  3.1 2.6 %collective-permute-start.1 = (bf16[8,2048]{1,0:T(8,128)(2,1)}, bf16[8,2048]{1,0:T(8,128)(2,1)S(1)}, u32[]{:S(2)}, u32[]{:S(2)}) collective-permute-start(bf16[8,2048]{1,0:T(8,128)(2,1)} %refs_0_.1), channel_id=1, source_target_pairs={{0,2},{1,3},{2,0},{3,1},{4,6},{5,7},{6,4},{7,5},{8,10},{9,11},{10,... | collective-permute-start | bytes 98312 | tf_op jit(solution)/shard_map/ppermute | solution.py:179
  5.7 0.7 copy-done.10
  7.0 1.8 %collective-permute-done.1.refs_2_ = bf16[8,2048]{1,0:T(8,128)(2,1)S(1)} collective-permute-done((bf16[8,2048]{1,0:T(8,128)(2,1)}, bf16[8,2048]{1,0:T(8,128)(2,1)S(1)}, u32[]{:S(2)}, u32[]{:S(2)}) %collective-permute-start.1) | collective-permute-done | bytes 32800 | tf_op jit(solution)/shard_map/ppermute | solution.py:179
  8.8 2.9 %collective-permute-done.2.refs_3_ = bf16[8,2048]{1,0:T(8,128)(2,1)S(1)} collective-permute-done((bf16[8,2048]{1,0:T(8,128)(2,1)}, bf16[8,2048]{1,0:T(8,128)(2,1)S(1)}, u32[]{:S(2)}, u32[]{:S(2)}) %collective-permute-start.2) | collective-permute-done | bytes 32800 | tf_op jit(solution)/shard_map/ppermute | solution.py:179
  11.9 1.0 %shard_map.137 = (bf16[16,24,128]{2,1,0:T(8,128)(2,1)S(1)}, bf16[32,2048]{1,0:T(8,128)(2,1)S(1)}) custom-call(f32[2,128]{1,0:T(2,128)S(1)} %get-tuple-element.21._.cosine_ref, bf16[8,2048]{1,0:T(8,128)(2,1)S(1)} %copy-done.8, bf16[8,2048]{1,0:T(8,128)(2,1)S(1)} %collective-permute-done.refs_1_, bf16[8,2048]{1,0:T(8,128)(2,1)S(1)} %collective-permute-done.1.refs_2_, ...), custom_call_target="tpu_custom_call" | custom-call | flops 99999997952 | bytes 1048576 | tf_op jit(solution)/shard_map/pallas_call | solution.py:189
  12.9 10.1 %all_to_all.10.got_ref = bf16[16,24,128]{2,1,0:T(8,128)(2,1)S(1)} all-to-all(bf16[16,24,128]{2,1,0:T(8,128)(2,1)S(1)} %get-tuple-element.23), channel_id=1, replica_groups=mesh['groups'=2,'role'=4,'tp'=4] {'role','tp'}, dimensions={0} | all-to-all | bytes 196608 | tf_op jit(solution)/shard_map/all_to_all | solution.py:546
  23.0 1.4 %shard_map.138 = bf16[16,16,128]{2,1,0:T(8,128)(2,1)S(1)} custom-call(s32[2]{0:T(128)S(1)} %copy-done.11, bf16[16,24,128]{2,1,0:T(8,128)(2,1)S(1)} %all_to_all.10.got_ref, f32[2,128]{1,0:T(2,128)S(1)} %get-tuple-element.21._.cosine_ref, f32[2,128]{1,0:T(2,128)S(1)} %get-tuple-element.24.sine_ref, bf16[2,256,512]{2,1,0:T(8,128)(2,1)S(1)} %copy-done.6, ...), custom_call_target="tpu_custom_call" | custom-call | flops 1000000000 | bytes 1048576 | tf_op jit(solution)/shard_map/pallas_call | solution.py:189
  24.4 9.5 %all_to_all.11.heads_ref = bf16[16,16,128]{2,1,0:T(8,128)(2,1)S(1)} all-to-all(bf16[16,16,128]{2,1,0:T(8,128)(2,1)S(1)} %shard_map.138), channel_id=1, replica_groups=mesh['groups'=2,'role'=4,'tp'=4] {'role','tp'}, dimensions={0} | all-to-all | bytes 131072 | tf_op jit(solution)/shard_map/all_to_all | solution.py:554
  33.9 0.8 %shard_map.139 = (bf16[16,2048]{1,0:T(8,128)(2,1)S(1)}, bf16[16,2048]{1,0:T(8,128)(2,1)S(1)}) custom-call(bf16[16,16,128]{2,1,0:T(8,128)(2,1)S(1)} %all_to_all.11.heads_ref, bf16[1024,2048]{1,0:T(8,128)(2,1)S(1)} %copy-done), custom_call_target="tpu_custom_call" | custom-call | flops 1000000000 | bytes 1048576 | tf_op jit(solution)/shard_map/pallas_call | solution.py:189
  35.1 1.7 %collective-permute-start.3 = (bf16[16,2048]{1,0:T(8,128)(2,1)S(1)}, bf16[16,2048]{1,0:T(8,128)(2,1)S(1)}, u32[]{:S(2)}, u32[]{:S(2)}) collective-permute-start(bf16[16,2048]{1,0:T(8,128)(2,1)S(1)} %get-tuple-element.25.keep_ref), channel_id=1, source_target_pairs={{0,1},{1,0},{2,3},{3,2},{4,5},{5,4},{6,7},{7,6},{8,9},{9,8},{10,11... | collective-permute-start | bytes 196616 | tf_op jit(solution)/shard_map/ppermute | solution.py:179
  36.8 2.8 %collective-permute-done.5.got_ref = bf16[16,2048]{1,0:T(8,128)(2,1)S(1)} collective-permute-done((bf16[16,2048]{1,0:T(8,128)(2,1)S(1)}, bf16[16,2048]{1,0:T(8,128)(2,1)S(1)}, u32[]{:S(2)}, u32[]{:S(2)}) %collective-permute-start.5) | collective-permute-done | bytes 65568 | tf_op jit(solution)/shard_map/ppermute | solution.py:179
  39.6 0.7 collective-permute-start.6
  40.3 2.4 %collective-permute-start.4 = (bf16[16,2048]{1,0:T(8,128)(2,1)S(1)}, bf16[16,2048]{1,0:T(8,128)(2,1)S(1)}, u32[]{:S(2)}, u32[]{:S(2)}) collective-permute-start(bf16[16,2048]{1,0:T(8,128)(2,1)S(1)} %shard_map.140.refs_2_), channel_id=1, source_target_pairs={{0,2},{1,3},{2,0},{3,1},{4,6},{5,7},{6,4},{7,5},{8,10},{9,11},{10,... | collective-permute-start | bytes 196616 | tf_op jit(solution)/shard_map/ppermute | solution.py:179
  42.7 3.7 %collective-permute-done.6.refs_5_ = bf16[16,2048]{1,0:T(8,128)(2,1)S(1)} collective-permute-done((bf16[16,2048]{1,0:T(8,128)(2,1)S(1)}, bf16[16,2048]{1,0:T(8,128)(2,1)S(1)}, u32[]{:S(2)}, u32[]{:S(2)}) %collective-permute-start.6) | collective-permute-done | bytes 65568 | tf_op jit(solution)/shard_map/ppermute | solution.py:179
  46.4 0.7 %collective-permute-done.4.refs_3_ = bf16[16,2048]{1,0:T(8,128)(2,1)S(1)} collective-permute-done((bf16[16,2048]{1,0:T(8,128)(2,1)S(1)}, bf16[16,2048]{1,0:T(8,128)(2,1)S(1)}, u32[]{:S(2)}, u32[]{:S(2)}) %collective-permute-start.4) | collective-permute-done | bytes 65568 | tf_op jit(solution)/shard_map/ppermute | solution.py:179
  47.3 1.6 %shard_map.142 = (bf16[32,2048]{1,0:T(8,128)(2,1)S(1)}, f32[32,128]{1,0:T(8,128)S(1)}, bf16[32,2176]{1,0:T(8,128)(2,1)S(1)}, bf16[8,2048]{1,0:T(8,128)(2,1)S(1)}) custom-call(s32[1,32]{1,0:T(1,128)S(1)} %bitcast.10, bf16[32,2048]{1,0:T(8,128)(2,1)S(1)} %get-tuple-element.22.refs_1_, bf16[16,2048]{1,0:T(8,128)(2,1)S(1)} %shard_map.140.refs_2_, ...), custom_call_target="tpu_custom_call" | custom-call | flops 1000000000 | bytes 1048576 | tf_op jit(solution)/shard_map/pallas_call | solution.py:189
  49.0 1.5 %shard_map.144.keep_ref = f32[32,2048]{1,0:T(8,128)S(1)} custom-call(bf16[32,2048]{1,0:T(8,128)(2,1)S(1)} %get-tuple-element.28.scaled_ref, bf16[2048,3584]{1,0:T(8,128)(2,1)S(1)} %bitcast.6, bf16[2048,3584]{1,0:T(8,128)(2,1)S(1)} %bitcast.8), custom_call_target="tpu_custom_call" | custom-call | flops 1000000000 | bytes 1048576 | tf_op jit(solution)/shard_map/pallas_call | solution.py:189
  50.6 0.7 collective-permute-start.10
  51.3 1.2 %shard_map.146 = bf16[32,1536]{1,0:T(8,128)(2,1)S(1)} custom-call(bf16[32,2048]{1,0:T(8,128)(2,1)S(1)} %get-tuple-element.28.scaled_ref, bf16[2048,3584]{1,0:T(8,128)(2,1)S(1)} %bitcast.6, bf16[2048,3584]{1,0:T(8,128)(2,1)S(1)} %bitcast.8, bf16[32,2176]{1,0:T(8,128)(2,1)S(1)} %shard_map.145.refs_0_.own_ref), custom_call_target="tpu_custom_call" | custom-call | flops 1000000000 | bytes 1048576 | tf_op jit(solution)/shard_map/pallas_call | solution.py:189
  52.7 1.2 %shard_map.143.keep_ref = f32[32,1536]{1,0:T(8,128)S(1)} custom-call(bf16[32,2048]{1,0:T(8,128)(2,1)S(1)} %get-tuple-element.28.scaled_ref, bf16[2048,3584]{1,0:T(8,128)(2,1)S(1)} %bitcast.6, bf16[2048,3584]{1,0:T(8,128)(2,1)S(1)} %bitcast.8), custom_call_target="tpu_custom_call" | custom-call | flops 1000000000 | bytes 1048576 | tf_op jit(solution)/shard_map/pallas_call | solution.py:189
  53.9 1.5 %collective-permute-start.9 = (bf16[32,1536]{1,0:T(8,128)(2,1)S(1)}, bf16[32,1536]{1,0:T(8,128)(2,1)S(1)}, u32[]{:S(2)}, u32[]{:S(2)}) collective-permute-start(bf16[32,1536]{1,0:T(8,128)(2,1)S(1)} %shard_map.147.own_ref), channel_id=1, source_target_pairs={{0,8},{4,12},{8,0},{12,4},{1,9},{5,13},{9,1},{13,5},{2,10},{6,14},... | collective-permute-start | bytes 294920 | tf_op jit(solution)/shard_map/ppermute | solution.py:179
  55.4 1.4 %collective-permute-done.10.got_ref = bf16[32,2176]{1,0:T(8,128)(2,1)S(1)} collective-permute-done((bf16[32,2176]{1,0:T(8,128)(2,1)S(1)}, bf16[32,2176]{1,0:T(8,128)(2,1)S(1)}, u32[]{:S(2)}, u32[]{:S(2)}) %collective-permute-start.10) | collective-permute-done | bytes 139296 | tf_op jit(solution)/shard_map/ppermute | solution.py:179
  57.0 0.8 %shard_map.149.refs_0_ = f32[32,2048]{1,0:T(8,128)S(1)} custom-call(bf16[32,1024]{1,0:T(8,128)(2,1)S(1)} %get-tuple-element.32.hidden_ref, bf16[3584,2048]{1,0:T(8,128)(2,1)S(1)} %bitcast.4), custom_call_target="tpu_custom_call" | custom-call | flops 1000000000 | bytes 1048576 | tf_op jit(solution)/shard_map/pallas_call | solution.py:189
  58.2 0.8 %shard_map.150._.refs_0_ = f32[32,2048]{1,0:T(8,128)S(1)} custom-call(bf16[32,1024]{1,0:T(8,128)(2,1)S(1)} %collective-permute-done.11.hidden_ref, bf16[3584,2048]{1,0:T(8,128)(2,1)S(1)} %bitcast.4, f32[32,2048]{1,0:T(8,128)S(1)} %shard_map.149.refs_0_), custom_call_target="tpu_custom_call" | custom-call | flops 1000000000 | bytes 1048576 | tf_op jit(solution)/shard_map/pallas_call | solution.py:189
  59.4 0.6 shard_map.152.before_ref
  60.5 0.7 shard_map.153
  61.2 1.3 %collective-permute-start.14 = (bf16[8,2048]{1,0:T(8,128)(2,1)S(1)}, bf16[8,2048]{1,0:T(8,128)(2,1)S(1)}, u32[]{:S(2)}, u32[]{:S(2)}) collective-permute-start(bf16[8,2048]{1,0:T(8,128)(2,1)S(1)} %get-tuple-element.35), channel_id=1, source_target_pairs={{0,2},{1,3},{2,0},{3,1},{4,6},{5,7},{6,4},{7,5},{8,10},{9,11},{10,... | collective-permute-start | bytes 98312 | tf_op jit(solution)/shard_map/ppermute | solution.py:179
  62.6 3.1 %collective-permute-start.15 = (bf16[8,2048]{1,0:T(8,128)(2,1)S(1)}, bf16[8,2048]{1,0:T(8,128)(2,1)S(1)}, u32[]{:S(2)}, u32[]{:S(2)}) collective-permute-start(bf16[8,2048]{1,0:T(8,128)(2,1)S(1)} %get-tuple-element.36), channel_id=1, source_target_pairs={{0,3},{1,2},{2,1},{3,0},{4,7},{5,6},{6,5},{7,4},{8,11},{9,10},{10,... | collective-permute-start | bytes 98312 | tf_op jit(solution)/shard_map/ppermute | solution.py:179
  65.6 1.4 %collective-permute-done.14.refs_2_ = bf16[8,2048]{1,0:T(8,128)(2,1)S(1)} collective-permute-done((bf16[8,2048]{1,0:T(8,128)(2,1)S(1)}, bf16[8,2048]{1,0:T(8,128)(2,1)S(1)}, u32[]{:S(2)}, u32[]{:S(2)}) %collective-permute-start.14) | collective-permute-done | bytes 32800 | tf_op jit(solution)/shard_map/ppermute | solution.py:179
  67.0 1.3 %collective-permute-done.15.refs_3_ = bf16[8,2048]{1,0:T(8,128)(2,1)S(1)} collective-permute-done((bf16[8,2048]{1,0:T(8,128)(2,1)S(1)}, bf16[8,2048]{1,0:T(8,128)(2,1)S(1)}, u32[]{:S(2)}, u32[]{:S(2)}) %collective-permute-start.15) | collective-permute-done | bytes 32800 | tf_op jit(solution)/shard_map/ppermute | solution.py:179
  68.3 1.2 %shard_map.154 = bf16[8,2048]{1,0:T(8,128)(2,1)} custom-call(s32[32]{0:T(128)S(1)} %copy-done.2, bf16[8,2048]{1,0:T(8,128)(2,1)S(1)} %get-tuple-element.27.stream_ref, bf16[8,2048]{1,0:T(8,128)(2,1)S(1)} %get-tuple-element.33.refs_0_, bf16[8,2048]{1,0:T(8,128)(2,1)S(1)} %collective-permute-done.13.refs_1_, ...), custom_call_target="tpu_custom_call" | custom-call | bytes 1048576 | tf_op jit(solution)/shard_map/pallas_call | solution.py:189
  (72 shorter events, 3.0 us)
Async XLA Ops:
  0.0 11.7 %copy-start.5 = (bf16[2048,128]{1,0:T(8,128)(2,1)S(1)}, bf16[2048,128]{1,0:T(8,128)(2,1)}, u32[]{:S(2)}) copy-start(bf16[2048,128]{1,0:T(8,128)(2,1)} %refs_7_.2) | copy-start | bytes 1572868
  0.0 7.0 %collective-permute-start = (bf16[8,2048]{1,0:T(8,128)(2,1)}, bf16[8,2048]{1,0:T(8,128)(2,1)S(1)}, u32[]{:S(2)}, u32[]{:S(2)}) collective-permute-start(bf16[8,2048]{1,0:T(8,128)(2,1)} %refs_0_.1), channel_id=1, source_target_pairs={{0,1},{1,0},{2,3},{3,2},{4,5},{5,4},{6,7},{7,6},{8,9},{9,8},{10,11... | collective-permute-start | bytes 98312 | tf_op jit(solution)/shard_map/ppermute | solution.py:179
  3.1 5.6 %collective-permute-start.1 = (bf16[8,2048]{1,0:T(8,128)(2,1)}, bf16[8,2048]{1,0:T(8,128)(2,1)S(1)}, u32[]{:S(2)}, u32[]{:S(2)}) collective-permute-start(bf16[8,2048]{1,0:T(8,128)(2,1)} %refs_0_.1), channel_id=1, source_target_pairs={{0,2},{1,3},{2,0},{3,1},{4,6},{5,7},{6,4},{7,5},{8,10},{9,11},{10,... | collective-permute-start | bytes 98312 | tf_op jit(solution)/shard_map/ppermute | solution.py:179
  5.7 5.9 %collective-permute-start.2 = (bf16[8,2048]{1,0:T(8,128)(2,1)}, bf16[8,2048]{1,0:T(8,128)(2,1)S(1)}, u32[]{:S(2)}, u32[]{:S(2)}) collective-permute-start(bf16[8,2048]{1,0:T(8,128)(2,1)} %refs_0_.1), channel_id=1, source_target_pairs={{0,3},{1,2},{2,1},{3,0},{4,7},{5,6},{6,5},{7,4},{8,11},{9,10},{10,... | collective-permute-start | bytes 98312 | tf_op jit(solution)/shard_map/ppermute | solution.py:179
  11.7 35.5 %slice-start = ((s8[14680064]{0:T(1024)(128)(4,1)}), s8[4194304]{0:T(1024)(128)(4,1)S(1)}, s32[]{:S(2)}) async-start(s8[14680064]{0:T(1024)(128)(4,1)} %bitcast.3), calls=%async_computation.2 | async-start | bytes 8388608
  11.7 35.5 %slice-start.4 = ((s8[14680064]{0:T(1024)(128)(4,1)}), s8[4194304]{0:T(1024)(128)(4,1)S(1)}, s32[]{:S(2)}) async-start(s8[14680064]{0:T(1024)(128)(4,1)} %bitcast.5), calls=%async_computation.6 | async-start | bytes 8388608
  11.7 35.5 %slice-start.8 = ((s8[14680064]{0:T(1024)(128)(4,1)}), s8[4194304]{0:T(1024)(128)(4,1)S(1)}, s32[]{:S(2)}) async-start(s8[14680064]{0:T(1024)(128)(4,1)} %bitcast.7), calls=%async_computation.10 | async-start | bytes 8388608
  11.7 22.2 %copy-start = (bf16[1024,2048]{1,0:T(8,128)(2,1)S(1)}, bf16[1024,2048]{1,0:T(8,128)(2,1)}, u32[]{:S(2)}) copy-start(bf16[1024,2048]{1,0:T(8,128)(2,1)} %w_ref.5) | copy-start | bytes 12582916
  11.8 35.4 %slice-start.1 = ((s8[14680064]{0:T(1024)(128)(4,1)}), s8[4194304]{0:T(1024)(128)(4,1)S(1)}, s32[]{:S(2)}) async-start(s8[14680064]{0:T(1024)(128)(4,1)} %bitcast.3), calls=%async_computation.3 | async-start | bytes 8388608
  11.8 35.4 %slice-start.2 = ((s8[14680064]{0:T(1024)(128)(4,1)}), s8[4194304]{0:T(1024)(128)(4,1)S(1)}, s32[]{:S(2)}) async-start(s8[14680064]{0:T(1024)(128)(4,1)} %bitcast.3), calls=%async_computation.4 | async-start | bytes 8388608
  11.8 35.4 %slice-start.3 = ((s8[14680064]{0:T(1024)(128)(4,1)}), s8[2097152]{0:T(1024)(128)(4,1)S(1)}, s32[]{:S(2)}) async-start(s8[14680064]{0:T(1024)(128)(4,1)} %bitcast.3), calls=%async_computation.5 | async-start | bytes 4194304
  11.8 35.4 %slice-start.5 = ((s8[14680064]{0:T(1024)(128)(4,1)}), s8[4194304]{0:T(1024)(128)(4,1)S(1)}, s32[]{:S(2)}) async-start(s8[14680064]{0:T(1024)(128)(4,1)} %bitcast.5), calls=%async_computation.7 | async-start | bytes 8388608
  11.8 35.4 %slice-start.6 = ((s8[14680064]{0:T(1024)(128)(4,1)}), s8[4194304]{0:T(1024)(128)(4,1)S(1)}, s32[]{:S(2)}) async-start(s8[14680064]{0:T(1024)(128)(4,1)} %bitcast.5), calls=%async_computation.8 | async-start | bytes 8388608
  11.8 35.4 %slice-start.7 = ((s8[14680064]{0:T(1024)(128)(4,1)}), s8[2097152]{0:T(1024)(128)(4,1)S(1)}, s32[]{:S(2)}) async-start(s8[14680064]{0:T(1024)(128)(4,1)} %bitcast.5), calls=%async_computation.9 | async-start | bytes 4194304
  11.8 35.4 %slice-start.9 = ((s8[14680064]{0:T(1024)(128)(4,1)}), s8[4194304]{0:T(1024)(128)(4,1)S(1)}, s32[]{:S(2)}) async-start(s8[14680064]{0:T(1024)(128)(4,1)} %bitcast.7), calls=%async_computation.11 | async-start | bytes 8388608
  11.8 35.4 %slice-start.10 = ((s8[14680064]{0:T(1024)(128)(4,1)}), s8[4194304]{0:T(1024)(128)(4,1)S(1)}, s32[]{:S(2)}) async-start(s8[14680064]{0:T(1024)(128)(4,1)} %bitcast.7), calls=%async_computation.12 | async-start | bytes 8388608
  11.8 35.4 %slice-start.11 = ((s8[14680064]{0:T(1024)(128)(4,1)}), s8[2097152]{0:T(1024)(128)(4,1)S(1)}, s32[]{:S(2)}) async-start(s8[14680064]{0:T(1024)(128)(4,1)} %bitcast.7), calls=%async_computation.13 | async-start | bytes 4194304
  11.9 35.4 %copy-start.1 = (f32[2048]{0:T(1024)S(1)}, f32[2048]{0:T(1024)}, u32[]{:S(2)}) copy-start(f32[2048]{0:T(1024)} %param.24) | copy-start | bytes 24580
  11.9 35.4 %copy-start.2 = (s32[32]{0:T(128)S(1)}, s32[32]{0:T(128)}, u32[]{:S(2)}) copy-start(s32[32]{0:T(128)} %served_ref.1) | copy-start | bytes 388
  34.8 4.8 %collective-permute-start.5 = (bf16[16,2048]{1,0:T(8,128)(2,1)S(1)}, bf16[16,2048]{1,0:T(8,128)(2,1)S(1)}, u32[]{:S(2)}, u32[]{:S(2)}) collective-permute-start(bf16[16,2048]{1,0:T(8,128)(2,1)S(1)} %get-tuple-element.26.keep_ref), channel_id=1, source_target_pairs={{0,1},{1,0},{2,3},{3,2},{4,5},{5,4},{6,7},{7,6},{8,9},{9,8},{10,11... | collective-permute-start | bytes 196616 | tf_op jit(solution)/shard_map/ppermute | solution.py:179
  35.1 5.2 %collective-permute-start.3 = (bf16[16,2048]{1,0:T(8,128)(2,1)S(1)}, bf16[16,2048]{1,0:T(8,128)(2,1)S(1)}, u32[]{:S(2)}, u32[]{:S(2)}) collective-permute-start(bf16[16,2048]{1,0:T(8,128)(2,1)S(1)} %get-tuple-element.25.keep_ref), channel_id=1, source_target_pairs={{0,1},{1,0},{2,3},{3,2},{4,5},{5,4},{6,7},{7,6},{8,9},{9,8},{10,11... | collective-permute-start | bytes 196616 | tf_op jit(solution)/shard_map/ppermute | solution.py:179
  39.6 6.8 %collective-permute-start.6 = (bf16[16,2048]{1,0:T(8,128)(2,1)S(1)}, bf16[16,2048]{1,0:T(8,128)(2,1)S(1)}, u32[]{:S(2)}, u32[]{:S(2)}) collective-permute-start(bf16[16,2048]{1,0:T(8,128)(2,1)S(1)} %shard_map.141.refs_4_), channel_id=1, source_target_pairs={{0,2},{1,3},{2,0},{3,1},{4,6},{5,7},{6,4},{7,5},{8,10},{9,11},{10,... | collective-permute-start | bytes 196616 | tf_op jit(solution)/shard_map/ppermute | solution.py:179
  40.3 6.8 %collective-permute-start.4 = (bf16[16,2048]{1,0:T(8,128)(2,1)S(1)}, bf16[16,2048]{1,0:T(8,128)(2,1)S(1)}, u32[]{:S(2)}, u32[]{:S(2)}) collective-permute-start(bf16[16,2048]{1,0:T(8,128)(2,1)S(1)} %shard_map.140.refs_2_), channel_id=1, source_target_pairs={{0,2},{1,3},{2,0},{3,1},{4,6},{5,7},{6,4},{7,5},{8,10},{9,11},{10,... | collective-permute-start | bytes 196616 | tf_op jit(solution)/shard_map/ppermute | solution.py:179
  48.9 1.6 %collective-permute-start.7 = (bf16[32,2176]{1,0:T(8,128)(2,1)S(1)}, bf16[32,2176]{1,0:T(8,128)(2,1)S(1)}, u32[]{:S(2)}, u32[]{:S(2)}) collective-permute-start(bf16[32,2176]{1,0:T(8,128)(2,1)S(1)} %get-tuple-element.30), channel_id=1, source_target_pairs={{0,4},{4,0},{8,12},{12,8},{1,5},{5,1},{9,13},{13,9},{2,6},{6,2},{1... | collective-permute-start | bytes 417800 | tf_op jit(solution)/shard_map/ppermute | solution.py:179
  50.6 6.1 %collective-permute-start.10 = (bf16[32,2176]{1,0:T(8,128)(2,1)S(1)}, bf16[32,2176]{1,0:T(8,128)(2,1)S(1)}, u32[]{:S(2)}, u32[]{:S(2)}) collective-permute-start(bf16[32,2176]{1,0:T(8,128)(2,1)S(1)} %shard_map.145.refs_0_.own_ref), channel_id=1, source_target_pairs={{0,8},{4,12},{8,0},{12,4},{1,9},{5,13},{9,1},{13,5},{2,10},{6,14},... | collective-permute-start | bytes 417800 | tf_op jit(solution)/shard_map/ppermute | solution.py:179
  52.5 1.4 %collective-permute-start.8 = (bf16[32,1536]{1,0:T(8,128)(2,1)S(1)}, bf16[32,1536]{1,0:T(8,128)(2,1)S(1)}, u32[]{:S(2)}, u32[]{:S(2)}) collective-permute-start(bf16[32,1536]{1,0:T(8,128)(2,1)S(1)} %shard_map.146), channel_id=1, source_target_pairs={{0,4},{4,0},{8,12},{12,8},{1,5},{5,1},{9,13},{13,9},{2,6},{6,2},{1... | collective-permute-start | bytes 294920 | tf_op jit(solution)/shard_map/ppermute | solution.py:179
  53.9 5.2 %collective-permute-start.9 = (bf16[32,1536]{1,0:T(8,128)(2,1)S(1)}, bf16[32,1536]{1,0:T(8,128)(2,1)S(1)}, u32[]{:S(2)}, u32[]{:S(2)}) collective-permute-start(bf16[32,1536]{1,0:T(8,128)(2,1)S(1)} %shard_map.147.own_ref), channel_id=1, source_target_pairs={{0,8},{4,12},{8,0},{12,4},{1,9},{5,13},{9,1},{13,5},{2,10},{6,14},... | collective-permute-start | bytes 294920 | tf_op jit(solution)/shard_map/ppermute | solution.py:179
  56.9 1.3 %collective-permute-start.11 = (bf16[32,1024]{1,0:T(8,128)(2,1)S(1)}, bf16[32,1024]{1,0:T(8,128)(2,1)S(1)}, u32[]{:S(2)}, u32[]{:S(2)}) collective-permute-start(bf16[32,1024]{1,0:T(8,128)(2,1)S(1)} %get-tuple-element.32.hidden_ref), channel_id=1, source_target_pairs={{0,4},{4,0},{8,12},{12,8},{1,5},{5,1},{9,13},{13,9},{2,6},{6,2},{1... | collective-permute-start | bytes 196616 | tf_op jit(solution)/shard_map/ppermute | solution.py:179
  59.2 1.3 %collective-permute-start.12 = (bf16[32,768]{1,0:T(8,128)(2,1)S(1)}, bf16[32,768]{1,0:T(8,128)(2,1)S(1)}, u32[]{:S(2)}, u32[]{:S(2)}) collective-permute-start(bf16[32,768]{1,0:T(8,128)(2,1)S(1)} %shard_map.151.hidden_ref), channel_id=1, source_target_pairs={{0,4},{4,0},{8,12},{12,8},{1,5},{5,1},{9,13},{13,9},{2,6},{6,2},{1... | collective-permute-start | bytes 147464 | tf_op jit(solution)/shard_map/ppermute | solution.py:179
  61.2 4.5 %collective-permute-start.13 = (bf16[8,2048]{1,0:T(8,128)(2,1)S(1)}, bf16[8,2048]{1,0:T(8,128)(2,1)S(1)}, u32[]{:S(2)}, u32[]{:S(2)}) collective-permute-start(bf16[8,2048]{1,0:T(8,128)(2,1)S(1)} %get-tuple-element.34), channel_id=1, source_target_pairs={{0,1},{1,0},{2,3},{3,2},{4,5},{5,4},{6,7},{7,6},{8,9},{9,8},{10,11... | collective-permute-start | bytes 98312 | tf_op jit(solution)/shard_map/ppermute | solution.py:179
  61.2 5.8 %collective-permute-start.14 = (bf16[8,2048]{1,0:T(8,128)(2,1)S(1)}, bf16[8,2048]{1,0:T(8,128)(2,1)S(1)}, u32[]{:S(2)}, u32[]{:S(2)}) collective-permute-start(bf16[8,2048]{1,0:T(8,128)(2,1)S(1)} %get-tuple-element.35), channel_id=1, source_target_pairs={{0,2},{1,3},{2,0},{3,1},{4,6},{5,7},{6,4},{7,5},{8,10},{9,11},{10,... | collective-permute-start | bytes 98312 | tf_op jit(solution)/shard_map/ppermute | solution.py:179
  62.6 5.7 %collective-permute-start.15 = (bf16[8,2048]{1,0:T(8,128)(2,1)S(1)}, bf16[8,2048]{1,0:T(8,128)(2,1)S(1)}, u32[]{:S(2)}, u32[]{:S(2)}) collective-permute-start(bf16[8,2048]{1,0:T(8,128)(2,1)S(1)} %get-tuple-element.36), channel_id=1, source_target_pairs={{0,3},{1,2},{2,1},{3,0},{4,7},{5,6},{6,5},{7,4},{8,11},{9,10},{10,... | collective-permute-start | bytes 98312 | tf_op jit(solution)/shard_map/ppermute | solution.py:179
  (8 other events, 81.2 us)

commit v6 on v4

--- a/solution.py
+++ b/solution.py
@@ -158,6 +158,8 @@
 MIB = 2**20
 COVER = (100, 100, 100, 1, 10, 10, 10, 1, 1, 1)
 CHUNK = 512
+PARTS = (16, 16)
+STEPS = (1, 2)
 FIRST_PART = 57
 
 
@@ -355,8 +357,8 @@
 
 
 def middle_kernel(*refs):
-    served_ref, stream_ref, *term_refs, gain_ref, wg_ref, wu_ref = refs[:-5]
-    scaled_ref, tail_ref, send_ref, middle_ref, rows_ref = refs[-5:]
+    served_ref, stream_ref, *term_refs, gain_ref, wg_ref, wu_ref = refs[:-7]
+    scaled_ref, tail_ref, send_ref, middle_ref, live_ref, rows_ref, live_rows_ref = refs[-7:]
     count = stream_ref.shape[0]
     row = lax.broadcasted_iota(jnp.int32, (count, count), 0)
     column = lax.broadcasted_iota(jnp.int32, (count, count), 1)
@@ -377,6 +379,8 @@
     own = middle_ref.shape[0]
     start = pl.multiple_of(lax.axis_index("tp") * own, own)
     middle_ref[...] = rows_ref[pl.ds(start, own), :].astype(jnp.bfloat16)
+    live_rows_ref[...] = jnp.broadcast_to(live, live_rows_ref.shape)
+    live_ref[...] = live_rows_ref[pl.ds(start, own), :]
     squares = jnp.sum(rows * rows, axis=1, keepdims=True)
     scaled_ref[...] = (rows * gain_ref[...]).astype(jnp.bfloat16)
     half = lax.rem(lax.axis_index("role"), 2)
@@ -552,20 +556,20 @@
         cost=COVER[2],
     )
     heads = lax.all_to_all(heads, ("role", "tp"), 0, 0)
-    pieces = 2
-    piece = jax.ShapeDtypeStruct((rows // pieces, features), jnp.bfloat16)
+    near, far = STEPS
+    pieces = [jax.ShapeDtypeStruct((rows * part // 32, features), jnp.bfloat16) for part in PARTS]
     attn = call(
         output_kernel,
-        [piece] * pieces,
+        pieces,
         [heads, in_vmem(w_output)],
         scratch=[pltpu.VMEM((rows * GROUP, LANES), jnp.float32)],
         cost=COVER[3],
     )
     terms = []
-    near = [swap(value, "tp", 1) for value in attn]
-    for value, got in zip(attn, near):
-        (paired,) = call(pair_kernel, [piece], [value, got])
-        terms += [paired, swap(paired, "tp", 2)]
+    got = [swap(value, "tp", near) for value in attn]
+    for value, arrived, piece in zip(attn, got, pieces):
+        (paired,) = call(pair_kernel, [piece], [value, arrived])
+        terms += [paired, swap(paired, "tp", far)]
     width = w_gate.shape[1] // 2
     first = -(-width * FIRST_PART // (100 * 2 * LANES)) * 2 * LANES
     sizes = (first, width - first)
@@ -579,16 +583,17 @@
     def half_of(piece):
         return jax.ShapeDtypeStruct((rows, sizes[piece]), jnp.bfloat16)
 
-    scaled, tail, send, middle = call(
+    scaled, tail, send, middle, live = call(
         middle_kernel,
         [
             jax.ShapeDtypeStruct((rows, features), jnp.bfloat16),
             jax.ShapeDtypeStruct((rows, LANES), jnp.float32),
             wide(sizes[0], jnp.bfloat16, LANES),
             block,
+            jax.ShapeDtypeStruct((own, LANES), jnp.float32),
         ],
         [served[None, :], stream, *terms, ffn_gain[None, :], w_gate, w_up],
-        scratch=[row_scratch],
+        scratch=[row_scratch, pltpu.VMEM((rows, LANES), jnp.float32)],
         cost=COVER[4],
     )
     got = swap(send, "role", 1)
@@ -645,7 +650,10 @@
         cost=COVER[9],
     )
     terms = [terms[0]] + [swap(terms[k], "tp", k) for k in range(1, tp_count)]
-    return call(add_kernel, [block], [served, middle, *terms], smem=1)[0]
+    ffn = terms[0].astype(jnp.float32)
+    for term in terms[1:]:
+        ffn = ffn + term.astype(jnp.float32)
+    return (middle.astype(jnp.float32) + live[:, :1] * ffn).astype(jnp.bfloat16)
 
 
 def solution(mesh):

time: 69.2 us -> 68.6 us (level)
  Pallas kernels: 13.9 us -> 12.7 us
    pallas_call x19 -> x18, Pallas kernels: 13.9 us -> 12.7 us  [call(): pl.pallas_call(kernel, out_shape=outs, in_specs=specs, out_specs=[pl.Bloc...]
where the time goes in v6:
time: 68.6 us; the launch traced here: 68.4 us
  blocking collectives  19.4 us (28%)
  starting transfers between devices  18 us (26%)
  waiting for transfers between devices  16.6 us (24%)
  Pallas kernels  12.7 us (19%)
  local copies, waits for them, and re-layouts  0.85 us (1%)
  other arithmetic  0.69 us (1%)
    ppermute x16, starting transfers between devices, swap(): return lax.ppermute(value, axis, [(i, i ^ distance) for i in range(count)])  18 us
    ppermute x16, waiting for transfers between devices, swap(): return lax.ppermute(value, axis, [(i, i ^ distance) for i in range(count)])  16.6 us
    pallas_call x18, Pallas kernels, call(): pl.pallas_call(kernel, out_shape=outs, in_specs=specs, out_specs=[pl.Bloc...  12.7 us
    all_to_all x1, blocking collectives, local_exchange(): heads = lax.all_to_all(heads, ('role', 'tp'), 0, 0)  9.72 us
    all_to_all x1, blocking collectives, local_exchange(): parts = lax.all_to_all(sums, ('role', 'tp'), 0, 0)  9.65 us
  transfers between devices with their start and end apart: 16, of which 10 were waited for; matrix products, arithmetic and copies ran while one was open for 0% of the time, Pallas kernels for 10%

profile of v6, /device:TPU:0, one launch (start us, length us, event | category | flops | bytes accessed | tf_op | source)
XLA Modules:
  0.0 68.4 jit_solution(17308449123556700097)
XLA Ops:
  0.0 3.1 %collective-permute-start = (bf16[8,2048]{1,0:T(8,128)(2,1)}, bf16[8,2048]{1,0:T(8,128)(2,1)S(1)}, u32[]{:S(2)}, u32[]{:S(2)}) collective-permute-start(bf16[8,2048]{1,0:T(8,128)(2,1)} %refs_0_.1), channel_id=1, source_target_pairs={{0,1},{1,0},{2,3},{3,2},{4,5},{5,4},{6,7},{7,6},{8,9},{9,8},{10,11... | collective-permute-start | bytes 98312 | tf_op jit(solution)/shard_map/ppermute | solution.py:181
  3.1 2.6 %collective-permute-start.1 = (bf16[8,2048]{1,0:T(8,128)(2,1)}, bf16[8,2048]{1,0:T(8,128)(2,1)S(1)}, u32[]{:S(2)}, u32[]{:S(2)}) collective-permute-start(bf16[8,2048]{1,0:T(8,128)(2,1)} %refs_0_.1), channel_id=1, source_target_pairs={{0,2},{1,3},{2,0},{3,1},{4,6},{5,7},{6,4},{7,5},{8,10},{9,11},{10,... | collective-permute-start | bytes 98312 | tf_op jit(solution)/shard_map/ppermute | solution.py:181
  5.7 0.7 copy-done.11
  7.0 1.8 %collective-permute-done.1.refs_2_ = bf16[8,2048]{1,0:T(8,128)(2,1)S(1)} collective-permute-done((bf16[8,2048]{1,0:T(8,128)(2,1)}, bf16[8,2048]{1,0:T(8,128)(2,1)S(1)}, u32[]{:S(2)}, u32[]{:S(2)}) %collective-permute-start.1) | collective-permute-done | bytes 32800 | tf_op jit(solution)/shard_map/ppermute | solution.py:181
  8.8 2.9 %collective-permute-done.2.refs_3_ = bf16[8,2048]{1,0:T(8,128)(2,1)S(1)} collective-permute-done((bf16[8,2048]{1,0:T(8,128)(2,1)}, bf16[8,2048]{1,0:T(8,128)(2,1)S(1)}, u32[]{:S(2)}, u32[]{:S(2)}) %collective-permute-start.2) | collective-permute-done | bytes 32800 | tf_op jit(solution)/shard_map/ppermute | solution.py:181
  11.7 1.0 %shard_map.137 = (bf16[16,24,128]{2,1,0:T(8,128)(2,1)S(1)}, bf16[32,2048]{1,0:T(8,128)(2,1)S(1)}) custom-call(f32[2,128]{1,0:T(2,128)S(1)} %get-tuple-element.22._.cosine_ref, bf16[8,2048]{1,0:T(8,128)(2,1)S(1)} %copy-done.8, bf16[8,2048]{1,0:T(8,128)(2,1)S(1)} %collective-permute-done.refs_1_, bf16[8,2048]{1,0:T(8,128)(2,1)S(1)} %collective-permute-done.1.refs_2_, ...), custom_call_target="tpu_custom_call" | custom-call | flops 99999997952 | bytes 1048576 | tf_op jit(solution)/shard_map/pallas_call | solution.py:191
  12.8 9.7 %all_to_all.10.got_ref = bf16[16,24,128]{2,1,0:T(8,128)(2,1)S(1)} all-to-all(bf16[16,24,128]{2,1,0:T(8,128)(2,1)S(1)} %get-tuple-element.24), channel_id=1, replica_groups=mesh['groups'=2,'role'=4,'tp'=4] {'role','tp'}, dimensions={0} | all-to-all | bytes 196608 | tf_op jit(solution)/shard_map/all_to_all | solution.py:550
  22.5 1.4 %shard_map.138 = bf16[16,16,128]{2,1,0:T(8,128)(2,1)S(1)} custom-call(s32[2]{0:T(128)S(1)} %copy-done.12, bf16[16,24,128]{2,1,0:T(8,128)(2,1)S(1)} %all_to_all.10.got_ref, f32[2,128]{1,0:T(2,128)S(1)} %get-tuple-element.22._.cosine_ref, f32[2,128]{1,0:T(2,128)S(1)} %get-tuple-element.25.sine_ref, bf16[2,256,512]{2,1,0:T(8,128)(2,1)S(1)} %copy-done.6, ...), custom_call_target="tpu_custom_call" | custom-call | flops 99999997952 | bytes 1048576 | tf_op jit(solution)/shard_map/pallas_call | solution.py:191
  23.9 9.7 %all_to_all.11.heads_ref = bf16[16,16,128]{2,1,0:T(8,128)(2,1)S(1)} all-to-all(bf16[16,16,128]{2,1,0:T(8,128)(2,1)S(1)} %shard_map.138), channel_id=1, replica_groups=mesh['groups'=2,'role'=4,'tp'=4] {'role','tp'}, dimensions={0} | all-to-all | bytes 131072 | tf_op jit(solution)/shard_map/all_to_all | solution.py:558
  33.6 0.8 %shard_map.139 = (bf16[16,2048]{1,0:T(8,128)(2,1)S(1)}, bf16[16,2048]{1,0:T(8,128)(2,1)S(1)}) custom-call(bf16[16,16,128]{2,1,0:T(8,128)(2,1)S(1)} %all_to_all.11.heads_ref, bf16[1024,2048]{1,0:T(8,128)(2,1)S(1)} %copy-done.2), custom_call_target="tpu_custom_call" | custom-call | flops 1000000000 | bytes 1048576 | tf_op jit(solution)/shard_map/pallas_call | solution.py:191
  34.8 1.7 %collective-permute-start.3 = (bf16[16,2048]{1,0:T(8,128)(2,1)S(1)}, bf16[16,2048]{1,0:T(8,128)(2,1)S(1)}, u32[]{:S(2)}, u32[]{:S(2)}) collective-permute-start(bf16[16,2048]{1,0:T(8,128)(2,1)S(1)} %get-tuple-element.26.keep_ref), channel_id=1, source_target_pairs={{0,1},{1,0},{2,3},{3,2},{4,5},{5,4},{6,7},{7,6},{8,9},{9,8},{10,11... | collective-permute-start | bytes 196616 | tf_op jit(solution)/shard_map/ppermute | solution.py:181
  36.5 2.8 %collective-permute-done.5.got_ref = bf16[16,2048]{1,0:T(8,128)(2,1)S(1)} collective-permute-done((bf16[16,2048]{1,0:T(8,128)(2,1)S(1)}, bf16[16,2048]{1,0:T(8,128)(2,1)S(1)}, u32[]{:S(2)}, u32[]{:S(2)}) %collective-permute-start.5) | collective-permute-done | bytes 65568 | tf_op jit(solution)/shard_map/ppermute | solution.py:181
  39.3 0.7 collective-permute-start.6
  40.0 2.4 %collective-permute-start.4 = (bf16[16,2048]{1,0:T(8,128)(2,1)S(1)}, bf16[16,2048]{1,0:T(8,128)(2,1)S(1)}, u32[]{:S(2)}, u32[]{:S(2)}) collective-permute-start(bf16[16,2048]{1,0:T(8,128)(2,1)S(1)} %shard_map.140.refs_2_), channel_id=1, source_target_pairs={{0,2},{1,3},{2,0},{3,1},{4,6},{5,7},{6,4},{7,5},{8,10},{9,11},{10,... | collective-permute-start | bytes 196616 | tf_op jit(solution)/shard_map/ppermute | solution.py:181
  42.3 3.7 %collective-permute-done.6.refs_5_ = bf16[16,2048]{1,0:T(8,128)(2,1)S(1)} collective-permute-done((bf16[16,2048]{1,0:T(8,128)(2,1)S(1)}, bf16[16,2048]{1,0:T(8,128)(2,1)S(1)}, u32[]{:S(2)}, u32[]{:S(2)}) %collective-permute-start.6) | collective-permute-done | bytes 65568 | tf_op jit(solution)/shard_map/ppermute | solution.py:181
  46.1 0.7 %collective-permute-done.4.refs_3_ = bf16[16,2048]{1,0:T(8,128)(2,1)S(1)} collective-permute-done((bf16[16,2048]{1,0:T(8,128)(2,1)S(1)}, bf16[16,2048]{1,0:T(8,128)(2,1)S(1)}, u32[]{:S(2)}, u32[]{:S(2)}) %collective-permute-start.4) | collective-permute-done | bytes 65568 | tf_op jit(solution)/shard_map/ppermute | solution.py:181
  46.8 1.6 %shard_map.142 = (bf16[32,2048]{1,0:T(8,128)(2,1)S(1)}, f32[32,128]{1,0:T(8,128)S(1)}, bf16[32,2176]{1,0:T(8,128)(2,1)S(1)}, bf16[8,2048]{1,0:T(8,128)(2,1)S(1)}, f32[8,128]{1,0:T(8,128)S(1)}) custom-call(s32[1,32]{1,0:T(1,128)S(1)} %bitcast.7, bf16[32,2048]{1,0:T(8,128)(2,1)S(1)} %get-tuple-element.23.refs_1_, bf16[16,2048]{1,0:T(8,128)(2,1)S(1)} %shard_map.140.refs_2_, ...), custom_call_target="tpu_custom_call" | custom-call | flops 10000000000 | bytes 1048576 | tf_op jit(solution)/shard_map/pallas_call | solution.py:191
  48.5 1.5 %shard_map.144.keep_ref = f32[32,2048]{1,0:T(8,128)S(1)} custom-call(bf16[32,2048]{1,0:T(8,128)(2,1)S(1)} %get-tuple-element.30.scaled_ref, bf16[2048,3584]{1,0:T(8,128)(2,1)S(1)} %copy-done, bf16[2048,3584]{1,0:T(8,128)(2,1)S(1)} %copy-done.1), custom_call_target="tpu_custom_call" | custom-call | flops 10000000000 | bytes 1048576 | tf_op jit(solution)/shard_map/pallas_call | solution.py:191
  50.1 0.6 collective-permute-start.10
  50.8 1.2 %shard_map.146 = bf16[32,1536]{1,0:T(8,128)(2,1)S(1)} custom-call(bf16[32,2048]{1,0:T(8,128)(2,1)S(1)} %get-tuple-element.30.scaled_ref, bf16[2048,3584]{1,0:T(8,128)(2,1)S(1)} %copy-done, bf16[2048,3584]{1,0:T(8,128)(2,1)S(1)} %copy-done.1, bf16[32,2176]{1,0:T(8,128)(2,1)S(1)} %shard_map.145.refs_0_.own_ref), custom_call_target="tpu_custom_call" | custom-call | flops 10000000000 | bytes 1048576 | tf_op jit(solution)/shard_map/pallas_call | solution.py:191
  52.2 1.2 %shard_map.143.keep_ref = f32[32,1536]{1,0:T(8,128)S(1)} custom-call(bf16[32,2048]{1,0:T(8,128)(2,1)S(1)} %get-tuple-element.30.scaled_ref, bf16[2048,3584]{1,0:T(8,128)(2,1)S(1)} %copy-done, bf16[2048,3584]{1,0:T(8,128)(2,1)S(1)} %copy-done.1), custom_call_target="tpu_custom_call" | custom-call | flops 1000000000 | bytes 1048576 | tf_op jit(solution)/shard_map/pallas_call | solution.py:191
  53.4 1.5 %collective-permute-start.9 = (bf16[32,1536]{1,0:T(8,128)(2,1)S(1)}, bf16[32,1536]{1,0:T(8,128)(2,1)S(1)}, u32[]{:S(2)}, u32[]{:S(2)}) collective-permute-start(bf16[32,1536]{1,0:T(8,128)(2,1)S(1)} %shard_map.147.own_ref), channel_id=1, source_target_pairs={{0,8},{4,12},{8,0},{12,4},{1,9},{5,13},{9,1},{13,5},{2,10},{6,14},... | collective-permute-start | bytes 294920 | tf_op jit(solution)/shard_map/ppermute | solution.py:181
  54.9 1.3 %collective-permute-done.10.got_ref = bf16[32,2176]{1,0:T(8,128)(2,1)S(1)} collective-permute-done((bf16[32,2176]{1,0:T(8,128)(2,1)S(1)}, bf16[32,2176]{1,0:T(8,128)(2,1)S(1)}, u32[]{:S(2)}, u32[]{:S(2)}) %collective-permute-start.10) | collective-permute-done | bytes 139296 | tf_op jit(solution)/shard_map/ppermute | solution.py:181
  56.5 0.8 %shard_map.149.refs_0_ = f32[32,2048]{1,0:T(8,128)S(1)} custom-call(bf16[32,1024]{1,0:T(8,128)(2,1)S(1)} %get-tuple-element.34.hidden_ref, bf16[3584,2048]{1,0:T(8,128)(2,1)S(1)} %bitcast.4), custom_call_target="tpu_custom_call" | custom-call | flops 1000000000 | bytes 1048576 | tf_op jit(solution)/shard_map/pallas_call | solution.py:191
  57.7 0.8 %shard_map.150._.refs_0_ = f32[32,2048]{1,0:T(8,128)S(1)} custom-call(bf16[32,1024]{1,0:T(8,128)(2,1)S(1)} %collective-permute-done.11.hidden_ref, bf16[3584,2048]{1,0:T(8,128)(2,1)S(1)} %bitcast.4, f32[32,2048]{1,0:T(8,128)S(1)} %shard_map.149.refs_0_), custom_call_target="tpu_custom_call" | custom-call | flops 1000000000 | bytes 1048576 | tf_op jit(solution)/shard_map/pallas_call | solution.py:191
  58.9 0.6 shard_map.152.before_ref
  60.0 0.7 shard_map.153
  60.7 1.3 %collective-permute-start.14 = (bf16[8,2048]{1,0:T(8,128)(2,1)S(1)}, bf16[8,2048]{1,0:T(8,128)(2,1)S(1)}, u32[]{:S(2)}, u32[]{:S(2)}) collective-permute-start(bf16[8,2048]{1,0:T(8,128)(2,1)S(1)} %get-tuple-element.37), channel_id=1, source_target_pairs={{0,2},{1,3},{2,0},{3,1},{4,6},{5,7},{6,4},{7,5},{8,10},{9,11},{10,... | collective-permute-start | bytes 98312 | tf_op jit(solution)/shard_map/ppermute | solution.py:181
  62.0 3.1 %collective-permute-start.15 = (bf16[8,2048]{1,0:T(8,128)(2,1)S(1)}, bf16[8,2048]{1,0:T(8,128)(2,1)S(1)}, u32[]{:S(2)}, u32[]{:S(2)}) collective-permute-start(bf16[8,2048]{1,0:T(8,128)(2,1)S(1)} %get-tuple-element.38), channel_id=1, source_target_pairs={{0,3},{1,2},{2,1},{3,0},{4,7},{5,6},{6,5},{7,4},{8,11},{9,10},{10,... | collective-permute-start | bytes 98312 | tf_op jit(solution)/shard_map/ppermute | solution.py:181
  65.2 1.3 %collective-permute-done.14 = bf16[8,2048]{1,0:T(8,128)(2,1)S(1)} collective-permute-done((bf16[8,2048]{1,0:T(8,128)(2,1)S(1)}, bf16[8,2048]{1,0:T(8,128)(2,1)S(1)}, u32[]{:S(2)}, u32[]{:S(2)}) %collective-permute-start.14) | collective-permute-done | bytes 32800 | tf_op jit(solution)/shard_map/ppermute | solution.py:181
  66.5 1.2 %collective-permute-done.15 = bf16[8,2048]{1,0:T(8,128)(2,1)S(1)} collective-permute-done((bf16[8,2048]{1,0:T(8,128)(2,1)S(1)}, bf16[8,2048]{1,0:T(8,128)(2,1)S(1)}, u32[]{:S(2)}, u32[]{:S(2)}) %collective-permute-start.15) | collective-permute-done | bytes 32800 | tf_op jit(solution)/shard_map/ppermute | solution.py:181
  67.7 0.7 %add_convert_fusion = bf16[8,2048]{1,0:T(8,128)(2,1)} fusion(bf16[8,2048]{1,0:T(8,128)(2,1)S(1)} %collective-permute-done.15, bf16[8,2048]{1,0:T(8,128)(2,1)S(1)} %collective-permute-done.14, bf16[8,2048]{1,0:T(8,128)(2,1)S(1)} %collective-permute-done.13, bf16[8,2048]{1,0:T(8,128)(2,1)S(1)} %get-tuple-element.35, bf16[8,2048]{1,0:T(8,128)(2,1)S(1)} %get-tuple-element.28, ...), kind=kLoop, calls=%fused_computation | loop fusion | flops 180224 | bytes 196640 | tf_op jit(solution)/shard_map/convert_element_type | solution.py:656
  (59 shorter events, 3.0 us)
Async XLA Ops:
  0.0 11.7 %copy-start.8 = (bf16[8,2048]{1,0:T(8,128)(2,1)S(1)}, bf16[8,2048]{1,0:T(8,128)(2,1)}, u32[]{:S(2)}) copy-start(bf16[8,2048]{1,0:T(8,128)(2,1)} %refs_0_.1) | copy-start | bytes 98308
  0.0 11.7 %copy-start.9 = (f32[2048]{0:T(1024)S(1)}, f32[2048]{0:T(1024)}, u32[]{:S(2)}) copy-start(f32[2048]{0:T(1024)} %param.15) | copy-start | bytes 24580
  0.0 11.7 %copy-start.3 = (bf16[2048,1024]{1,0:T(8,128)(2,1)S(1)}, bf16[2048,1024]{1,0:T(8,128)(2,1)}, u32[]{:S(2)}) copy-start(bf16[2048,1024]{1,0:T(8,128)(2,1)} %refs_5_.1) | copy-start | bytes 12582916
  0.0 11.7 %copy-start.4 = (bf16[2048,128]{1,0:T(8,128)(2,1)S(1)}, bf16[2048,128]{1,0:T(8,128)(2,1)}, u32[]{:S(2)}) copy-start(bf16[2048,128]{1,0:T(8,128)(2,1)} %refs_6_.1) | copy-start | bytes 1572868
  0.0 11.7 %copy-start.5 = (bf16[2048,128]{1,0:T(8,128)(2,1)S(1)}, bf16[2048,128]{1,0:T(8,128)(2,1)}, u32[]{:S(2)}) copy-start(bf16[2048,128]{1,0:T(8,128)(2,1)} %refs_7_.2) | copy-start | bytes 1572868
  0.0 7.0 %collective-permute-start = (bf16[8,2048]{1,0:T(8,128)(2,1)}, bf16[8,2048]{1,0:T(8,128)(2,1)S(1)}, u32[]{:S(2)}, u32[]{:S(2)}) collective-permute-start(bf16[8,2048]{1,0:T(8,128)(2,1)} %refs_0_.1), channel_id=1, source_target_pairs={{0,1},{1,0},{2,3},{3,2},{4,5},{5,4},{6,7},{7,6},{8,9},{9,8},{10,11... | collective-permute-start | bytes 98312 | tf_op jit(solution)/shard_map/ppermute | solution.py:181
  3.1 5.6 %collective-permute-start.1 = (bf16[8,2048]{1,0:T(8,128)(2,1)}, bf16[8,2048]{1,0:T(8,128)(2,1)S(1)}, u32[]{:S(2)}, u32[]{:S(2)}) collective-permute-start(bf16[8,2048]{1,0:T(8,128)(2,1)} %refs_0_.1), channel_id=1, source_target_pairs={{0,2},{1,3},{2,0},{3,1},{4,6},{5,7},{6,4},{7,5},{8,10},{9,11},{10,... | collective-permute-start | bytes 98312 | tf_op jit(solution)/shard_map/ppermute | solution.py:181
  5.7 5.9 %collective-permute-start.2 = (bf16[8,2048]{1,0:T(8,128)(2,1)}, bf16[8,2048]{1,0:T(8,128)(2,1)S(1)}, u32[]{:S(2)}, u32[]{:S(2)}) collective-permute-start(bf16[8,2048]{1,0:T(8,128)(2,1)} %refs_0_.1), channel_id=1, source_target_pairs={{0,3},{1,2},{2,1},{3,0},{4,7},{5,6},{6,5},{7,4},{8,11},{9,10},{10,... | collective-permute-start | bytes 98312 | tf_op jit(solution)/shard_map/ppermute | solution.py:181
  11.7 10.7 %copy-start.6 = (bf16[2,256,512]{2,1,0:T(8,128)(2,1)S(1)}, bf16[2,256,512]{2,1,0:T(8,128)(2,1)}, u32[]{:S(2)}) copy-start(bf16[2,256,512]{2,1,0:T(8,128)(2,1)} %keys_ref.1) | copy-start | bytes 1572868
  11.7 10.7 %copy-start.7 = (bf16[2,256,512]{2,1,0:T(8,128)(2,1)S(1)}, bf16[2,256,512]{2,1,0:T(8,128)(2,1)}, u32[]{:S(2)}) copy-start(bf16[2,256,512]{2,1,0:T(8,128)(2,1)} %values_ref.1) | copy-start | bytes 1572868
  11.7 10.7 %copy-start.12 = (s32[2]{0:T(128)S(1)}, s32[2]{0:T(128)}, u32[]{:S(2)}) copy-start(s32[2]{0:T(128)} %lengths_ref.3) | copy-start | bytes 28
  22.4 11.2 %copy-start.2 = (bf16[1024,2048]{1,0:T(8,128)(2,1)S(1)}, bf16[1024,2048]{1,0:T(8,128)(2,1)}, u32[]{:S(2)}) copy-start(bf16[1024,2048]{1,0:T(8,128)(2,1)} %w_ref.5) | copy-start | bytes 12582916
  22.4 24.4 %copy-start = (bf16[2048,3584]{1,0:T(8,128)(2,1)S(1)}, bf16[2048,3584]{1,0:T(8,128)(2,1)}, u32[]{:S(2)}) copy-start(bf16[2048,3584]{1,0:T(8,128)(2,1)} %wg_ref.5) | copy-start | bytes 44040196
  22.5 24.3 %copy-start.1 = (bf16[2048,3584]{1,0:T(8,128)(2,1)S(1)}, bf16[2048,3584]{1,0:T(8,128)(2,1)}, u32[]{:S(2)}) copy-start(bf16[2048,3584]{1,0:T(8,128)(2,1)} %wu_ref.5) | copy-start | bytes 44040196
  22.5 24.3 %copy-start.10 = (f32[2048]{0:T(1024)S(1)}, f32[2048]{0:T(1024)}, u32[]{:S(2)}) copy-start(f32[2048]{0:T(1024)} %param.24) | copy-start | bytes 24580
  22.5 24.3 %copy-start.13 = (s32[32]{0:T(128)S(1)}, s32[32]{0:T(128)}, u32[]{:S(2)}) copy-start(s32[32]{0:T(128)} %param.23) | copy-start | bytes 388
  34.4 4.8 %collective-permute-start.5 = (bf16[16,2048]{1,0:T(8,128)(2,1)S(1)}, bf16[16,2048]{1,0:T(8,128)(2,1)S(1)}, u32[]{:S(2)}, u32[]{:S(2)}) collective-permute-start(bf16[16,2048]{1,0:T(8,128)(2,1)S(1)} %get-tuple-element.27.keep_ref), channel_id=1, source_target_pairs={{0,1},{1,0},{2,3},{3,2},{4,5},{5,4},{6,7},{7,6},{8,9},{9,8},{10,11... | collective-permute-start | bytes 196616 | tf_op jit(solution)/shard_map/ppermute | solution.py:181
  34.8 5.2 %collective-permute-start.3 = (bf16[16,2048]{1,0:T(8,128)(2,1)S(1)}, bf16[16,2048]{1,0:T(8,128)(2,1)S(1)}, u32[]{:S(2)}, u32[]{:S(2)}) collective-permute-start(bf16[16,2048]{1,0:T(8,128)(2,1)S(1)} %get-tuple-element.26.keep_ref), channel_id=1, source_target_pairs={{0,1},{1,0},{2,3},{3,2},{4,5},{5,4},{6,7},{7,6},{8,9},{9,8},{10,11... | collective-permute-start | bytes 196616 | tf_op jit(solution)/shard_map/ppermute | solution.py:181
  39.3 6.8 %collective-permute-start.6 = (bf16[16,2048]{1,0:T(8,128)(2,1)S(1)}, bf16[16,2048]{1,0:T(8,128)(2,1)S(1)}, u32[]{:S(2)}, u32[]{:S(2)}) collective-permute-start(bf16[16,2048]{1,0:T(8,128)(2,1)S(1)} %shard_map.141.refs_4_), channel_id=1, source_target_pairs={{0,2},{1,3},{2,0},{3,1},{4,6},{5,7},{6,4},{7,5},{8,10},{9,11},{10,... | collective-permute-start | bytes 196616 | tf_op jit(solution)/shard_map/ppermute | solution.py:181
  40.0 6.8 %collective-permute-start.4 = (bf16[16,2048]{1,0:T(8,128)(2,1)S(1)}, bf16[16,2048]{1,0:T(8,128)(2,1)S(1)}, u32[]{:S(2)}, u32[]{:S(2)}) collective-permute-start(bf16[16,2048]{1,0:T(8,128)(2,1)S(1)} %shard_map.140.refs_2_), channel_id=1, source_target_pairs={{0,2},{1,3},{2,0},{3,1},{4,6},{5,7},{6,4},{7,5},{8,10},{9,11},{10,... | collective-permute-start | bytes 196616 | tf_op jit(solution)/shard_map/ppermute | solution.py:181
  48.4 1.6 %collective-permute-start.7 = (bf16[32,2176]{1,0:T(8,128)(2,1)S(1)}, bf16[32,2176]{1,0:T(8,128)(2,1)S(1)}, u32[]{:S(2)}, u32[]{:S(2)}) collective-permute-start(bf16[32,2176]{1,0:T(8,128)(2,1)S(1)} %get-tuple-element.32), channel_id=1, source_target_pairs={{0,4},{4,0},{8,12},{12,8},{1,5},{5,1},{9,13},{13,9},{2,6},{6,2},{1... | collective-permute-start | bytes 417800 | tf_op jit(solution)/shard_map/ppermute | solution.py:181
  50.1 6.1 %collective-permute-start.10 = (bf16[32,2176]{1,0:T(8,128)(2,1)S(1)}, bf16[32,2176]{1,0:T(8,128)(2,1)S(1)}, u32[]{:S(2)}, u32[]{:S(2)}) collective-permute-start(bf16[32,2176]{1,0:T(8,128)(2,1)S(1)} %shard_map.145.refs_0_.own_ref), channel_id=1, source_target_pairs={{0,8},{4,12},{8,0},{12,4},{1,9},{5,13},{9,1},{13,5},{2,10},{6,14},... | collective-permute-start | bytes 417800 | tf_op jit(solution)/shard_map/ppermute | solution.py:181
  50.8 5.7 %slice-start = ((s8[14680064]{0:T(1024)(128)(4,1)}), s8[2097152]{0:T(1024)(128)(4,1)S(1)}, s32[]{:S(2)}) async-start(s8[14680064]{0:T(1024)(128)(4,1)} %bitcast.3), calls=%async_computation.2 | async-start | bytes 4194304
  50.8 5.7 %slice-start.1 = ((s8[14680064]{0:T(1024)(128)(4,1)}), s8[4194304]{0:T(1024)(128)(4,1)S(1)}, s32[]{:S(2)}) async-start(s8[14680064]{0:T(1024)(128)(4,1)} %bitcast.3), calls=%async_computation.3 | async-start | bytes 8388608
  50.8 5.7 %slice-start.2 = ((s8[14680064]{0:T(1024)(128)(4,1)}), s8[4194304]{0:T(1024)(128)(4,1)S(1)}, s32[]{:S(2)}) async-start(s8[14680064]{0:T(1024)(128)(4,1)} %bitcast.3), calls=%async_computation.4 | async-start | bytes 8388608
  52.0 1.4 %collective-permute-start.8 = (bf16[32,1536]{1,0:T(8,128)(2,1)S(1)}, bf16[32,1536]{1,0:T(8,128)(2,1)S(1)}, u32[]{:S(2)}, u32[]{:S(2)}) collective-permute-start(bf16[32,1536]{1,0:T(8,128)(2,1)S(1)} %shard_map.146), channel_id=1, source_target_pairs={{0,4},{4,0},{8,12},{12,8},{1,5},{5,1},{9,13},{13,9},{2,6},{6,2},{1... | collective-permute-start | bytes 294920 | tf_op jit(solution)/shard_map/ppermute | solution.py:181
  53.4 5.2 %collective-permute-start.9 = (bf16[32,1536]{1,0:T(8,128)(2,1)S(1)}, bf16[32,1536]{1,0:T(8,128)(2,1)S(1)}, u32[]{:S(2)}, u32[]{:S(2)}) collective-permute-start(bf16[32,1536]{1,0:T(8,128)(2,1)S(1)} %shard_map.147.own_ref), channel_id=1, source_target_pairs={{0,8},{4,12},{8,0},{12,4},{1,9},{5,13},{9,1},{13,5},{2,10},{6,14},... | collective-permute-start | bytes 294920 | tf_op jit(solution)/shard_map/ppermute | solution.py:181
  56.4 1.3 %collective-permute-start.11 = (bf16[32,1024]{1,0:T(8,128)(2,1)S(1)}, bf16[32,1024]{1,0:T(8,128)(2,1)S(1)}, u32[]{:S(2)}, u32[]{:S(2)}) collective-permute-start(bf16[32,1024]{1,0:T(8,128)(2,1)S(1)} %get-tuple-element.34.hidden_ref), channel_id=1, source_target_pairs={{0,4},{4,0},{8,12},{12,8},{1,5},{5,1},{9,13},{13,9},{2,6},{6,2},{1... | collective-permute-start | bytes 196616 | tf_op jit(solution)/shard_map/ppermute | solution.py:181
  58.7 1.3 %collective-permute-start.12 = (bf16[32,768]{1,0:T(8,128)(2,1)S(1)}, bf16[32,768]{1,0:T(8,128)(2,1)S(1)}, u32[]{:S(2)}, u32[]{:S(2)}) collective-permute-start(bf16[32,768]{1,0:T(8,128)(2,1)S(1)} %shard_map.151.hidden_ref), channel_id=1, source_target_pairs={{0,4},{4,0},{8,12},{12,8},{1,5},{5,1},{9,13},{13,9},{2,6},{6,2},{1... | collective-permute-start | bytes 147464 | tf_op jit(solution)/shard_map/ppermute | solution.py:181
  60.6 4.6 %collective-permute-start.13 = (bf16[8,2048]{1,0:T(8,128)(2,1)S(1)}, bf16[8,2048]{1,0:T(8,128)(2,1)S(1)}, u32[]{:S(2)}, u32[]{:S(2)}) collective-permute-start(bf16[8,2048]{1,0:T(8,128)(2,1)S(1)} %get-tuple-element.36), channel_id=1, source_target_pairs={{0,1},{1,0},{2,3},{3,2},{4,5},{5,4},{6,7},{7,6},{8,9},{9,8},{10,11... | collective-permute-start | bytes 98312 | tf_op jit(solution)/shard_map/ppermute | solution.py:181
  60.7 5.8 %collective-permute-start.14 = (bf16[8,2048]{1,0:T(8,128)(2,1)S(1)}, bf16[8,2048]{1,0:T(8,128)(2,1)S(1)}, u32[]{:S(2)}, u32[]{:S(2)}) collective-permute-start(bf16[8,2048]{1,0:T(8,128)(2,1)S(1)} %get-tuple-element.37), channel_id=1, source_target_pairs={{0,2},{1,3},{2,0},{3,1},{4,6},{5,7},{6,4},{7,5},{8,10},{9,11},{10,... | collective-permute-start | bytes 98312 | tf_op jit(solution)/shard_map/ppermute | solution.py:181
  62.0 5.7 %collective-permute-start.15 = (bf16[8,2048]{1,0:T(8,128)(2,1)S(1)}, bf16[8,2048]{1,0:T(8,128)(2,1)S(1)}, u32[]{:S(2)}, u32[]{:S(2)}) collective-permute-start(bf16[8,2048]{1,0:T(8,128)(2,1)S(1)} %get-tuple-element.38), channel_id=1, source_target_pairs={{0,3},{1,2},{2,1},{3,0},{4,7},{5,6},{6,5},{7,4},{8,11},{9,10},{10,... | collective-permute-start | bytes 98312 | tf_op jit(solution)/shard_map/ppermute | solution.py:181
  (2 other events, 5.2 us)
